TPU v7x, 32 devices: a whole 2x2x4 slice. The times are simulated.
32 devices in a mesh: tile: 8 (over z, core), view: 4 (over y, x).
Axes of the slice: x: 2, y: 2, z: 4, core: 2. Of those that a mesh axis runs over, the one named last changes fastest.
Arguments:
- estimate: float32 [256, 128, 256], P('tile'), may hold values from 0.25 to 4
- views_data: bfloat16 [4, 256, 128, 256], P('view', 'tile'), may hold values from 0.25 to 4
- psf_bank: bfloat16 [8, 3, 33], replicated, as said below
- psf_index: int32 [4], P('view'), may hold values from 0 to 7
- margin_extent: int32 [8, 2], P('tile'), may hold values from 1 to 32, as said below
Outputs:
- refined: float32 [256, 128, 256], P('tile')
Inputs may be any that keep to these rules, and one draw needn't show every extreme that they name: `psf_bank`: every kernel tap is positive. `margin_extent`: some tile takes exactly 32 cells on some side.
All inputs are finite; a program needn't handle non-finite values.
Results may differ from a plain program's by a relative error of at most 0.00043.
Values may be sent and summed in bfloat16 or wider, within the bound.
No kernel may reach another device: no remote copies, remote signals or barrier semaphores. Data moves between devices by JAX's collectives and lax.ppermute only.
A program may use at most 128 MiB of HBM per device.

v0:
```python
import functools

import jax
import jax.numpy as jnp
from jax import lax
from jax.experimental import pallas as pl
from jax.experimental.pallas import tpu as pltpu
from jax.sharding import PartitionSpec as P

MARGIN = 32
ITERS = 2
REACH = 16
LEVELS = 32766.0
LANES = 128
GROUP = 4


def dot32(a, b):
    return jnp.dot(a, b, preferred_element_type=jnp.float32)


def halves(value):
    return [value[:, h * LANES : (h + 1) * LANES] for h in range(value.shape[1] // LANES)]


def sweep_kernel(plan, *refs):
    pieces_in, pieces_out, depths, core, rows, cols = plan
    refs = list(refs)
    take = lambda n: [refs.pop(0) for _ in range(n)]
    (mask_ref,) = take(1)
    lows, owns, highs = take(pieces_in), take(pieces_in), take(pieces_in)
    meas_low, meas_own, meas_high = take(3)
    z_band, z_back, y_band, y_back, x_band, x_back = take(6)
    codes, scales = take(pieces_out), take(pieces_out)
    by_plane, by_row = take(2)
    lane_parts = cols // LANES

    rows_in = rows // pieces_in
    for p in range(pieces_in):

        def z_pass(step, carry, p=p):
            for u in range(2):
                y = step * 2 + u
                block = jnp.concatenate([lows[p][y], owns[p][y], highs[p][y]], axis=0)
                out = dot32(z_band[...], block)
                for h, part in enumerate(halves(out)):
                    by_plane[h, pl.ds(p * rows_in + y, depths, stride=rows), :] = part
            return carry

        lax.fori_loop(0, rows_in // 2, z_pass, 0)

    def planes(first, measured, count):
        def body(step, carry):
            passed = []
            for g in range(GROUP):
                k = first + step * GROUP + g
                start = pl.multiple_of(k * rows, rows)
                plane = jnp.concatenate(
                    [by_plane[h, pl.ds(start, rows), :].astype(jnp.bfloat16) for h in range(lane_parts)],
                    axis=1,
                )
                passed.append(dot32(y_band[...], plane).astype(jnp.bfloat16))
            blurred = dot32(jnp.concatenate(passed, axis=0), x_band[...])
            ratios = []
            for g in range(GROUP):
                k = first + step * GROUP + g
                inside = mask_ref[k] > 0
                data = measured[step * GROUP + g].astype(jnp.float32)
                under = jnp.where(inside, blurred[g * rows : (g + 1) * rows], jnp.float32(1.0))
                ratios.append(jnp.where(inside, data / under, jnp.float32(0.0)).astype(jnp.bfloat16))
            back = dot32(jnp.concatenate(ratios, axis=0), x_back[...]).astype(jnp.bfloat16)
            for g in range(GROUP):
                k = first + step * GROUP + g
                out = dot32(y_back[...], back[g * rows : (g + 1) * rows])
                for h, part in enumerate(halves(out)):
                    by_row[h, pl.ds(k, rows, stride=depths), :] = part
            return carry

        lax.fori_loop(0, count // GROUP, body, 0)

    planes(0, meas_low, REACH)
    planes(REACH, meas_own, core)
    planes(REACH + core, meas_high, REACH)

    rows_out = rows // pieces_out
    for p in range(pieces_out):

        def z_return(step, carry, p=p):
            for u in range(2):
                y = step * 2 + u
                start = pl.multiple_of((p * rows_out + y) * depths, depths)
                column = jnp.concatenate(
                    [by_row[h, pl.ds(start, depths), :].astype(jnp.bfloat16) for h in range(lane_parts)],
                    axis=1,
                )
                term = dot32(z_back[...], column)
                top = jnp.maximum(jnp.max(jnp.abs(term), axis=0, keepdims=True), jnp.float32(1e-30))
                codes[p][y] = jnp.round(term * (LEVELS / top)).astype(jnp.int32).astype(jnp.int16)
                scales[p][pl.ds(y, 1), :] = top * jnp.float32(1.0 / LEVELS)
            return carry

        lax.fori_loop(0, rows_out // 2, z_return, 0)


def sweep(mask, lows, owns, highs, measured, bands, pieces_out):
    core, (rows, cols) = measured[1].shape[0], measured[1].shape[1:]
    depths = core + 2 * REACH
    plan = (len(owns), pieces_out, depths, core, rows, cols)
    rows_out = rows // pieces_out
    vmem = pl.BlockSpec(memory_space=pltpu.VMEM)
    out = pl.pallas_call(
        functools.partial(sweep_kernel, plan),
        out_shape=[jax.ShapeDtypeStruct((rows_out, core, cols), jnp.int16)] * pieces_out
        + [jax.ShapeDtypeStruct((rows_out, cols), jnp.float32)] * pieces_out,
        in_specs=[pl.BlockSpec(memory_space=pltpu.SMEM)] + [vmem] * (3 * len(owns) + 9),
        out_specs=[vmem] * (2 * pieces_out),
        scratch_shapes=[
            pltpu.VMEM((cols // LANES, depths * rows, LANES), jnp.float32),
            pltpu.VMEM((cols // LANES, rows * depths, LANES), jnp.float32),
        ],
        compiler_params=pltpu.CompilerParams(vmem_limit_bytes=56 * 1024 * 1024),
        name="sweep",
    )(mask, *lows, *owns, *highs, *measured, *bands)
    return out[:pieces_out], out[pieces_out:]


def band(taps, row_index, col_index):
    count = taps.shape[0]
    offsets = col_index[None, :] - row_index[:, None] + (count - 1) // 2
    chosen = offsets[None, :, :] == jnp.arange(count, dtype=jnp.int32)[:, None, None]
    return jnp.sum(jnp.where(chosen, taps[:, None, None], jnp.float32(0.0)), axis=0)


def encode(values, axis):
    top = jnp.maximum(jnp.max(jnp.abs(values), axis=axis, keepdims=True), jnp.float32(1e-30))
    code = jnp.round(values * (LEVELS / top)).astype(jnp.int32).astype(jnp.int16)
    return code, top * jnp.float32(1.0 / LEVELS)


def on_device(estimate, views_data, psf_bank, psf_index, margin_extent):
    core, rows, cols = estimate.shape
    kernels_count = psf_bank.shape[0]
    tiles = lax.axis_size("tile")
    views = lax.axis_size("view")
    tile_id = lax.axis_index("tile")
    view_id = lax.axis_index("view")
    rows_piece = rows // views
    forward = [(i, i + 1) for i in range(tiles - 1)]
    backward = [(target, source) for source, target in forward]

    def from_below(x):
        return lax.ppermute(x, "tile", forward)

    def from_above(x):
        return lax.ppermute(x, "tile", backward)

    def from_view(x, bits):
        return lax.ppermute(x, "view", [(v, v ^ bits) for v in range(views)])

    start = jnp.transpose(estimate.astype(jnp.bfloat16), (1, 0, 2))
    low, high = from_below(start), from_above(start)
    data = views_data[0]
    measured = (
        from_below(data[core - REACH :]),
        data,
        from_above(data[:REACH]),
    )

    chosen = (jnp.arange(kernels_count, dtype=jnp.int32) == psf_index[0]).astype(jnp.float32)
    taps = jnp.einsum("k,kat->at", chosen, psf_bank.astype(jnp.float32))
    position = jnp.arange(core + 2 * MARGIN, dtype=jnp.int32)
    global_pos = tile_id * core - MARGIN + position
    inside = (position >= MARGIN - margin_extent[0, 0]) & (
        position < MARGIN + core + margin_extent[0, 1]
    )
    inside = inside & (global_pos >= 0) & (global_pos < core * tiles)
    wanted = jnp.arange(core + 2 * REACH, dtype=jnp.int32) + (MARGIN - REACH)
    cores = jnp.arange(core, dtype=jnp.int32) + MARGIN
    natural = jnp.arange(rows, dtype=jnp.int32)
    held = ((natural // rows_piece) ^ view_id) * rows_piece + natural % rows_piece
    columns = jnp.arange(cols, dtype=jnp.int32)
    half = jnp.bfloat16
    z_band = jnp.where(inside[None, :], band(taps[0], wanted, position), 0.0).astype(half)
    z_back = band(taps[0], wanted, cores).T.astype(half)
    y_natural = band(taps[1], natural, natural).astype(half)
    y_held = band(taps[1], natural, held).astype(half)
    y_back = y_held.T
    x_back = band(taps[2], columns, columns).astype(half)
    x_band = x_back.T
    mask = lax.slice_in_dim(inside, MARGIN - REACH, MARGIN + core + REACH).astype(jnp.int32)

    mine = jnp.transpose(
        lax.dynamic_slice_in_dim(estimate, view_id * rows_piece, rows_piece, axis=1), (1, 0, 2)
    )
    lows, owns, highs = [low], [start], [high]
    for it in range(ITERS):
        bands = (z_band, z_back, y_natural if it == 0 else y_held, y_back, x_band, x_back)
        codes, scales = sweep(mask, lows, owns, highs, measured, bands, views)
        total = codes[0].astype(jnp.float32) * scales[0][:, None, :]
        for bits in range(1, views):
            code, scale = from_view(codes[bits], bits), from_view(scales[bits], bits)
            total = total + code.astype(jnp.float32) * scale[:, None, :]
        mine = mine * total / views
        if it + 1 < ITERS:
            rounded = mine.astype(half)
            owns = [rounded] + [from_view(rounded, bits) for bits in range(1, views)]
            lows = [from_below(x) for x in owns]
            highs = [from_above(x) for x in owns]
    code, scale = encode(jnp.transpose(mine, (1, 0, 2)), 0)
    out = jnp.zeros((core, rows, cols), jnp.float32)
    for bits in range(views):
        c, s = (code, scale) if bits == 0 else (from_view(code, bits), from_view(scale, bits))
        piece = c.astype(jnp.float32) * s
        out = lax.dynamic_update_slice_in_dim(out, piece, (view_id ^ bits) * rows_piece, axis=1)
    return out


def solution(mesh):
    return jax.shard_map(
        on_device,
        mesh=mesh,
        in_specs=(
            P("tile", None, None),
            P("view", "tile", None, None),
            P(),
            P("view"),
            P("tile", None),
        ),
        out_specs=P("tile", None, None),
        check_vma=False,
    )
```

profile of v0, /device:TPU:8, one launch (start us, length us, event | category | flops | bytes accessed | tf_op | source)
XLA Modules:
  0.0 293.1 jit_solution(13517571388459288243)
XLA Ops:
  0.0 4.6 %copy.32 = bf16[32,128,256]{2,0,1:T(8,128)(2,1)S(1)} copy(f32[32,128,256]{2,1,0:T(8,128)} %param.5) | data formatting | bytes 6291456 | tf_op args[0]
  4.6 2.1 collective-permute-start
  6.7 3.6 %collective-permute-start.1 = (bf16[128,32,256]{2,1,0:T(8,128)(2,1)S(1)}, bf16[128,32,256]{2,1,0:T(8,128)(2,1)}, u32[]{:S(2)}, u32[]{:S(2)}) collective-permute-start(bf16[128,32,256]{2,1,0:T(8,128)(2,1)S(1)} %bitcast.46), channel_id=1, source_target_pairs={{4,0},{8,4},{12,8},{16,12},{20,16},{24,20},{28,24},{5,1},{9,5},{13... | collective-permute-start | bytes 6291464 | tf_op jit(solution)/shard_map/ppermute | solution.py:155
  10.3 1.4 slice_bitcast_fusion
  11.8 1.9 collective-permute-start.2
  13.7 3.6 %collective-permute-start.3 = (bf16[16,128,256]{2,1,0:T(8,128)(2,1)}, bf16[16,128,256]{2,1,0:T(8,128)(2,1)}, u32[]{:S(2)}, u32[]{:S(2)}) collective-permute-start(bf16[16,128,256]{2,1,0:T(8,128)(2,1)} %get-tuple-element.45), channel_id=1, source_target_pairs={{4,0},{8,4},{12,8},{16,12},{20,16},{24,20},{28,24},{5,1},{9,5},{13... | collective-permute-start | bytes 3145736 | tf_op jit(solution)/shard_map/ppermute | solution.py:155
  18.2 1.1 select_reduce_fusion.1
  19.3 0.7 copy.17
  20.0 0.9 select_reduce_fusion.refs_12_.refs_21_
  20.9 0.8 copy.18.refs_11_.refs_20_
  21.7 0.7 fusion.14
  23.8 0.7 select_reduce_fusion.4
  24.8 0.6 slice_convert_fusion.refs_0_
  25.4 0.6 select_convert_fusion.refs_7_.refs_16_
  26.0 17.3 %collective-permute-done.2.refs_4_.refs_13_ = bf16[16,128,256]{2,1,0:T(8,128)(2,1)S(1)} collective-permute-done((bf16[16,128,256]{2,1,0:T(8,128)(2,1)}, bf16[16,128,256]{2,1,0:T(8,128)(2,1)S(1)}, u32[]{:S(2)}, u32[]{:S(2)}) %collective-permute-start.2) | collective-permute-done | bytes 1048608 | tf_op jit(solution)/shard_map/ppermute | solution.py:152
  43.3 1.9 collective-permute-done.3.refs_6_.refs_15_
  45.2 46.1 %sweep.2 = (s16[32,32,256]{2,1,0:T(8,128)(2,1)}, s16[32,32,256]{2,1,0:T(8,128)(2,1)}, s16[32,32,256]{2,1,0:T(8,128)(2,1)}, s16[32,32,256]{2,1,0:T(8,128)(2,1)}, ...) custom-call(s32[64]{0:T(128)} %slice_convert_fusion.refs_0_, ...), custom_call_target="tpu_custom_call" | custom-call | tf_op jit(solution)/shard_map/sweep/pallas_call | solution.py:111
  91.3 1.6 collective-permute-start.4
  92.8 1.5 collective-permute-start.6
  94.4 0.5 collective-permute-start.8
  94.8 1.5 collective-permute-start.5
  96.3 1.5 collective-permute-start.7
  97.9 19.6 %collective-permute-done.5 = f32[32,256]{1,0:T(8,128)S(1)} collective-permute-done((f32[32,256]{1,0:T(8,128)}, f32[32,256]{1,0:T(8,128)S(1)}, u32[]{:S(2)}, u32[]{:S(2)}) %collective-permute-start.5) | collective-permute-done | bytes 32800 | tf_op jit(solution)/shard_map/ppermute | solution.py:158
  117.5 2.4 collective-permute-start.9
  119.9 6.7 %copy.15 = f32[32,128,256]{2,0,1:T(8,128)} copy(f32[32,128,256]{2,1,0:T(8,128)} %param.5) | data formatting | bytes 8388608 | tf_op args[0]
  126.7 0.8 copy-done.15
  127.5 2.4 fusion.12
  129.8 0.6 collective-permute-start.11
  130.4 0.5 collective-permute-start.13
  130.9 2.5 collective-permute-start.15
  133.4 1.9 collective-permute-start.10
  135.3 3.8 %collective-permute-start.17 = (bf16[32,32,256]{2,1,0:T(8,128)(2,1)S(1)}, bf16[32,32,256]{2,1,0:T(8,128)(2,1)S(1)}, u32[]{:S(2)}, u32[]{:S(2)}) collective-permute-start(bf16[32,32,256]{2,1,0:T(8,128)(2,1)S(1)} %get-tuple-element.43.refs_5_), channel_id=1, source_target_pairs={{4,0},{8,4},{12,8},{16,12},{20,16},{24,20},{28,24},{5,1},{9,5},{13... | collective-permute-start | bytes 1572872 | tf_op jit(solution)/shard_map/ppermute | solution.py:155
  139.2 5.5 %collective-permute-done.11.refs_6_ = bf16[32,32,256]{2,1,0:T(8,128)(2,1)S(1)} collective-permute-done((bf16[32,32,256]{2,1,0:T(8,128)(2,1)S(1)}, bf16[32,32,256]{2,1,0:T(8,128)(2,1)S(1)}, u32[]{:S(2)}, u32[]{:S(2)}) %collective-permute-start.11) | collective-permute-done | bytes 524320 | tf_op jit(solution)/shard_map/ppermute | solution.py:158
  144.7 1.9 collective-permute-start.12
  146.6 9.3 %collective-permute-done.13.refs_7_ = bf16[32,32,256]{2,1,0:T(8,128)(2,1)S(1)} collective-permute-done((bf16[32,32,256]{2,1,0:T(8,128)(2,1)S(1)}, bf16[32,32,256]{2,1,0:T(8,128)(2,1)S(1)}, u32[]{:S(2)}, u32[]{:S(2)}) %collective-permute-start.13) | collective-permute-done | bytes 524320 | tf_op jit(solution)/shard_map/ppermute | solution.py:158
  155.9 1.9 collective-permute-start.18
  157.9 2.4 collective-permute-start.14
  160.3 3.1 %collective-permute-start.16 = (bf16[32,32,256]{2,1,0:T(8,128)(2,1)S(1)}, bf16[32,32,256]{2,1,0:T(8,128)(2,1)}, u32[]{:S(2)}, u32[]{:S(2)}) collective-permute-start(bf16[32,32,256]{2,1,0:T(8,128)(2,1)S(1)} %collective-permute-done.15.refs_8_), channel_id=1, source_target_pairs={{0,4},{4,8},{8,12},{12,16},{16,20},{20,24},{24,28},{1,5},{5,9},{9,... | collective-permute-start | bytes 1572872 | tf_op jit(solution)/shard_map/ppermute | solution.py:152
  163.5 2.5 collective-permute-start.19
  166.0 0.8 copy-done.13
  166.8 2.7 collective-permute-start.20
  169.5 0.7 copy.19.refs_18_
  170.2 3.9 %collective-permute-done.16.refs_4_ = bf16[32,32,256]{2,1,0:T(8,128)(2,1)} collective-permute-done((bf16[32,32,256]{2,1,0:T(8,128)(2,1)S(1)}, bf16[32,32,256]{2,1,0:T(8,128)(2,1)}, u32[]{:S(2)}, u32[]{:S(2)}) %collective-permute-start.16) | collective-permute-done | bytes 524320 | tf_op jit(solution)/shard_map/ppermute | solution.py:152
  174.1 4.1 %collective-permute-done.20.refs_12_ = bf16[32,32,256]{2,1,0:T(8,128)(2,1)} collective-permute-done((bf16[32,32,256]{2,1,0:T(8,128)(2,1)S(1)}, bf16[32,32,256]{2,1,0:T(8,128)(2,1)}, u32[]{:S(2)}, u32[]{:S(2)}) %collective-permute-start.20) | collective-permute-done | bytes 524320 | tf_op jit(solution)/shard_map/ppermute | solution.py:155
  178.2 46.1 %sweep.3 = (s16[32,32,256]{2,1,0:T(8,128)(2,1)}, s16[32,32,256]{2,1,0:T(8,128)(2,1)}, s16[32,32,256]{2,1,0:T(8,128)(2,1)}, s16[32,32,256]{2,1,0:T(8,128)(2,1)}, ...) custom-call(s32[64]{0:T(128)} %slice_convert_fusion.refs_0_, ...), custom_call_target="tpu_custom_call" | custom-call | tf_op jit(solution)/shard_map/sweep/pallas_call | solution.py:111
  224.3 1.5 collective-permute-start.21
  225.8 2.1 collective-permute-start.25
  227.8 1.4 collective-permute-start.22
  229.3 21.1 %collective-permute-done.22 = f32[32,256]{1,0:T(8,128)S(1)} collective-permute-done((f32[32,256]{1,0:T(8,128)}, f32[32,256]{1,0:T(8,128)S(1)}, u32[]{:S(2)}, u32[]{:S(2)}) %collective-permute-start.22) | collective-permute-done | bytes 32800 | tf_op jit(solution)/shard_map/ppermute | solution.py:158
  250.8 1.3 collective-permute-done.24
  252.0 3.5 %collective-permute-done.26 = f32[32,256]{1,0:T(8,128)S(1)} collective-permute-done((f32[32,256]{1,0:T(8,128)}, f32[32,256]{1,0:T(8,128)S(1)}, u32[]{:S(2)}, u32[]{:S(2)}) %collective-permute-start.26) | collective-permute-done | bytes 32800 | tf_op jit(solution)/shard_map/ppermute | solution.py:158
  255.6 2.1 abs_reduce_fusion
  258.0 1.5 collective-permute-start.27
  259.5 2.0 collective-permute-start.29
  261.5 0.9 collective-permute-start.32
  262.4 0.6 collective-permute-start.28
  263.0 0.5 broadcast_in_dim.103
  263.5 0.7 copy_dynamic-update-slice_fusion.3
  264.2 20.5 %collective-permute-done.28 = f32[1,32,256]{2,1,0:T(8,128)S(1)} collective-permute-done((f32[1,32,256]{2,1,0:T(8,128)S(1)}, f32[1,32,256]{2,1,0:T(8,128)S(1)}, u32[]{:S(2)}, u32[]{:S(2)}) %collective-permute-start.28) | collective-permute-done | bytes 32800 | tf_op jit(solution)/shard_map/ppermute | solution.py:158
  284.9 0.7 copy_dynamic-update-slice_fusion.2
  285.6 3.0 %collective-permute-done.30 = f32[1,32,256]{2,1,0:T(8,128)S(1)} collective-permute-done((f32[1,32,256]{2,1,0:T(8,128)S(1)}, f32[1,32,256]{2,1,0:T(8,128)S(1)}, u32[]{:S(2)}, u32[]{:S(2)}) %collective-permute-start.30) | collective-permute-done | bytes 32800 | tf_op jit(solution)/shard_map/ppermute | solution.py:158
  288.8 0.7 copy_dynamic-update-slice_fusion.1
  289.7 1.8 copy-done.4
  291.5 1.6 copy_dynamic-update-slice_fusion
  (76 shorter events, 1.9 us)
Async XLA Ops:
  0.0 18.0 %copy-start = (bf16[8,3,33]{2,0,1:T(8,128)(2,1)S(1)}, bf16[8,3,33]{2,0,1:T(8,128)(2,1)}, u32[]{:S(2)}) copy-start(bf16[8,3,33]{2,0,1:T(8,128)(2,1)} %param.7) | copy-start | bytes 4756
  0.0 10.3 %copy-start.1 = (bf16[1,32,128,256]{3,2,1,0:T(8,128)(2,1)S(1)}, bf16[1,32,128,256]{3,2,1,0:T(8,128)(2,1)}, u32[]{:S(2)}) copy-start(bf16[1,32,128,256]{3,2,1,0:T(8,128)(2,1)} %param.6) | copy-start | bytes 6291460
  4.6 40.6 %copy-start.2 = (bf16[32,128,256]{2,0,1:T(8,128)(2,1)}, bf16[32,128,256]{2,0,1:T(8,128)(2,1)S(1)}, u32[]{:S(2)}) copy-start(bf16[32,128,256]{2,0,1:T(8,128)(2,1)S(1)} %copy.32) | copy-start | bytes 6291460
  4.6 17.1 %copy-start.17 = (s32[1,2]{1,0:T(1,128)S(1)}, s32[1,2]{1,0:T(1,128)}, u32[]{:S(2)}) copy-start(s32[1,2]{1,0:T(1,128)} %param.9) | copy-start | bytes 28
  4.6 40.6 %collective-permute-start = (bf16[128,32,256]{2,1,0:T(8,128)(2,1)S(1)}, bf16[128,32,256]{2,1,0:T(8,128)(2,1)}, u32[]{:S(2)}, u32[]{:S(2)}) collective-permute-start(bf16[128,32,256]{2,1,0:T(8,128)(2,1)S(1)} %bitcast.45), channel_id=1, source_target_pairs={{0,4},{4,8},{8,12},{12,16},{16,20},{20,24},{24,28},{1,5},{5,9},{9,... | collective-permute-start | bytes 6291464 | tf_op jit(solution)/shard_map/ppermute | solution.py:152
  6.7 38.5 %collective-permute-start.1 = (bf16[128,32,256]{2,1,0:T(8,128)(2,1)S(1)}, bf16[128,32,256]{2,1,0:T(8,128)(2,1)}, u32[]{:S(2)}, u32[]{:S(2)}) collective-permute-start(bf16[128,32,256]{2,1,0:T(8,128)(2,1)S(1)} %bitcast.46), channel_id=1, source_target_pairs={{4,0},{8,4},{12,8},{16,12},{20,16},{24,20},{28,24},{5,1},{9,5},{13... | collective-permute-start | bytes 6291464 | tf_op jit(solution)/shard_map/ppermute | solution.py:155
  11.8 31.6 %collective-permute-start.2 = (bf16[16,128,256]{2,1,0:T(8,128)(2,1)}, bf16[16,128,256]{2,1,0:T(8,128)(2,1)S(1)}, u32[]{:S(2)}, u32[]{:S(2)}) collective-permute-start(bf16[16,128,256]{2,1,0:T(8,128)(2,1)} %get-tuple-element.46), channel_id=1, source_target_pairs={{0,4},{4,8},{8,12},{12,16},{16,20},{20,24},{24,28},{1,5},{5,9},{9,... | collective-permute-start | bytes 3145736 | tf_op jit(solution)/shard_map/ppermute | solution.py:152
  13.7 31.5 %collective-permute-start.3 = (bf16[16,128,256]{2,1,0:T(8,128)(2,1)}, bf16[16,128,256]{2,1,0:T(8,128)(2,1)}, u32[]{:S(2)}, u32[]{:S(2)}) collective-permute-start(bf16[16,128,256]{2,1,0:T(8,128)(2,1)} %get-tuple-element.45), channel_id=1, source_target_pairs={{4,0},{8,4},{12,8},{16,12},{20,16},{24,20},{28,24},{5,1},{9,5},{13... | collective-permute-start | bytes 3145736 | tf_op jit(solution)/shard_map/ppermute | solution.py:155
  20.9 24.3 %copy-start.5 = (bf16[256,256]{1,0:T(8,128)(2,1)}, bf16[256,256]{1,0:T(8,128)(2,1)S(1)}, u32[]{:S(2)}) copy-start(bf16[256,256]{1,0:T(8,128)(2,1)S(1)} %select_reduce_fusion.refs_12_.refs_21_) | copy-start | bytes 393220
  43.3 1.9 copy-start.3
  91.3 35.3 %collective-permute-start.4 = (s16[32,32,256]{2,1,0:T(8,128)(2,1)}, s16[32,32,256]{2,1,0:T(8,128)(2,1)S(1)}, u32[]{:S(2)}, u32[]{:S(2)}) collective-permute-start(s16[32,32,256]{2,1,0:T(8,128)(2,1)} %get-tuple-element.23), channel_id=1, source_target_pairs={{0,1},{1,0},{2,3},{3,2},{4,5},{5,4},{6,7},{7,6},{8,9},{9,8},{10,11... | collective-permute-start | bytes 1572872 | tf_op jit(solution)/shard_map/ppermute | solution.py:158
  92.8 33.8 %collective-permute-start.6 = (s16[32,32,256]{2,1,0:T(8,128)(2,1)}, s16[32,32,256]{2,1,0:T(8,128)(2,1)S(1)}, u32[]{:S(2)}, u32[]{:S(2)}) collective-permute-start(s16[32,32,256]{2,1,0:T(8,128)(2,1)} %get-tuple-element.25), channel_id=1, source_target_pairs={{0,2},{1,3},{2,0},{3,1},{4,6},{5,7},{6,4},{7,5},{8,10},{9,11},{10,... | collective-permute-start | bytes 1572872 | tf_op jit(solution)/shard_map/ppermute | solution.py:158
  94.4 32.3 %collective-permute-start.8 = (s16[32,32,256]{2,1,0:T(8,128)(2,1)}, s16[32,32,256]{2,1,0:T(8,128)(2,1)S(1)}, u32[]{:S(2)}, u32[]{:S(2)}) collective-permute-start(s16[32,32,256]{2,1,0:T(8,128)(2,1)} %get-tuple-element.27), channel_id=1, source_target_pairs={{0,3},{1,2},{2,1},{3,0},{4,7},{5,6},{6,5},{7,4},{8,11},{9,10},{10,... | collective-permute-start | bytes 1572872 | tf_op jit(solution)/shard_map/ppermute | solution.py:158
  94.8 22.6 %collective-permute-start.5 = (f32[32,256]{1,0:T(8,128)}, f32[32,256]{1,0:T(8,128)S(1)}, u32[]{:S(2)}, u32[]{:S(2)}) collective-permute-start(f32[32,256]{1,0:T(8,128)} %get-tuple-element.24), channel_id=1, source_target_pairs={{0,1},{1,0},{2,3},{3,2},{4,5},{5,4},{6,7},{7,6},{8,9},{9,8},{10,11... | collective-permute-start | bytes 98312 | tf_op jit(solution)/shard_map/ppermute | solution.py:158
  96.3 30.3 %collective-permute-start.7 = (f32[32,256]{1,0:T(8,128)}, f32[32,256]{1,0:T(8,128)S(1)}, u32[]{:S(2)}, u32[]{:S(2)}) collective-permute-start(f32[32,256]{1,0:T(8,128)} %get-tuple-element.26), channel_id=1, source_target_pairs={{0,2},{1,3},{2,0},{3,1},{4,6},{5,7},{6,4},{7,5},{8,10},{9,11},{10,... | collective-permute-start | bytes 98312 | tf_op jit(solution)/shard_map/ppermute | solution.py:158
  117.5 9.1 %collective-permute-start.9 = (f32[32,256]{1,0:T(8,128)}, f32[32,256]{1,0:T(8,128)S(1)}, u32[]{:S(2)}, u32[]{:S(2)}) collective-permute-start(f32[32,256]{1,0:T(8,128)} %get-tuple-element.28), channel_id=1, source_target_pairs={{0,3},{1,2},{2,1},{3,0},{4,7},{5,6},{6,5},{7,4},{8,11},{9,10},{10,... | collective-permute-start | bytes 98312 | tf_op jit(solution)/shard_map/ppermute | solution.py:158
  119.9 7.5 %copy-start.14 = (s16[32,32,256]{2,1,0:T(8,128)(2,1)S(1)}, s16[32,32,256]{2,1,0:T(8,128)(2,1)}, u32[]{:S(2)}) copy-start(s16[32,32,256]{2,1,0:T(8,128)(2,1)} %get-tuple-element.21) | copy-start | bytes 1572868
  119.9 7.5 %copy-start.16 = (f32[32,256]{1,0:T(8,128)S(1)}, f32[32,256]{1,0:T(8,128)}, u32[]{:S(2)}) copy-start(f32[32,256]{1,0:T(8,128)} %get-tuple-element.22) | copy-start | bytes 98308
  126.6 42.8 %copy-start.7 = (bf16[128,128]{0,1:T(8,128)(2,1)S(1)}, bf16[128,128]{0,1:T(8,128)(2,1)}, u32[]{:S(2)}) copy-start(bf16[128,128]{0,1:T(8,128)(2,1)} %copy.17) | copy-start | bytes 98308
  126.7 0.8 copy-start.15
  129.8 48.4 %copy-start.6 = (bf16[32,32,256]{2,1,0:T(8,128)(2,1)}, bf16[32,32,256]{2,1,0:T(8,128)(2,1)S(1)}, u32[]{:S(2)}) copy-start(bf16[32,32,256]{2,1,0:T(8,128)(2,1)S(1)} %get-tuple-element.43.refs_5_) | copy-start | bytes 1572868
  129.8 14.9 %collective-permute-start.11 = (bf16[32,32,256]{2,1,0:T(8,128)(2,1)S(1)}, bf16[32,32,256]{2,1,0:T(8,128)(2,1)S(1)}, u32[]{:S(2)}, u32[]{:S(2)}) collective-permute-start(bf16[32,32,256]{2,1,0:T(8,128)(2,1)S(1)} %get-tuple-element.43.refs_5_), channel_id=1, source_target_pairs={{0,1},{1,0},{2,3},{3,2},{4,5},{5,4},{6,7},{7,6},{8,9},{9,8},{10,11... | collective-permute-start | bytes 1572872 | tf_op jit(solution)/shard_map/ppermute | solution.py:158
  130.4 25.5 %collective-permute-start.13 = (bf16[32,32,256]{2,1,0:T(8,128)(2,1)S(1)}, bf16[32,32,256]{2,1,0:T(8,128)(2,1)S(1)}, u32[]{:S(2)}, u32[]{:S(2)}) collective-permute-start(bf16[32,32,256]{2,1,0:T(8,128)(2,1)S(1)} %get-tuple-element.43.refs_5_), channel_id=1, source_target_pairs={{0,2},{1,3},{2,0},{3,1},{4,6},{5,7},{6,4},{7,5},{8,10},{9,11},{10,... | collective-permute-start | bytes 1572872 | tf_op jit(solution)/shard_map/ppermute | solution.py:158
  130.9 26.9 %collective-permute-start.15 = (bf16[32,32,256]{2,1,0:T(8,128)(2,1)S(1)}, bf16[32,32,256]{2,1,0:T(8,128)(2,1)S(1)}, u32[]{:S(2)}, u32[]{:S(2)}) collective-permute-start(bf16[32,32,256]{2,1,0:T(8,128)(2,1)S(1)} %get-tuple-element.43.refs_5_), channel_id=1, source_target_pairs={{0,3},{1,2},{2,1},{3,0},{4,7},{5,6},{6,5},{7,4},{8,11},{9,10},{10,... | collective-permute-start | bytes 1572872 | tf_op jit(solution)/shard_map/ppermute | solution.py:158
  133.4 26.9 %collective-permute-start.10 = (bf16[32,32,256]{2,1,0:T(8,128)(2,1)S(1)}, bf16[32,32,256]{2,1,0:T(8,128)(2,1)S(1)}, u32[]{:S(2)}, u32[]{:S(2)}) collective-permute-start(bf16[32,32,256]{2,1,0:T(8,128)(2,1)S(1)} %get-tuple-element.43.refs_5_), channel_id=1, source_target_pairs={{0,4},{4,8},{8,12},{12,16},{16,20},{20,24},{24,28},{1,5},{5,9},{9,... | collective-permute-start | bytes 1572872 | tf_op jit(solution)/shard_map/ppermute | solution.py:152
  135.3 28.1 %collective-permute-start.17 = (bf16[32,32,256]{2,1,0:T(8,128)(2,1)S(1)}, bf16[32,32,256]{2,1,0:T(8,128)(2,1)S(1)}, u32[]{:S(2)}, u32[]{:S(2)}) collective-permute-start(bf16[32,32,256]{2,1,0:T(8,128)(2,1)S(1)} %get-tuple-element.43.refs_5_), channel_id=1, source_target_pairs={{4,0},{8,4},{12,8},{16,12},{20,16},{24,20},{28,24},{5,1},{9,5},{13... | collective-permute-start | bytes 1572872 | tf_op jit(solution)/shard_map/ppermute | solution.py:155
  144.7 33.5 %copy-start.8 = (bf16[32,32,256]{2,1,0:T(8,128)(2,1)}, bf16[32,32,256]{2,1,0:T(8,128)(2,1)S(1)}, u32[]{:S(2)}) copy-start(bf16[32,32,256]{2,1,0:T(8,128)(2,1)S(1)} %collective-permute-done.11.refs_6_) | copy-start | bytes 1572868
  144.7 21.2 %collective-permute-start.12 = (bf16[32,32,256]{2,1,0:T(8,128)(2,1)S(1)}, bf16[32,32,256]{2,1,0:T(8,128)(2,1)S(1)}, u32[]{:S(2)}, u32[]{:S(2)}) collective-permute-start(bf16[32,32,256]{2,1,0:T(8,128)(2,1)S(1)} %collective-permute-done.11.refs_6_), channel_id=1, source_target_pairs={{0,4},{4,8},{8,12},{12,16},{16,20},{20,24},{24,28},{1,5},{5,9},{9,... | collective-permute-start | bytes 1572872 | tf_op jit(solution)/shard_map/ppermute | solution.py:152
  155.9 22.3 %copy-start.9 = (bf16[32,32,256]{2,1,0:T(8,128)(2,1)}, bf16[32,32,256]{2,1,0:T(8,128)(2,1)S(1)}, u32[]{:S(2)}) copy-start(bf16[32,32,256]{2,1,0:T(8,128)(2,1)S(1)} %collective-permute-done.13.refs_7_) | copy-start | bytes 1572868
  155.9 18.2 %collective-permute-start.18 = (bf16[32,32,256]{2,1,0:T(8,128)(2,1)S(1)}, bf16[32,32,256]{2,1,0:T(8,128)(2,1)}, u32[]{:S(2)}, u32[]{:S(2)}) collective-permute-start(bf16[32,32,256]{2,1,0:T(8,128)(2,1)S(1)} %collective-permute-done.11.refs_6_), channel_id=1, source_target_pairs={{4,0},{8,4},{12,8},{16,12},{20,16},{24,20},{28,24},{5,1},{9,5},{13... | collective-permute-start | bytes 1572872 | tf_op jit(solution)/shard_map/ppermute | solution.py:155
  157.9 20.4 %copy-start.10 = (bf16[32,32,256]{2,1,0:T(8,128)(2,1)}, bf16[32,32,256]{2,1,0:T(8,128)(2,1)S(1)}, u32[]{:S(2)}) copy-start(bf16[32,32,256]{2,1,0:T(8,128)(2,1)S(1)} %collective-permute-done.15.refs_8_) | copy-start | bytes 1572868
  157.9 12.3 %collective-permute-start.14 = (bf16[32,32,256]{2,1,0:T(8,128)(2,1)S(1)}, bf16[32,32,256]{2,1,0:T(8,128)(2,1)}, u32[]{:S(2)}, u32[]{:S(2)}) collective-permute-start(bf16[32,32,256]{2,1,0:T(8,128)(2,1)S(1)} %collective-permute-done.13.refs_7_), channel_id=1, source_target_pairs={{0,4},{4,8},{8,12},{12,16},{16,20},{20,24},{24,28},{1,5},{5,9},{9,... | collective-permute-start | bytes 1572872 | tf_op jit(solution)/shard_map/ppermute | solution.py:152
  160.3 5.6 %copy-start.11 = (bf16[32,32,256]{2,1,0:T(8,128)(2,1)}, bf16[32,32,256]{2,1,0:T(8,128)(2,1)S(1)}, u32[]{:S(2)}) copy-start(bf16[32,32,256]{2,1,0:T(8,128)(2,1)S(1)} %collective-permute-done.10.refs_1_) | copy-start | bytes 1572868
  160.3 13.8 %collective-permute-start.16 = (bf16[32,32,256]{2,1,0:T(8,128)(2,1)S(1)}, bf16[32,32,256]{2,1,0:T(8,128)(2,1)}, u32[]{:S(2)}, u32[]{:S(2)}) collective-permute-start(bf16[32,32,256]{2,1,0:T(8,128)(2,1)S(1)} %collective-permute-done.15.refs_8_), channel_id=1, source_target_pairs={{0,4},{4,8},{8,12},{12,16},{16,20},{20,24},{24,28},{1,5},{5,9},{9,... | collective-permute-start | bytes 1572872 | tf_op jit(solution)/shard_map/ppermute | solution.py:152
  163.4 2.5 copy-start.12
  163.5 10.7 %collective-permute-start.19 = (bf16[32,32,256]{2,1,0:T(8,128)(2,1)S(1)}, bf16[32,32,256]{2,1,0:T(8,128)(2,1)}, u32[]{:S(2)}, u32[]{:S(2)}) collective-permute-start(bf16[32,32,256]{2,1,0:T(8,128)(2,1)S(1)} %collective-permute-done.13.refs_7_), channel_id=1, source_target_pairs={{4,0},{8,4},{12,8},{16,12},{20,16},{24,20},{28,24},{5,1},{9,5},{13... | collective-permute-start | bytes 1572872 | tf_op jit(solution)/shard_map/ppermute | solution.py:155
  166.0 0.8 copy-start.13
  166.8 11.5 %collective-permute-start.20 = (bf16[32,32,256]{2,1,0:T(8,128)(2,1)S(1)}, bf16[32,32,256]{2,1,0:T(8,128)(2,1)}, u32[]{:S(2)}, u32[]{:S(2)}) collective-permute-start(bf16[32,32,256]{2,1,0:T(8,128)(2,1)S(1)} %collective-permute-done.15.refs_8_), channel_id=1, source_target_pairs={{4,0},{8,4},{12,8},{16,12},{20,16},{24,20},{28,24},{5,1},{9,5},{13... | collective-permute-start | bytes 1572872 | tf_op jit(solution)/shard_map/ppermute | solution.py:155
  224.3 31.3 %collective-permute-start.21 = (s16[32,32,256]{2,1,0:T(8,128)(2,1)}, s16[32,32,256]{2,1,0:T(8,128)(2,1)S(1)}, u32[]{:S(2)}, u32[]{:S(2)}) collective-permute-start(s16[32,32,256]{2,1,0:T(8,128)(2,1)} %get-tuple-element.31), channel_id=1, source_target_pairs={{0,1},{1,0},{2,3},{3,2},{4,5},{5,4},{6,7},{7,6},{8,9},{9,8},{10,11... | collective-permute-start | bytes 1572872 | tf_op jit(solution)/shard_map/ppermute | solution.py:158
  225.8 29.8 %collective-permute-start.23 = (s16[32,32,256]{2,1,0:T(8,128)(2,1)}, s16[32,32,256]{2,1,0:T(8,128)(2,1)S(1)}, u32[]{:S(2)}, u32[]{:S(2)}) collective-permute-start(s16[32,32,256]{2,1,0:T(8,128)(2,1)} %get-tuple-element.33), channel_id=1, source_target_pairs={{0,2},{1,3},{2,0},{3,1},{4,6},{5,7},{6,4},{7,5},{8,10},{9,11},{10,... | collective-permute-start | bytes 1572872 | tf_op jit(solution)/shard_map/ppermute | solution.py:158
  225.8 29.8 %collective-permute-start.25 = (s16[32,32,256]{2,1,0:T(8,128)(2,1)}, s16[32,32,256]{2,1,0:T(8,128)(2,1)S(1)}, u32[]{:S(2)}, u32[]{:S(2)}) collective-permute-start(s16[32,32,256]{2,1,0:T(8,128)(2,1)} %get-tuple-element.35), channel_id=1, source_target_pairs={{0,3},{1,2},{2,1},{3,0},{4,7},{5,6},{6,5},{7,4},{8,11},{9,10},{10,... | collective-permute-start | bytes 1572872 | tf_op jit(solution)/shard_map/ppermute | solution.py:158
  227.8 22.5 %collective-permute-start.22 = (f32[32,256]{1,0:T(8,128)}, f32[32,256]{1,0:T(8,128)S(1)}, u32[]{:S(2)}, u32[]{:S(2)}) collective-permute-start(f32[32,256]{1,0:T(8,128)} %get-tuple-element.32), channel_id=1, source_target_pairs={{0,1},{1,0},{2,3},{3,2},{4,5},{5,4},{6,7},{7,6},{8,9},{9,8},{10,11... | collective-permute-start | bytes 98312 | tf_op jit(solution)/shard_map/ppermute | solution.py:158
  229.3 22.8 %collective-permute-start.24 = (f32[32,256]{1,0:T(8,128)}, f32[32,256]{1,0:T(8,128)S(1)}, u32[]{:S(2)}, u32[]{:S(2)}) collective-permute-start(f32[32,256]{1,0:T(8,128)} %get-tuple-element.34), channel_id=1, source_target_pairs={{0,2},{1,3},{2,0},{3,1},{4,6},{5,7},{6,4},{7,5},{8,10},{9,11},{10,... | collective-permute-start | bytes 98312 | tf_op jit(solution)/shard_map/ppermute | solution.py:158
  250.3 5.2 %collective-permute-start.26 = (f32[32,256]{1,0:T(8,128)}, f32[32,256]{1,0:T(8,128)S(1)}, u32[]{:S(2)}, u32[]{:S(2)}) collective-permute-start(f32[32,256]{1,0:T(8,128)} %get-tuple-element.36), channel_id=1, source_target_pairs={{0,3},{1,2},{2,1},{3,0},{4,7},{5,6},{6,5},{7,4},{8,11},{9,10},{10,... | collective-permute-start | bytes 98312 | tf_op jit(solution)/shard_map/ppermute | solution.py:158
  258.0 26.7 %collective-permute-start.27 = (s16[32,32,256]{2,0,1:T(8,128)(2,1)S(1)}, s16[32,32,256]{2,0,1:T(8,128)(2,1)S(1)}, u32[]{:S(2)}, u32[]{:S(2)}) collective-permute-start(s16[32,32,256]{2,0,1:T(8,128)(2,1)S(1)} %get-tuple-element.40), channel_id=1, source_target_pairs={{0,1},{1,0},{2,3},{3,2},{4,5},{5,4},{6,7},{7,6},{8,9},{9,8},{10,11... | collective-permute-start | bytes 1572872 | tf_op jit(solution)/shard_map/ppermute | solution.py:158
  259.5 30.0 %collective-permute-start.31 = (s16[32,32,256]{2,0,1:T(8,128)(2,1)S(1)}, s16[32,32,256]{2,0,1:T(8,128)(2,1)S(1)}, u32[]{:S(2)}, u32[]{:S(2)}) collective-permute-start(s16[32,32,256]{2,0,1:T(8,128)(2,1)S(1)} %get-tuple-element.40), channel_id=1, source_target_pairs={{0,3},{1,2},{2,1},{3,0},{4,7},{5,6},{6,5},{7,4},{8,11},{9,10},{10,... | collective-permute-start | bytes 1572872 | tf_op jit(solution)/shard_map/ppermute | solution.py:158
  259.5 29.1 %collective-permute-start.29 = (s16[32,32,256]{2,0,1:T(8,128)(2,1)S(1)}, s16[32,32,256]{2,0,1:T(8,128)(2,1)S(1)}, u32[]{:S(2)}, u32[]{:S(2)}) collective-permute-start(s16[32,32,256]{2,0,1:T(8,128)(2,1)S(1)} %get-tuple-element.40), channel_id=1, source_target_pairs={{0,2},{1,3},{2,0},{3,1},{4,6},{5,7},{6,4},{7,5},{8,10},{9,11},{10,... | collective-permute-start | bytes 1572872 | tf_op jit(solution)/shard_map/ppermute | solution.py:158
  261.5 28.0 %collective-permute-start.32 = (f32[1,32,256]{2,1,0:T(8,128)S(1)}, f32[1,32,256]{2,1,0:T(8,128)S(1)}, u32[]{:S(2)}, u32[]{:S(2)}) collective-permute-start(f32[1,32,256]{2,1,0:T(8,128)S(1)} %get-tuple-element.47), channel_id=1, source_target_pairs={{0,3},{1,2},{2,1},{3,0},{4,7},{5,6},{6,5},{7,4},{8,11},{9,10},{10,... | collective-permute-start | bytes 98312 | tf_op jit(solution)/shard_map/ppermute | solution.py:158
  262.4 22.3 %collective-permute-start.28 = (f32[1,32,256]{2,1,0:T(8,128)S(1)}, f32[1,32,256]{2,1,0:T(8,128)S(1)}, u32[]{:S(2)}, u32[]{:S(2)}) collective-permute-start(f32[1,32,256]{2,1,0:T(8,128)S(1)} %get-tuple-element.47), channel_id=1, source_target_pairs={{0,1},{1,0},{2,3},{3,2},{4,5},{5,4},{6,7},{7,6},{8,9},{9,8},{10,11... | collective-permute-start | bytes 98312 | tf_op jit(solution)/shard_map/ppermute | solution.py:158
  284.7 3.9 %collective-permute-start.30 = (f32[1,32,256]{2,1,0:T(8,128)S(1)}, f32[1,32,256]{2,1,0:T(8,128)S(1)}, u32[]{:S(2)}, u32[]{:S(2)}) collective-permute-start(f32[1,32,256]{2,1,0:T(8,128)S(1)} %get-tuple-element.47), channel_id=1, source_target_pairs={{0,2},{1,3},{2,0},{3,1},{4,6},{5,7},{6,4},{7,5},{8,10},{9,11},{10,... | collective-permute-start | bytes 98312 | tf_op jit(solution)/shard_map/ppermute | solution.py:158
  289.5 2.0 copy-start.4
where the time goes:
time: 294 us; the launch traced here: 293 us
  waiting for transfers between devices  111 us (38%)
  Pallas kernels  92.1 us (31%)
  starting transfers between devices  54.4 us (19%)
  local copies, waits for them, and re-layouts  23.2 us (8%)
  other arithmetic  9.66 us (3%)
    pallas_call x2, Pallas kernels, sweep(): pl.pallas_call(functools.partial(sweep_kernel, plan), out_shape=[jax.Shap...  92.1 us
    ppermute x21, waiting for transfers between devices, from_view(): return lax.ppermute(x, 'view', [(v, v ^ bits) for v in range(views)])  83.9 us
    ppermute x21, starting transfers between devices, from_view(): return lax.ppermute(x, 'view', [(v, v ^ bits) for v in range(views)])  23 us
    ppermute x6, waiting for transfers between devices, from_below(): return lax.ppermute(x, 'tile', forward)  21.2 us
    ppermute x6, starting transfers between devices, from_above(): return lax.ppermute(x, 'tile', backward)  18.2 us
    unnamed x38, local copies, waits for them, and re-layouts  14.7 us
    ppermute x6, starting transfers between devices, from_below(): return lax.ppermute(x, 'tile', forward)  13.3 us
    ppermute x6, waiting for transfers between devices, from_above(): return lax.ppermute(x, 'tile', backward)  5.97 us
  transfers between devices with their start and end apart: 33, of which 12 were waited for; matrix products, arithmetic and copies ran while one was open for 6% of the time, Pallas kernels for 0%

commit v1 on v0

--- a/solution.py
+++ b/solution.py
@@ -12,7 +12,9 @@
 REACH = 16
 LEVELS = 32766.0
 LANES = 128
-GROUP = 4
+GROUP = 16
+UNROLL = 32
+PAD = 8
 
 
 def dot32(a, b):
@@ -34,27 +36,29 @@
     codes, scales = take(pieces_out), take(pieces_out)
     by_plane, by_row = take(2)
     lane_parts = cols // LANES
+    plane_rows, row_depths = rows + PAD, depths + PAD
 
     rows_in = rows // pieces_in
+    unroll_in = min(UNROLL, rows_in)
     for p in range(pieces_in):
 
         def z_pass(step, carry, p=p):
-            for u in range(2):
-                y = step * 2 + u
+            for u in range(unroll_in):
+                y = step * unroll_in + u
                 block = jnp.concatenate([lows[p][y], owns[p][y], highs[p][y]], axis=0)
                 out = dot32(z_band[...], block)
                 for h, part in enumerate(halves(out)):
-                    by_plane[h, pl.ds(p * rows_in + y, depths, stride=rows), :] = part
+                    by_plane[h, pl.ds(p * rows_in + y, depths, stride=plane_rows), :] = part
             return carry
 
-        lax.fori_loop(0, rows_in // 2, z_pass, 0)
+        lax.fori_loop(0, rows_in // unroll_in, z_pass, 0)
 
     def planes(first, measured, count):
         def body(step, carry):
             passed = []
             for g in range(GROUP):
                 k = first + step * GROUP + g
-                start = pl.multiple_of(k * rows, rows)
+                start = pl.multiple_of(k * plane_rows, PAD)
                 plane = jnp.concatenate(
                     [by_plane[h, pl.ds(start, rows), :].astype(jnp.bfloat16) for h in range(lane_parts)],
                     axis=1,
@@ -73,7 +77,7 @@
                 k = first + step * GROUP + g
                 out = dot32(y_back[...], back[g * rows : (g + 1) * rows])
                 for h, part in enumerate(halves(out)):
-                    by_row[h, pl.ds(k, rows, stride=depths), :] = part
+                    by_row[h, pl.ds(k, rows, stride=row_depths), :] = part
             return carry
 
         lax.fori_loop(0, count // GROUP, body, 0)
@@ -83,12 +87,13 @@
     planes(REACH + core, meas_high, REACH)
 
     rows_out = rows // pieces_out
+    unroll_out = min(UNROLL, rows_out)
     for p in range(pieces_out):
 
         def z_return(step, carry, p=p):
-            for u in range(2):
-                y = step * 2 + u
-                start = pl.multiple_of((p * rows_out + y) * depths, depths)
+            for u in range(unroll_out):
+                y = step * unroll_out + u
+                start = pl.multiple_of((p * rows_out + y) * row_depths, PAD)
                 column = jnp.concatenate(
                     [by_row[h, pl.ds(start, depths), :].astype(jnp.bfloat16) for h in range(lane_parts)],
                     axis=1,
@@ -99,7 +104,7 @@
                 scales[p][pl.ds(y, 1), :] = top * jnp.float32(1.0 / LEVELS)
             return carry
 
-        lax.fori_loop(0, rows_out // 2, z_return, 0)
+        lax.fori_loop(0, rows_out // unroll_out, z_return, 0)
 
 
 def sweep(mask, lows, owns, highs, measured, bands, pieces_out):
@@ -115,8 +120,8 @@
         in_specs=[pl.BlockSpec(memory_space=pltpu.SMEM)] + [vmem] * (3 * len(owns) + 9),
         out_specs=[vmem] * (2 * pieces_out),
         scratch_shapes=[
-            pltpu.VMEM((cols // LANES, depths * rows, LANES), jnp.float32),
-            pltpu.VMEM((cols // LANES, rows * depths, LANES), jnp.float32),
+            pltpu.VMEM((cols // LANES, depths * (rows + PAD), LANES), jnp.float32),
+            pltpu.VMEM((cols // LANES, rows * (depths + PAD), LANES), jnp.float32),
         ],
         compiler_params=pltpu.CompilerParams(vmem_limit_bytes=56 * 1024 * 1024),
         name="sweep",
@@ -157,14 +162,14 @@
     def from_view(x, bits):
         return lax.ppermute(x, "view", [(v, v ^ bits) for v in range(views)])
 
-    start = jnp.transpose(estimate.astype(jnp.bfloat16), (1, 0, 2))
-    low, high = from_below(start), from_above(start)
     data = views_data[0]
     measured = (
         from_below(data[core - REACH :]),
         data,
         from_above(data[:REACH]),
     )
+    start = jnp.transpose(estimate.astype(jnp.bfloat16), (1, 0, 2))
+    low, high = from_below(start), from_above(start)
 
     chosen = (jnp.arange(kernels_count, dtype=jnp.int32) == psf_index[0]).astype(jnp.float32)
     taps = jnp.einsum("k,kat->at", chosen, psf_bank.astype(jnp.float32))

time: 294 us -> 230 us (0.78)
  Pallas kernels: 92.1 us -> 28.6 us
    pallas_call x2, Pallas kernels: 92.1 us -> 28.6 us  [sweep(): pl.pallas_call(functools.partial(sweep_kernel, plan), out_shape=[jax.Shap...]
  transfers between devices with their start and end apart: 33 -> 33, of which waited for: 12 -> 12; matrix products, arithmetic and copies ran while one was open for 6% -> 8% of each run, Pallas kernels for 0% -> 0%
where the time goes in v1:
time: 230 us
  waiting for transfers between devices  111 us (48%)
  starting transfers between devices  54.5 us (24%)
  Pallas kernels  28.6 us (12%)
  local copies, waits for them, and re-layouts  23.2 us (10%)
  other arithmetic  9.66 us (4%)
  between operations  2.44 us (1%)
    ppermute x21, waiting for transfers between devices, from_view(): return lax.ppermute(x, 'view', [(v, v ^ bits) for v in range(views)])  84.1 us
    pallas_call x2, Pallas kernels, sweep(): pl.pallas_call(functools.partial(sweep_kernel, plan), out_shape=[jax.Shap...  28.6 us
    ppermute x21, starting transfers between devices, from_view(): return lax.ppermute(x, 'view', [(v, v ^ bits) for v in range(views)])  23 us
    ppermute x6, waiting for transfers between devices, from_below(): return lax.ppermute(x, 'tile', forward)  21 us
    ppermute x6, starting transfers between devices, from_above(): return lax.ppermute(x, 'tile', backward)  18.2 us
    unnamed x38, local copies, waits for them, and re-layouts  14.7 us
    ppermute x6, starting transfers between devices, from_below(): return lax.ppermute(x, 'tile', forward)  13.3 us
    ppermute x6, waiting for transfers between devices, from_above(): return lax.ppermute(x, 'tile', backward)  5.97 us
  transfers between devices with their start and end apart: 33, of which 12 were waited for; matrix products, arithmetic and copies ran while one was open for 8% of the time, Pallas kernels for 0%

profile of v1, /device:TPU:8, one launch (start us, length us, event | category | flops | bytes accessed | tf_op | source)
XLA Modules:
  0.0 229.6 jit_solution(7402196877685535382)
XLA Ops:
  0.0 4.6 %copy.32 = bf16[32,128,256]{2,0,1:T(8,128)(2,1)S(1)} copy(f32[32,128,256]{2,1,0:T(8,128)} %param.5) | data formatting | bytes 6291456 | tf_op args[0]
  4.6 2.1 collective-permute-start
  6.7 3.6 %collective-permute-start.1 = (bf16[128,32,256]{2,1,0:T(8,128)(2,1)S(1)}, bf16[128,32,256]{2,1,0:T(8,128)(2,1)}, u32[]{:S(2)}, u32[]{:S(2)}) collective-permute-start(bf16[128,32,256]{2,1,0:T(8,128)(2,1)S(1)} %bitcast.46), channel_id=1, source_target_pairs={{4,0},{8,4},{12,8},{16,12},{20,16},{24,20},{28,24},{5,1},{9,5},{13... | collective-permute-start | bytes 6291464 | tf_op jit(solution)/shard_map/ppermute | solution.py:160
  10.3 1.4 slice_bitcast_fusion
  11.8 1.9 collective-permute-start.2
  13.7 3.6 %collective-permute-start.3 = (bf16[16,128,256]{2,1,0:T(8,128)(2,1)}, bf16[16,128,256]{2,1,0:T(8,128)(2,1)}, u32[]{:S(2)}, u32[]{:S(2)}) collective-permute-start(bf16[16,128,256]{2,1,0:T(8,128)(2,1)} %get-tuple-element.45), channel_id=1, source_target_pairs={{4,0},{8,4},{12,8},{16,12},{20,16},{24,20},{28,24},{5,1},{9,5},{13... | collective-permute-start | bytes 3145736 | tf_op jit(solution)/shard_map/ppermute | solution.py:160
  18.2 1.1 select_reduce_fusion.1
  19.3 0.7 copy.17
  20.0 0.9 select_reduce_fusion.refs_12_.refs_21_
  20.9 0.8 copy.18.refs_11_.refs_20_
  21.7 0.7 fusion.14
  23.8 0.7 select_reduce_fusion.4
  24.8 0.6 slice_convert_fusion.refs_0_
  25.4 0.6 select_convert_fusion.refs_7_.refs_16_
  26.0 17.3 %collective-permute-done.2.refs_4_.refs_13_ = bf16[16,128,256]{2,1,0:T(8,128)(2,1)S(1)} collective-permute-done((bf16[16,128,256]{2,1,0:T(8,128)(2,1)}, bf16[16,128,256]{2,1,0:T(8,128)(2,1)S(1)}, u32[]{:S(2)}, u32[]{:S(2)}) %collective-permute-start.2) | collective-permute-done | bytes 1048608 | tf_op jit(solution)/shard_map/ppermute | solution.py:157
  43.3 1.9 collective-permute-done.3.refs_6_.refs_15_
  45.2 14.4 %sweep.2 = (s16[32,32,256]{2,1,0:T(8,128)(2,1)}, s16[32,32,256]{2,1,0:T(8,128)(2,1)}, s16[32,32,256]{2,1,0:T(8,128)(2,1)}, s16[32,32,256]{2,1,0:T(8,128)(2,1)}, ...) custom-call(s32[64]{0:T(128)} %slice_convert_fusion.refs_0_, ...), custom_call_target="tpu_custom_call" | custom-call | tf_op jit(solution)/shard_map/sweep/pallas_call | solution.py:116
  59.6 1.6 collective-permute-start.4
  61.2 1.5 collective-permute-start.6
  62.7 0.5 collective-permute-start.8
  63.2 1.5 collective-permute-start.5
  64.6 1.5 collective-permute-start.7
  66.2 19.6 %collective-permute-done.5 = f32[32,256]{1,0:T(8,128)S(1)} collective-permute-done((f32[32,256]{1,0:T(8,128)}, f32[32,256]{1,0:T(8,128)S(1)}, u32[]{:S(2)}, u32[]{:S(2)}) %collective-permute-start.5) | collective-permute-done | bytes 32800 | tf_op jit(solution)/shard_map/ppermute | solution.py:163
  85.8 2.4 %collective-permute-start.9 = (f32[32,256]{1,0:T(8,128)}, f32[32,256]{1,0:T(8,128)S(1)}, u32[]{:S(2)}, u32[]{:S(2)}) collective-permute-start(f32[32,256]{1,0:T(8,128)} %get-tuple-element.28), channel_id=1, source_target_pairs={{0,3},{1,2},{2,1},{3,0},{4,7},{5,6},{6,5},{7,4},{8,11},{9,10},{10,... | collective-permute-start | bytes 98312 | tf_op jit(solution)/shard_map/ppermute | solution.py:163
  88.2 6.7 %copy.15 = f32[32,128,256]{2,0,1:T(8,128)} copy(f32[32,128,256]{2,1,0:T(8,128)} %param.5) | data formatting | bytes 8388608 | tf_op args[0]
  95.0 0.8 copy-done.15
  95.8 2.4 %fusion.12 = (bf16[32,32,256]{2,1,0:T(8,128)(2,1)S(1)}, f32[32,32,256]{2,1,0:T(8,128)S(1)}) fusion(f32[32,256]{1,0:T(8,128)S(1)} %collective-permute-done.9, s16[32,32,256]{2,1,0:T(8,128)(2,1)} %copy-done.15, f32[32,256]{1,0:T(8,128)S(1)} %collective-permute-done.7, s16[32,32,256]{2,1,0:T(8,128)(2,1)S(1)} %collective-permute-done.6, ...), kind=kLoop, calls=%fused_computation.58 | loop fusion | flops 3670016 | bytes 4849668 | tf_op jit(solution)/shard_map/convert_element_type | solution.py:210
  98.2 0.6 collective-permute-start.11
  98.8 0.5 collective-permute-start.13
  99.3 2.5 %collective-permute-start.15 = (bf16[32,32,256]{2,1,0:T(8,128)(2,1)S(1)}, bf16[32,32,256]{2,1,0:T(8,128)(2,1)S(1)}, u32[]{:S(2)}, u32[]{:S(2)}) collective-permute-start(bf16[32,32,256]{2,1,0:T(8,128)(2,1)S(1)} %get-tuple-element.43.refs_5_), channel_id=1, source_target_pairs={{0,3},{1,2},{2,1},{3,0},{4,7},{5,6},{6,5},{7,4},{8,11},{9,10},{10,... | collective-permute-start | bytes 1572872 | tf_op jit(solution)/shard_map/ppermute | solution.py:163
  101.7 1.9 collective-permute-start.10
  103.6 3.6 %collective-permute-start.17 = (bf16[32,32,256]{2,1,0:T(8,128)(2,1)S(1)}, bf16[32,32,256]{2,1,0:T(8,128)(2,1)S(1)}, u32[]{:S(2)}, u32[]{:S(2)}) collective-permute-start(bf16[32,32,256]{2,1,0:T(8,128)(2,1)S(1)} %get-tuple-element.43.refs_5_), channel_id=1, source_target_pairs={{4,0},{8,4},{12,8},{16,12},{20,16},{24,20},{28,24},{5,1},{9,5},{13... | collective-permute-start | bytes 1572872 | tf_op jit(solution)/shard_map/ppermute | solution.py:160
  107.3 5.7 %collective-permute-done.11.refs_6_ = bf16[32,32,256]{2,1,0:T(8,128)(2,1)S(1)} collective-permute-done((bf16[32,32,256]{2,1,0:T(8,128)(2,1)S(1)}, bf16[32,32,256]{2,1,0:T(8,128)(2,1)S(1)}, u32[]{:S(2)}, u32[]{:S(2)}) %collective-permute-start.11) | collective-permute-done | bytes 524320 | tf_op jit(solution)/shard_map/ppermute | solution.py:163
  113.0 1.9 collective-permute-start.12
  114.9 9.3 %collective-permute-done.13.refs_7_ = bf16[32,32,256]{2,1,0:T(8,128)(2,1)S(1)} collective-permute-done((bf16[32,32,256]{2,1,0:T(8,128)(2,1)S(1)}, bf16[32,32,256]{2,1,0:T(8,128)(2,1)S(1)}, u32[]{:S(2)}, u32[]{:S(2)}) %collective-permute-start.13) | collective-permute-done | bytes 524320 | tf_op jit(solution)/shard_map/ppermute | solution.py:163
  124.3 1.9 collective-permute-start.18
  126.2 2.4 %collective-permute-start.14 = (bf16[32,32,256]{2,1,0:T(8,128)(2,1)S(1)}, bf16[32,32,256]{2,1,0:T(8,128)(2,1)}, u32[]{:S(2)}, u32[]{:S(2)}) collective-permute-start(bf16[32,32,256]{2,1,0:T(8,128)(2,1)S(1)} %collective-permute-done.13.refs_7_), channel_id=1, source_target_pairs={{0,4},{4,8},{8,12},{12,16},{16,20},{20,24},{24,28},{1,5},{5,9},{9,... | collective-permute-start | bytes 1572872 | tf_op jit(solution)/shard_map/ppermute | solution.py:157
  128.6 3.1 %collective-permute-start.16 = (bf16[32,32,256]{2,1,0:T(8,128)(2,1)S(1)}, bf16[32,32,256]{2,1,0:T(8,128)(2,1)}, u32[]{:S(2)}, u32[]{:S(2)}) collective-permute-start(bf16[32,32,256]{2,1,0:T(8,128)(2,1)S(1)} %collective-permute-done.15.refs_8_), channel_id=1, source_target_pairs={{0,4},{4,8},{8,12},{12,16},{16,20},{20,24},{24,28},{1,5},{5,9},{9,... | collective-permute-start | bytes 1572872 | tf_op jit(solution)/shard_map/ppermute | solution.py:157
  131.8 2.5 %collective-permute-start.19 = (bf16[32,32,256]{2,1,0:T(8,128)(2,1)S(1)}, bf16[32,32,256]{2,1,0:T(8,128)(2,1)}, u32[]{:S(2)}, u32[]{:S(2)}) collective-permute-start(bf16[32,32,256]{2,1,0:T(8,128)(2,1)S(1)} %collective-permute-done.13.refs_7_), channel_id=1, source_target_pairs={{4,0},{8,4},{12,8},{16,12},{20,16},{24,20},{28,24},{5,1},{9,5},{13... | collective-permute-start | bytes 1572872 | tf_op jit(solution)/shard_map/ppermute | solution.py:160
  134.3 0.8 copy-done.13
  135.1 2.9 %collective-permute-start.20 = (bf16[32,32,256]{2,1,0:T(8,128)(2,1)S(1)}, bf16[32,32,256]{2,1,0:T(8,128)(2,1)}, u32[]{:S(2)}, u32[]{:S(2)}) collective-permute-start(bf16[32,32,256]{2,1,0:T(8,128)(2,1)S(1)} %collective-permute-done.15.refs_8_), channel_id=1, source_target_pairs={{4,0},{8,4},{12,8},{16,12},{20,16},{24,20},{28,24},{5,1},{9,5},{13... | collective-permute-start | bytes 1572872 | tf_op jit(solution)/shard_map/ppermute | solution.py:160
  138.0 0.7 copy.19.refs_18_
  138.7 3.7 %collective-permute-done.16.refs_4_ = bf16[32,32,256]{2,1,0:T(8,128)(2,1)} collective-permute-done((bf16[32,32,256]{2,1,0:T(8,128)(2,1)S(1)}, bf16[32,32,256]{2,1,0:T(8,128)(2,1)}, u32[]{:S(2)}, u32[]{:S(2)}) %collective-permute-start.16) | collective-permute-done | bytes 524320 | tf_op jit(solution)/shard_map/ppermute | solution.py:157
  142.4 4.1 %collective-permute-done.20.refs_12_ = bf16[32,32,256]{2,1,0:T(8,128)(2,1)} collective-permute-done((bf16[32,32,256]{2,1,0:T(8,128)(2,1)S(1)}, bf16[32,32,256]{2,1,0:T(8,128)(2,1)}, u32[]{:S(2)}, u32[]{:S(2)}) %collective-permute-start.20) | collective-permute-done | bytes 524320 | tf_op jit(solution)/shard_map/ppermute | solution.py:160
  146.5 14.2 %sweep.3 = (s16[32,32,256]{2,1,0:T(8,128)(2,1)}, s16[32,32,256]{2,1,0:T(8,128)(2,1)}, s16[32,32,256]{2,1,0:T(8,128)(2,1)}, s16[32,32,256]{2,1,0:T(8,128)(2,1)}, ...) custom-call(s32[64]{0:T(128)} %slice_convert_fusion.refs_0_, ...), custom_call_target="tpu_custom_call" | custom-call | tf_op jit(solution)/shard_map/sweep/pallas_call | solution.py:116
  160.7 1.5 collective-permute-start.21
  162.2 2.1 collective-permute-start.25
  164.3 1.4 collective-permute-start.22
  165.7 21.1 %collective-permute-done.22 = f32[32,256]{1,0:T(8,128)S(1)} collective-permute-done((f32[32,256]{1,0:T(8,128)}, f32[32,256]{1,0:T(8,128)S(1)}, u32[]{:S(2)}, u32[]{:S(2)}) %collective-permute-start.22) | collective-permute-done | bytes 32800 | tf_op jit(solution)/shard_map/ppermute | solution.py:163
  187.2 1.3 collective-permute-done.24
  188.5 3.5 %collective-permute-done.26 = f32[32,256]{1,0:T(8,128)S(1)} collective-permute-done((f32[32,256]{1,0:T(8,128)}, f32[32,256]{1,0:T(8,128)S(1)}, u32[]{:S(2)}, u32[]{:S(2)}) %collective-permute-start.26) | collective-permute-done | bytes 32800 | tf_op jit(solution)/shard_map/ppermute | solution.py:163
  192.0 2.1 abs_reduce_fusion
  194.5 1.6 collective-permute-start.27
  196.0 2.0 collective-permute-start.29
  198.0 0.9 collective-permute-start.32
  198.9 0.6 collective-permute-start.28
  199.5 0.5 broadcast_in_dim.103
  200.0 0.7 copy_dynamic-update-slice_fusion.3
  200.7 20.5 %collective-permute-done.28 = f32[1,32,256]{2,1,0:T(8,128)S(1)} collective-permute-done((f32[1,32,256]{2,1,0:T(8,128)S(1)}, f32[1,32,256]{2,1,0:T(8,128)S(1)}, u32[]{:S(2)}, u32[]{:S(2)}) %collective-permute-start.28) | collective-permute-done | bytes 32800 | tf_op jit(solution)/shard_map/ppermute | solution.py:163
  221.3 0.7 copy_dynamic-update-slice_fusion.2
  222.1 3.0 %collective-permute-done.30 = f32[1,32,256]{2,1,0:T(8,128)S(1)} collective-permute-done((f32[1,32,256]{2,1,0:T(8,128)S(1)}, f32[1,32,256]{2,1,0:T(8,128)S(1)}, u32[]{:S(2)}, u32[]{:S(2)}) %collective-permute-start.30) | collective-permute-done | bytes 32800 | tf_op jit(solution)/shard_map/ppermute | solution.py:163
  225.2 0.7 copy_dynamic-update-slice_fusion.1
  226.2 1.8 copy-done.4
  228.0 1.6 copy_dynamic-update-slice_fusion
  (76 shorter events, 1.9 us)
Async XLA Ops:
  0.0 18.0 %copy-start = (bf16[8,3,33]{2,0,1:T(8,128)(2,1)S(1)}, bf16[8,3,33]{2,0,1:T(8,128)(2,1)}, u32[]{:S(2)}) copy-start(bf16[8,3,33]{2,0,1:T(8,128)(2,1)} %param.7) | copy-start | bytes 4756
  0.0 10.3 %copy-start.1 = (bf16[1,32,128,256]{3,2,1,0:T(8,128)(2,1)S(1)}, bf16[1,32,128,256]{3,2,1,0:T(8,128)(2,1)}, u32[]{:S(2)}) copy-start(bf16[1,32,128,256]{3,2,1,0:T(8,128)(2,1)} %param.6) | copy-start | bytes 6291460
  4.6 40.6 %copy-start.2 = (bf16[32,128,256]{2,0,1:T(8,128)(2,1)}, bf16[32,128,256]{2,0,1:T(8,128)(2,1)S(1)}, u32[]{:S(2)}) copy-start(bf16[32,128,256]{2,0,1:T(8,128)(2,1)S(1)} %copy.32) | copy-start | bytes 6291460
  4.6 17.1 %copy-start.17 = (s32[1,2]{1,0:T(1,128)S(1)}, s32[1,2]{1,0:T(1,128)}, u32[]{:S(2)}) copy-start(s32[1,2]{1,0:T(1,128)} %param.9) | copy-start | bytes 28
  4.6 40.6 %collective-permute-start = (bf16[128,32,256]{2,1,0:T(8,128)(2,1)S(1)}, bf16[128,32,256]{2,1,0:T(8,128)(2,1)}, u32[]{:S(2)}, u32[]{:S(2)}) collective-permute-start(bf16[128,32,256]{2,1,0:T(8,128)(2,1)S(1)} %bitcast.45), channel_id=1, source_target_pairs={{0,4},{4,8},{8,12},{12,16},{16,20},{20,24},{24,28},{1,5},{5,9},{9,... | collective-permute-start | bytes 6291464 | tf_op jit(solution)/shard_map/ppermute | solution.py:157
  6.7 38.5 %collective-permute-start.1 = (bf16[128,32,256]{2,1,0:T(8,128)(2,1)S(1)}, bf16[128,32,256]{2,1,0:T(8,128)(2,1)}, u32[]{:S(2)}, u32[]{:S(2)}) collective-permute-start(bf16[128,32,256]{2,1,0:T(8,128)(2,1)S(1)} %bitcast.46), channel_id=1, source_target_pairs={{4,0},{8,4},{12,8},{16,12},{20,16},{24,20},{28,24},{5,1},{9,5},{13... | collective-permute-start | bytes 6291464 | tf_op jit(solution)/shard_map/ppermute | solution.py:160
  11.8 31.6 %collective-permute-start.2 = (bf16[16,128,256]{2,1,0:T(8,128)(2,1)}, bf16[16,128,256]{2,1,0:T(8,128)(2,1)S(1)}, u32[]{:S(2)}, u32[]{:S(2)}) collective-permute-start(bf16[16,128,256]{2,1,0:T(8,128)(2,1)} %get-tuple-element.46), channel_id=1, source_target_pairs={{0,4},{4,8},{8,12},{12,16},{16,20},{20,24},{24,28},{1,5},{5,9},{9,... | collective-permute-start | bytes 3145736 | tf_op jit(solution)/shard_map/ppermute | solution.py:157
  13.7 31.5 %collective-permute-start.3 = (bf16[16,128,256]{2,1,0:T(8,128)(2,1)}, bf16[16,128,256]{2,1,0:T(8,128)(2,1)}, u32[]{:S(2)}, u32[]{:S(2)}) collective-permute-start(bf16[16,128,256]{2,1,0:T(8,128)(2,1)} %get-tuple-element.45), channel_id=1, source_target_pairs={{4,0},{8,4},{12,8},{16,12},{20,16},{24,20},{28,24},{5,1},{9,5},{13... | collective-permute-start | bytes 3145736 | tf_op jit(solution)/shard_map/ppermute | solution.py:160
  20.9 24.3 %copy-start.5 = (bf16[256,256]{1,0:T(8,128)(2,1)}, bf16[256,256]{1,0:T(8,128)(2,1)S(1)}, u32[]{:S(2)}) copy-start(bf16[256,256]{1,0:T(8,128)(2,1)S(1)} %select_reduce_fusion.refs_12_.refs_21_) | copy-start | bytes 393220
  43.3 1.9 copy-start.3
  59.6 35.3 %collective-permute-start.4 = (s16[32,32,256]{2,1,0:T(8,128)(2,1)}, s16[32,32,256]{2,1,0:T(8,128)(2,1)S(1)}, u32[]{:S(2)}, u32[]{:S(2)}) collective-permute-start(s16[32,32,256]{2,1,0:T(8,128)(2,1)} %get-tuple-element.23), channel_id=1, source_target_pairs={{0,1},{1,0},{2,3},{3,2},{4,5},{5,4},{6,7},{7,6},{8,9},{9,8},{10,11... | collective-permute-start | bytes 1572872 | tf_op jit(solution)/shard_map/ppermute | solution.py:163
  61.2 33.8 %collective-permute-start.6 = (s16[32,32,256]{2,1,0:T(8,128)(2,1)}, s16[32,32,256]{2,1,0:T(8,128)(2,1)S(1)}, u32[]{:S(2)}, u32[]{:S(2)}) collective-permute-start(s16[32,32,256]{2,1,0:T(8,128)(2,1)} %get-tuple-element.25), channel_id=1, source_target_pairs={{0,2},{1,3},{2,0},{3,1},{4,6},{5,7},{6,4},{7,5},{8,10},{9,11},{10,... | collective-permute-start | bytes 1572872 | tf_op jit(solution)/shard_map/ppermute | solution.py:163
  62.7 32.3 %collective-permute-start.8 = (s16[32,32,256]{2,1,0:T(8,128)(2,1)}, s16[32,32,256]{2,1,0:T(8,128)(2,1)S(1)}, u32[]{:S(2)}, u32[]{:S(2)}) collective-permute-start(s16[32,32,256]{2,1,0:T(8,128)(2,1)} %get-tuple-element.27), channel_id=1, source_target_pairs={{0,3},{1,2},{2,1},{3,0},{4,7},{5,6},{6,5},{7,4},{8,11},{9,10},{10,... | collective-permute-start | bytes 1572872 | tf_op jit(solution)/shard_map/ppermute | solution.py:163
  63.2 22.6 %collective-permute-start.5 = (f32[32,256]{1,0:T(8,128)}, f32[32,256]{1,0:T(8,128)S(1)}, u32[]{:S(2)}, u32[]{:S(2)}) collective-permute-start(f32[32,256]{1,0:T(8,128)} %get-tuple-element.24), channel_id=1, source_target_pairs={{0,1},{1,0},{2,3},{3,2},{4,5},{5,4},{6,7},{7,6},{8,9},{9,8},{10,11... | collective-permute-start | bytes 98312 | tf_op jit(solution)/shard_map/ppermute | solution.py:163
  64.6 30.3 %collective-permute-start.7 = (f32[32,256]{1,0:T(8,128)}, f32[32,256]{1,0:T(8,128)S(1)}, u32[]{:S(2)}, u32[]{:S(2)}) collective-permute-start(f32[32,256]{1,0:T(8,128)} %get-tuple-element.26), channel_id=1, source_target_pairs={{0,2},{1,3},{2,0},{3,1},{4,6},{5,7},{6,4},{7,5},{8,10},{9,11},{10,... | collective-permute-start | bytes 98312 | tf_op jit(solution)/shard_map/ppermute | solution.py:163
  85.8 9.1 %collective-permute-start.9 = (f32[32,256]{1,0:T(8,128)}, f32[32,256]{1,0:T(8,128)S(1)}, u32[]{:S(2)}, u32[]{:S(2)}) collective-permute-start(f32[32,256]{1,0:T(8,128)} %get-tuple-element.28), channel_id=1, source_target_pairs={{0,3},{1,2},{2,1},{3,0},{4,7},{5,6},{6,5},{7,4},{8,11},{9,10},{10,... | collective-permute-start | bytes 98312 | tf_op jit(solution)/shard_map/ppermute | solution.py:163
  88.2 7.5 %copy-start.14 = (s16[32,32,256]{2,1,0:T(8,128)(2,1)S(1)}, s16[32,32,256]{2,1,0:T(8,128)(2,1)}, u32[]{:S(2)}) copy-start(s16[32,32,256]{2,1,0:T(8,128)(2,1)} %get-tuple-element.21) | copy-start | bytes 1572868
  88.2 7.5 %copy-start.16 = (f32[32,256]{1,0:T(8,128)S(1)}, f32[32,256]{1,0:T(8,128)}, u32[]{:S(2)}) copy-start(f32[32,256]{1,0:T(8,128)} %get-tuple-element.22) | copy-start | bytes 98308
  94.9 43.0 %copy-start.7 = (bf16[128,128]{0,1:T(8,128)(2,1)S(1)}, bf16[128,128]{0,1:T(8,128)(2,1)}, u32[]{:S(2)}) copy-start(bf16[128,128]{0,1:T(8,128)(2,1)} %copy.17) | copy-start | bytes 98308
  95.0 0.8 copy-start.15
  98.1 48.4 %copy-start.6 = (bf16[32,32,256]{2,1,0:T(8,128)(2,1)}, bf16[32,32,256]{2,1,0:T(8,128)(2,1)S(1)}, u32[]{:S(2)}) copy-start(bf16[32,32,256]{2,1,0:T(8,128)(2,1)S(1)} %get-tuple-element.43.refs_5_) | copy-start | bytes 1572868
  98.2 14.9 %collective-permute-start.11 = (bf16[32,32,256]{2,1,0:T(8,128)(2,1)S(1)}, bf16[32,32,256]{2,1,0:T(8,128)(2,1)S(1)}, u32[]{:S(2)}, u32[]{:S(2)}) collective-permute-start(bf16[32,32,256]{2,1,0:T(8,128)(2,1)S(1)} %get-tuple-element.43.refs_5_), channel_id=1, source_target_pairs={{0,1},{1,0},{2,3},{3,2},{4,5},{5,4},{6,7},{7,6},{8,9},{9,8},{10,11... | collective-permute-start | bytes 1572872 | tf_op jit(solution)/shard_map/ppermute | solution.py:163
  98.8 25.5 %collective-permute-start.13 = (bf16[32,32,256]{2,1,0:T(8,128)(2,1)S(1)}, bf16[32,32,256]{2,1,0:T(8,128)(2,1)S(1)}, u32[]{:S(2)}, u32[]{:S(2)}) collective-permute-start(bf16[32,32,256]{2,1,0:T(8,128)(2,1)S(1)} %get-tuple-element.43.refs_5_), channel_id=1, source_target_pairs={{0,2},{1,3},{2,0},{3,1},{4,6},{5,7},{6,4},{7,5},{8,10},{9,11},{10,... | collective-permute-start | bytes 1572872 | tf_op jit(solution)/shard_map/ppermute | solution.py:163
  99.3 26.9 %collective-permute-start.15 = (bf16[32,32,256]{2,1,0:T(8,128)(2,1)S(1)}, bf16[32,32,256]{2,1,0:T(8,128)(2,1)S(1)}, u32[]{:S(2)}, u32[]{:S(2)}) collective-permute-start(bf16[32,32,256]{2,1,0:T(8,128)(2,1)S(1)} %get-tuple-element.43.refs_5_), channel_id=1, source_target_pairs={{0,3},{1,2},{2,1},{3,0},{4,7},{5,6},{6,5},{7,4},{8,11},{9,10},{10,... | collective-permute-start | bytes 1572872 | tf_op jit(solution)/shard_map/ppermute | solution.py:163
  101.7 26.9 %collective-permute-start.10 = (bf16[32,32,256]{2,1,0:T(8,128)(2,1)S(1)}, bf16[32,32,256]{2,1,0:T(8,128)(2,1)S(1)}, u32[]{:S(2)}, u32[]{:S(2)}) collective-permute-start(bf16[32,32,256]{2,1,0:T(8,128)(2,1)S(1)} %get-tuple-element.43.refs_5_), channel_id=1, source_target_pairs={{0,4},{4,8},{8,12},{12,16},{16,20},{20,24},{24,28},{1,5},{5,9},{9,... | collective-permute-start | bytes 1572872 | tf_op jit(solution)/shard_map/ppermute | solution.py:157
  103.6 28.1 %collective-permute-start.17 = (bf16[32,32,256]{2,1,0:T(8,128)(2,1)S(1)}, bf16[32,32,256]{2,1,0:T(8,128)(2,1)S(1)}, u32[]{:S(2)}, u32[]{:S(2)}) collective-permute-start(bf16[32,32,256]{2,1,0:T(8,128)(2,1)S(1)} %get-tuple-element.43.refs_5_), channel_id=1, source_target_pairs={{4,0},{8,4},{12,8},{16,12},{20,16},{24,20},{28,24},{5,1},{9,5},{13... | collective-permute-start | bytes 1572872 | tf_op jit(solution)/shard_map/ppermute | solution.py:160
  113.0 33.5 %copy-start.8 = (bf16[32,32,256]{2,1,0:T(8,128)(2,1)}, bf16[32,32,256]{2,1,0:T(8,128)(2,1)S(1)}, u32[]{:S(2)}) copy-start(bf16[32,32,256]{2,1,0:T(8,128)(2,1)S(1)} %collective-permute-done.11.refs_6_) | copy-start | bytes 1572868
  113.0 21.2 %collective-permute-start.12 = (bf16[32,32,256]{2,1,0:T(8,128)(2,1)S(1)}, bf16[32,32,256]{2,1,0:T(8,128)(2,1)S(1)}, u32[]{:S(2)}, u32[]{:S(2)}) collective-permute-start(bf16[32,32,256]{2,1,0:T(8,128)(2,1)S(1)} %collective-permute-done.11.refs_6_), channel_id=1, source_target_pairs={{0,4},{4,8},{8,12},{12,16},{16,20},{20,24},{24,28},{1,5},{5,9},{9,... | collective-permute-start | bytes 1572872 | tf_op jit(solution)/shard_map/ppermute | solution.py:157
  124.2 22.3 %copy-start.9 = (bf16[32,32,256]{2,1,0:T(8,128)(2,1)}, bf16[32,32,256]{2,1,0:T(8,128)(2,1)S(1)}, u32[]{:S(2)}) copy-start(bf16[32,32,256]{2,1,0:T(8,128)(2,1)S(1)} %collective-permute-done.13.refs_7_) | copy-start | bytes 1572868
  124.3 18.2 %collective-permute-start.18 = (bf16[32,32,256]{2,1,0:T(8,128)(2,1)S(1)}, bf16[32,32,256]{2,1,0:T(8,128)(2,1)}, u32[]{:S(2)}, u32[]{:S(2)}) collective-permute-start(bf16[32,32,256]{2,1,0:T(8,128)(2,1)S(1)} %collective-permute-done.11.refs_6_), channel_id=1, source_target_pairs={{4,0},{8,4},{12,8},{16,12},{20,16},{24,20},{28,24},{5,1},{9,5},{13... | collective-permute-start | bytes 1572872 | tf_op jit(solution)/shard_map/ppermute | solution.py:160
  126.2 20.4 %copy-start.10 = (bf16[32,32,256]{2,1,0:T(8,128)(2,1)}, bf16[32,32,256]{2,1,0:T(8,128)(2,1)S(1)}, u32[]{:S(2)}) copy-start(bf16[32,32,256]{2,1,0:T(8,128)(2,1)S(1)} %collective-permute-done.15.refs_8_) | copy-start | bytes 1572868
  126.2 12.5 %collective-permute-start.14 = (bf16[32,32,256]{2,1,0:T(8,128)(2,1)S(1)}, bf16[32,32,256]{2,1,0:T(8,128)(2,1)}, u32[]{:S(2)}, u32[]{:S(2)}) collective-permute-start(bf16[32,32,256]{2,1,0:T(8,128)(2,1)S(1)} %collective-permute-done.13.refs_7_), channel_id=1, source_target_pairs={{0,4},{4,8},{8,12},{12,16},{16,20},{20,24},{24,28},{1,5},{5,9},{9,... | collective-permute-start | bytes 1572872 | tf_op jit(solution)/shard_map/ppermute | solution.py:157
  128.6 5.6 %copy-start.11 = (bf16[32,32,256]{2,1,0:T(8,128)(2,1)}, bf16[32,32,256]{2,1,0:T(8,128)(2,1)S(1)}, u32[]{:S(2)}) copy-start(bf16[32,32,256]{2,1,0:T(8,128)(2,1)S(1)} %collective-permute-done.10.refs_1_) | copy-start | bytes 1572868
  128.6 13.8 %collective-permute-start.16 = (bf16[32,32,256]{2,1,0:T(8,128)(2,1)S(1)}, bf16[32,32,256]{2,1,0:T(8,128)(2,1)}, u32[]{:S(2)}, u32[]{:S(2)}) collective-permute-start(bf16[32,32,256]{2,1,0:T(8,128)(2,1)S(1)} %collective-permute-done.15.refs_8_), channel_id=1, source_target_pairs={{0,4},{4,8},{8,12},{12,16},{16,20},{20,24},{24,28},{1,5},{5,9},{9,... | collective-permute-start | bytes 1572872 | tf_op jit(solution)/shard_map/ppermute | solution.py:157
  131.8 2.5 %copy-start.12 = (bf16[32,32,256]{2,1,0:T(8,128)(2,1)}, bf16[32,32,256]{2,1,0:T(8,128)(2,1)S(1)}, u32[]{:S(2)}) copy-start(bf16[32,32,256]{2,1,0:T(8,128)(2,1)S(1)} %collective-permute-done.17.refs_9_) | copy-start | bytes 1572868
  131.8 10.7 %collective-permute-start.19 = (bf16[32,32,256]{2,1,0:T(8,128)(2,1)S(1)}, bf16[32,32,256]{2,1,0:T(8,128)(2,1)}, u32[]{:S(2)}, u32[]{:S(2)}) collective-permute-start(bf16[32,32,256]{2,1,0:T(8,128)(2,1)S(1)} %collective-permute-done.13.refs_7_), channel_id=1, source_target_pairs={{4,0},{8,4},{12,8},{16,12},{20,16},{24,20},{28,24},{5,1},{9,5},{13... | collective-permute-start | bytes 1572872 | tf_op jit(solution)/shard_map/ppermute | solution.py:160
  134.3 0.8 copy-start.13
  135.1 11.5 %collective-permute-start.20 = (bf16[32,32,256]{2,1,0:T(8,128)(2,1)S(1)}, bf16[32,32,256]{2,1,0:T(8,128)(2,1)}, u32[]{:S(2)}, u32[]{:S(2)}) collective-permute-start(bf16[32,32,256]{2,1,0:T(8,128)(2,1)S(1)} %collective-permute-done.15.refs_8_), channel_id=1, source_target_pairs={{4,0},{8,4},{12,8},{16,12},{20,16},{24,20},{28,24},{5,1},{9,5},{13... | collective-permute-start | bytes 1572872 | tf_op jit(solution)/shard_map/ppermute | solution.py:160
  160.7 31.3 %collective-permute-start.21 = (s16[32,32,256]{2,1,0:T(8,128)(2,1)}, s16[32,32,256]{2,1,0:T(8,128)(2,1)S(1)}, u32[]{:S(2)}, u32[]{:S(2)}) collective-permute-start(s16[32,32,256]{2,1,0:T(8,128)(2,1)} %get-tuple-element.31), channel_id=1, source_target_pairs={{0,1},{1,0},{2,3},{3,2},{4,5},{5,4},{6,7},{7,6},{8,9},{9,8},{10,11... | collective-permute-start | bytes 1572872 | tf_op jit(solution)/shard_map/ppermute | solution.py:163
  162.2 29.8 %collective-permute-start.23 = (s16[32,32,256]{2,1,0:T(8,128)(2,1)}, s16[32,32,256]{2,1,0:T(8,128)(2,1)S(1)}, u32[]{:S(2)}, u32[]{:S(2)}) collective-permute-start(s16[32,32,256]{2,1,0:T(8,128)(2,1)} %get-tuple-element.33), channel_id=1, source_target_pairs={{0,2},{1,3},{2,0},{3,1},{4,6},{5,7},{6,4},{7,5},{8,10},{9,11},{10,... | collective-permute-start | bytes 1572872 | tf_op jit(solution)/shard_map/ppermute | solution.py:163
  162.2 29.8 %collective-permute-start.25 = (s16[32,32,256]{2,1,0:T(8,128)(2,1)}, s16[32,32,256]{2,1,0:T(8,128)(2,1)S(1)}, u32[]{:S(2)}, u32[]{:S(2)}) collective-permute-start(s16[32,32,256]{2,1,0:T(8,128)(2,1)} %get-tuple-element.35), channel_id=1, source_target_pairs={{0,3},{1,2},{2,1},{3,0},{4,7},{5,6},{6,5},{7,4},{8,11},{9,10},{10,... | collective-permute-start | bytes 1572872 | tf_op jit(solution)/shard_map/ppermute | solution.py:163
  164.3 22.5 %collective-permute-start.22 = (f32[32,256]{1,0:T(8,128)}, f32[32,256]{1,0:T(8,128)S(1)}, u32[]{:S(2)}, u32[]{:S(2)}) collective-permute-start(f32[32,256]{1,0:T(8,128)} %get-tuple-element.32), channel_id=1, source_target_pairs={{0,1},{1,0},{2,3},{3,2},{4,5},{5,4},{6,7},{7,6},{8,9},{9,8},{10,11... | collective-permute-start | bytes 98312 | tf_op jit(solution)/shard_map/ppermute | solution.py:163
  165.7 22.8 %collective-permute-start.24 = (f32[32,256]{1,0:T(8,128)}, f32[32,256]{1,0:T(8,128)S(1)}, u32[]{:S(2)}, u32[]{:S(2)}) collective-permute-start(f32[32,256]{1,0:T(8,128)} %get-tuple-element.34), channel_id=1, source_target_pairs={{0,2},{1,3},{2,0},{3,1},{4,6},{5,7},{6,4},{7,5},{8,10},{9,11},{10,... | collective-permute-start | bytes 98312 | tf_op jit(solution)/shard_map/ppermute | solution.py:163
  186.8 5.2 %collective-permute-start.26 = (f32[32,256]{1,0:T(8,128)}, f32[32,256]{1,0:T(8,128)S(1)}, u32[]{:S(2)}, u32[]{:S(2)}) collective-permute-start(f32[32,256]{1,0:T(8,128)} %get-tuple-element.36), channel_id=1, source_target_pairs={{0,3},{1,2},{2,1},{3,0},{4,7},{5,6},{6,5},{7,4},{8,11},{9,10},{10,... | collective-permute-start | bytes 98312 | tf_op jit(solution)/shard_map/ppermute | solution.py:163
  194.5 26.7 %collective-permute-start.27 = (s16[32,32,256]{2,0,1:T(8,128)(2,1)S(1)}, s16[32,32,256]{2,0,1:T(8,128)(2,1)S(1)}, u32[]{:S(2)}, u32[]{:S(2)}) collective-permute-start(s16[32,32,256]{2,0,1:T(8,128)(2,1)S(1)} %get-tuple-element.40), channel_id=1, source_target_pairs={{0,1},{1,0},{2,3},{3,2},{4,5},{5,4},{6,7},{7,6},{8,9},{9,8},{10,11... | collective-permute-start | bytes 1572872 | tf_op jit(solution)/shard_map/ppermute | solution.py:163
  196.0 30.0 %collective-permute-start.31 = (s16[32,32,256]{2,0,1:T(8,128)(2,1)S(1)}, s16[32,32,256]{2,0,1:T(8,128)(2,1)S(1)}, u32[]{:S(2)}, u32[]{:S(2)}) collective-permute-start(s16[32,32,256]{2,0,1:T(8,128)(2,1)S(1)} %get-tuple-element.40), channel_id=1, source_target_pairs={{0,3},{1,2},{2,1},{3,0},{4,7},{5,6},{6,5},{7,4},{8,11},{9,10},{10,... | collective-permute-start | bytes 1572872 | tf_op jit(solution)/shard_map/ppermute | solution.py:163
  196.0 29.1 %collective-permute-start.29 = (s16[32,32,256]{2,0,1:T(8,128)(2,1)S(1)}, s16[32,32,256]{2,0,1:T(8,128)(2,1)S(1)}, u32[]{:S(2)}, u32[]{:S(2)}) collective-permute-start(s16[32,32,256]{2,0,1:T(8,128)(2,1)S(1)} %get-tuple-element.40), channel_id=1, source_target_pairs={{0,2},{1,3},{2,0},{3,1},{4,6},{5,7},{6,4},{7,5},{8,10},{9,11},{10,... | collective-permute-start | bytes 1572872 | tf_op jit(solution)/shard_map/ppermute | solution.py:163
  198.0 28.0 %collective-permute-start.32 = (f32[1,32,256]{2,1,0:T(8,128)S(1)}, f32[1,32,256]{2,1,0:T(8,128)S(1)}, u32[]{:S(2)}, u32[]{:S(2)}) collective-permute-start(f32[1,32,256]{2,1,0:T(8,128)S(1)} %get-tuple-element.47), channel_id=1, source_target_pairs={{0,3},{1,2},{2,1},{3,0},{4,7},{5,6},{6,5},{7,4},{8,11},{9,10},{10,... | collective-permute-start | bytes 98312 | tf_op jit(solution)/shard_map/ppermute | solution.py:163
  198.9 22.2 %collective-permute-start.28 = (f32[1,32,256]{2,1,0:T(8,128)S(1)}, f32[1,32,256]{2,1,0:T(8,128)S(1)}, u32[]{:S(2)}, u32[]{:S(2)}) collective-permute-start(f32[1,32,256]{2,1,0:T(8,128)S(1)} %get-tuple-element.47), channel_id=1, source_target_pairs={{0,1},{1,0},{2,3},{3,2},{4,5},{5,4},{6,7},{7,6},{8,9},{9,8},{10,11... | collective-permute-start | bytes 98312 | tf_op jit(solution)/shard_map/ppermute | solution.py:163
  221.1 3.9 %collective-permute-start.30 = (f32[1,32,256]{2,1,0:T(8,128)S(1)}, f32[1,32,256]{2,1,0:T(8,128)S(1)}, u32[]{:S(2)}, u32[]{:S(2)}) collective-permute-start(f32[1,32,256]{2,1,0:T(8,128)S(1)} %get-tuple-element.47), channel_id=1, source_target_pairs={{0,2},{1,3},{2,0},{3,1},{4,6},{5,7},{6,4},{7,5},{8,10},{9,11},{10,... | collective-permute-start | bytes 98312 | tf_op jit(solution)/shard_map/ppermute | solution.py:163
  226.0 2.0 copy-start.4

commit v2 on v1

v2 whole, which is shorter than its diff:
```python
import functools

import jax
import jax.numpy as jnp
from jax import lax
from jax.experimental import pallas as pl
from jax.experimental.pallas import tpu as pltpu
from jax.sharding import PartitionSpec as P

MARGIN = 32
ITERS = 2
REACH = 16
LANES = 128
GROUP = 16
UNROLL = 32
PAD = 8
STEPS = 8.0
ROOM = 32768.0 / 32000.0
SMALL = 1e-30
VMEM_LIMIT = 56 * 1024 * 1024
ANY = pl.BlockSpec(memory_space=pl.ANY)
VMEM = pl.BlockSpec(memory_space=pltpu.VMEM)
SMEM = pl.BlockSpec(memory_space=pltpu.SMEM)


def dot32(a, b):
    return jnp.dot(a, b, preferred_element_type=jnp.float32)


def halves(value):
    return [value[:, h * LANES : (h + 1) * LANES] for h in range(value.shape[1] // LANES)]


def encode(values):
    top = jnp.maximum(jnp.max(jnp.abs(values), axis=0, keepdims=True), jnp.float32(SMALL))
    power = jnp.ceil(jnp.log2(top * jnp.float32(ROOM)) * jnp.float32(STEPS))
    code = jnp.round(values * jnp.exp2(15.0 - power * jnp.float32(1.0 / STEPS)))
    return code.astype(jnp.int32).astype(jnp.int16), power


def scale_of(powers):
    return jnp.exp2(powers.astype(jnp.float32) * jnp.float32(1.0 / STEPS) - 15.0)


def put_powers(slab_ref, powers):
    depth, count = slab_ref.shape[0], powers.shape[0]
    slab_ref[0:count, :] = powers.astype(jnp.int32).astype(jnp.int16)
    if count < depth:
        slab_ref[count:depth, :] = jnp.zeros((depth - count, powers.shape[1]), jnp.int16)


def sweep_kernel(plan, *refs):
    pieces, shares, pieces_out, core, rows, cols = plan
    refs = list(refs)
    take = lambda n: [refs.pop(0) for _ in range(n)]
    view_ref, mask_ref = take(2)
    sources = [take(n) for n in shares]
    data_sources = take(3)
    z_band, z_back, y_band, y_back, x_band, x_back = take(6)
    outs = take(pieces_out)
    block, measured, by_plane, by_row, codes, powers, in_sem, data_sem, out_sem = refs
    depths = core + 2 * REACH
    lane_parts = cols // LANES
    plane_rows, row_depths = rows + PAD, depths + PAD
    rows_out = rows // pieces_out
    unroll_out = min(UNROLL, rows_out)

    def block_copies(index):
        bits, offset, count = pieces[index]
        copies = []
        for part, given in enumerate(sources):
            if len(given) == 1:
                first = (view_ref[0] ^ bits) * rows_out + offset
                source = given[0].at[pl.ds(first, count)]
            else:
                source = given[index]
            target = block.at[pl.ds(bits * rows_out + offset, count), pl.ds(part * core, core)]
            copies.append(pltpu.make_async_copy(source, target, in_sem.at[part, index]))
        return copies

    starts = (0, REACH, REACH + core)
    counts = (REACH, core, REACH)
    data_copies = [
        pltpu.make_async_copy(
            data_sources[i], measured.at[pl.ds(starts[i], counts[i])], data_sem.at[i]
        )
        for i in range(3)
    ]
    for index in range(len(pieces)):
        for copy in block_copies(index):
            copy.start()
    for copy in data_copies:
        copy.start()

    for index, (bits, offset, count) in enumerate(pieces):
        for copy in block_copies(index):
            copy.wait()
        for y in range(bits * rows_out + offset, bits * rows_out + offset + count):
            for h, part in enumerate(halves(dot32(z_band[...], block[y]))):
                by_plane[h, pl.ds(y, depths, stride=plane_rows), :] = part
    for copy in data_copies:
        copy.wait()

    def planes(step, carry):
        passed = []
        for g in range(GROUP):
            start = pl.multiple_of((step * GROUP + g) * plane_rows, PAD)
            plane = jnp.concatenate(
                [by_plane[h, pl.ds(start, rows), :].astype(jnp.bfloat16) for h in range(lane_parts)],
                axis=1,
            )
            passed.append(dot32(y_band[...], plane).astype(jnp.bfloat16))
        blurred = dot32(jnp.concatenate(passed, axis=0), x_band[...])
        ratios = []
        for g in range(GROUP):
            k = step * GROUP + g
            inside = mask_ref[k] > 0
            data = measured[k].astype(jnp.float32)
            under = jnp.where(inside, blurred[g * rows : (g + 1) * rows], jnp.float32(1.0))
            ratios.append(jnp.where(inside, data / under, jnp.float32(0.0)).astype(jnp.bfloat16))
        back = dot32(jnp.concatenate(ratios, axis=0), x_back[...]).astype(jnp.bfloat16)
        for g in range(GROUP):
            out = dot32(y_back[...], back[g * rows : (g + 1) * rows])
            for h, part in enumerate(halves(out)):
                by_row[h, pl.ds(step * GROUP + g, rows, stride=row_depths), :] = part
        return carry

    lax.fori_loop(0, depths // GROUP, planes, 0)

    out_copies = []
    for p in range(pieces_out):

        def z_return(step, carry, p=p):
            for u in range(unroll_out):
                y = step * unroll_out + u
                start = pl.multiple_of((p * rows_out + y) * row_depths, PAD)
                column = jnp.concatenate(
                    [by_row[h, pl.ds(start, depths), :].astype(jnp.bfloat16) for h in range(lane_parts)],
                    axis=1,
                )
                code, power = encode(dot32(z_back[...], column))
                codes[p, y] = code
                powers[pl.ds(y, 1), :] = power
            return carry

        lax.fori_loop(0, rows_out // unroll_out, z_return, 0)
        put_powers(codes.at[p, rows_out], powers[...])
        copy = pltpu.make_async_copy(codes.at[p], outs[p], out_sem.at[p])
        copy.start()
        out_copies.append(copy)
    for copy in out_copies:
        copy.wait()


def sweep(view_id, mask, pieces, blocks, measured, bands, pieces_out):
    core, (rows, cols) = measured[1].shape[0], measured[1].shape[1:]
    depths = core + 2 * REACH
    rows_out = rows // pieces_out
    shares = tuple(len(part) for part in blocks)
    flat = [piece for part in blocks for piece in part]
    return pl.pallas_call(
        functools.partial(sweep_kernel, (pieces, shares, pieces_out, core, rows, cols)),
        out_shape=[jax.ShapeDtypeStruct((rows_out + 1, core, cols), jnp.int16)] * pieces_out,
        in_specs=[SMEM] * 2 + [ANY] * (len(flat) + 3) + [VMEM] * 6,
        out_specs=[ANY] * pieces_out,
        scratch_shapes=[
            pltpu.VMEM((rows, 3 * core, cols), jnp.bfloat16),
            pltpu.VMEM((depths, rows, cols), jnp.bfloat16),
            pltpu.VMEM((cols // LANES, depths * (rows + PAD), LANES), jnp.float32),
            pltpu.VMEM((cols // LANES, rows * (depths + PAD), LANES), jnp.float32),
            pltpu.VMEM((pieces_out, rows_out + 1, core, cols), jnp.int16),
            pltpu.VMEM((rows_out, cols), jnp.float32),
            pltpu.SemaphoreType.DMA((3, len(pieces))),
            pltpu.SemaphoreType.DMA((3,)),
            pltpu.SemaphoreType.DMA((pieces_out,)),
        ],
        compiler_params=pltpu.CompilerParams(vmem_limit_bytes=VMEM_LIMIT),
        name="sweep",
    )(view_id, mask, *flat, *measured, *bands)


def update_kernel(last, views, *refs):
    codes, mine, outs = refs[:views], refs[views], refs[views + 1 :]
    count = mine.shape[0]
    scales = [scale_of(code[count][0:count]) for code in codes]
    powers = []
    for y in range(count):
        total = sum(
            code[y].astype(jnp.float32) * scale[y : y + 1] for code, scale in zip(codes, scales)
        )
        value = mine[y] * total * jnp.float32(1.0 / views)
        if last:
            outs[0][y], power = encode(value)
            powers.append(power)
        else:
            outs[0][y] = value
            outs[1][y] = value.astype(jnp.bfloat16)
    if last:
        put_powers(outs[0].at[count], jnp.concatenate(powers, axis=0))


def update(codes, mine, last):
    views = len(codes)
    if last:
        shapes = [jax.ShapeDtypeStruct(codes[0].shape, jnp.int16)]
    else:
        shapes = [jax.ShapeDtypeStruct(mine.shape, t) for t in (jnp.float32, jnp.bfloat16)]
    return pl.pallas_call(
        functools.partial(update_kernel, last, views),
        out_shape=shapes,
        in_specs=[VMEM] * (views + 1),
        out_specs=[VMEM] * len(shapes),
        compiler_params=pltpu.CompilerParams(vmem_limit_bytes=VMEM_LIMIT),
        name="update",
    )(*codes, mine)


def gather_kernel(pieces, rows_piece, core, rows, cols, *refs):
    n = len(pieces)
    view_ref, codes, out, planes, sem = refs[0], refs[1 : n + 1], *refs[n + 1 :]
    plane_rows = rows + PAD
    for code, (bits, offset, count) in zip(codes, pieces):
        base = (view_ref[0] ^ bits) * rows_piece + offset
        scale = scale_of(code[count][0:rows_piece])
        for y in range(count):
            value = code[y].astype(jnp.float32) * scale[offset + y : offset + y + 1]
            for h, part in enumerate(halves(value)):
                planes[h, pl.ds(base + y, core, stride=plane_rows), :] = part
    copies = [
        pltpu.make_async_copy(
            planes.at[h, pl.ds(z * plane_rows, rows)],
            out.at[z, :, pl.ds(h * LANES, LANES)],
            sem.at[h, z],
        )
        for z in range(core)
        for h in range(cols // LANES)
    ]
    for copy in copies:
        copy.start()
    for copy in copies:
        copy.wait()


def gather(view_id, pieces, codes, rows, views):
    core, cols = codes[0].shape[1:]
    return pl.pallas_call(
        functools.partial(gather_kernel, pieces, rows // views, core, rows, cols),
        out_shape=jax.ShapeDtypeStruct((core, rows, cols), jnp.float32),
        in_specs=[SMEM] + [VMEM] * len(codes),
        out_specs=ANY,
        scratch_shapes=[
            pltpu.VMEM((cols // LANES, core * (rows + PAD), LANES), jnp.float32),
            pltpu.SemaphoreType.DMA((cols // LANES, core)),
        ],
        compiler_params=pltpu.CompilerParams(vmem_limit_bytes=VMEM_LIMIT),
        name="gather",
    )(view_id, *codes)


def band(taps, row_index, col_index):
    count = taps.shape[0]
    offsets = col_index[None, :] - row_index[:, None] + (count - 1) // 2
    chosen = offsets[None, :, :] == jnp.arange(count, dtype=jnp.int32)[:, None, None]
    return jnp.sum(jnp.where(chosen, taps[:, None, None], jnp.float32(0.0)), axis=0)


def on_device(estimate, views_data, psf_bank, psf_index, margin_extent):
    core, rows, cols = estimate.shape
    kernels_count = psf_bank.shape[0]
    tiles = lax.axis_size("tile")
    views = lax.axis_size("view")
    tile_id = lax.axis_index("tile")
    view_id = lax.axis_index("view")
    rows_piece = rows // views
    half = jnp.bfloat16

    near_pairs = [(t, t ^ 1) for t in range(tiles)]
    far_pairs = [(t, ((t + 1) ^ 1) - 1) for t in range(1, tiles - 1)]
    even = tile_id % 2 == 0

    def far(x):
        return lax.ppermute(x, "tile", far_pairs)

    def near(x):
        return lax.ppermute(x, "tile", near_pairs)

    def from_view(x, bits):
        return lax.ppermute(x, "view", [(v, v ^ bits) for v in range(views)])

    part = rows_piece // 2
    if views == 4:
        pieces = ((0, 0, rows_piece), (1, 0, rows_piece), (2, 0, rows_piece), (3, 0, part), (3, part, part))
    else:
        pieces = tuple((bits, 0, rows_piece) for bits in range(views))

    def share(x):
        if views != 4:
            return [x] + [from_view(x, bits) for bits in range(1, views)]
        one, two = from_view(x, 1), from_view(x, 2)
        first, second = one[:part], two[part:]
        if x.shape[0] > rows_piece:
            first = jnp.concatenate([first, one[rows_piece:]], axis=0)
        return [x, one, two, from_view(first, 2), from_view(second, 1)]

    def own_rows(volume):
        return lax.dynamic_slice_in_dim(volume, view_id * rows_piece, rows_piece, axis=1)

    first_piece = jnp.transpose(own_rows(estimate).astype(half), (1, 0, 2))
    first_piece, volume, data = lax.optimization_barrier((first_piece, estimate, views_data[0]))
    far_blocks = share(far(first_piece))
    bottom, top = data[:REACH], data[core - REACH :]
    to_far, to_near = jnp.where(even, bottom, top), jnp.where(even, top, bottom)
    measured = (far(to_far), data, near(to_near))
    start = jnp.transpose(volume.astype(half), (1, 0, 2))
    blocks = [far_blocks, [start], [near(start)]]

    chosen = (jnp.arange(kernels_count, dtype=jnp.int32) == psf_index[0]).astype(jnp.float32)
    taps = jnp.einsum("k,kat->at", chosen, psf_bank.astype(jnp.float32))
    cores = jnp.arange(core, dtype=jnp.int32) + MARGIN
    below, above = jnp.where(even, 0, MARGIN + core), jnp.where(even, MARGIN + core, 0)
    deep = jnp.arange(MARGIN, dtype=jnp.int32)
    position = jnp.concatenate([deep + below, cores, deep + above])
    low_reach, high_reach = MARGIN - REACH, MARGIN + core
    thin = jnp.arange(REACH, dtype=jnp.int32)
    wanted = jnp.concatenate(
        [
            thin + jnp.where(even, low_reach, high_reach),
            cores,
            thin + jnp.where(even, high_reach, low_reach),
        ]
    )

    def inside(k):
        global_pos = tile_id * core - MARGIN + k
        held = (k >= MARGIN - margin_extent[0, 0]) & (k < MARGIN + core + margin_extent[0, 1])
        return held & (global_pos >= 0) & (global_pos < core * tiles)

    natural = jnp.arange(rows, dtype=jnp.int32)
    held = ((natural // rows_piece) ^ view_id) * rows_piece + natural % rows_piece
    columns = jnp.arange(cols, dtype=jnp.int32)
    z_band = jnp.where(inside(position)[None, :], band(taps[0], wanted, position), 0.0).astype(half)
    z_back = band(taps[0], wanted, cores).T.astype(half)
    y_band = band(taps[1], natural, held).astype(half)
    y_back = y_band.T
    x_back = band(taps[2], columns, columns).astype(half)
    x_band = x_back.T
    mask = inside(wanted).astype(jnp.int32)

    here = view_id.astype(jnp.int32).reshape(1)
    bands = (z_band, z_back, y_band, y_back, x_band, x_back)
    for it in range(ITERS):
        codes = list(sweep(here, mask, pieces, blocks, measured, bands, views))
        if it == 0:
            volume, codes[0] = lax.optimization_barrier((estimate, codes[0]))
            mine = jnp.transpose(own_rows(volume), (1, 0, 2))
        arrived = [codes[0]] + [from_view(codes[bits], bits) for bits in range(1, views)]
        if it + 1 < ITERS:
            mine, rounded = update(arrived, mine, False)
            own = share(rounded)
            blocks = [[far(x) for x in own], own, [near(x) for x in own]]
        else:
            (code,) = update(arrived, mine, True)
    return gather(here, pieces, share(code), rows, views)


def solution(mesh):
    return jax.shard_map(
        on_device,
        mesh=mesh,
        in_specs=(
            P("tile", None, None),
            P("view", "tile", None, None),
            P(),
            P("view"),
            P("tile", None),
        ),
        out_specs=P("tile", None, None),
        check_vma=False,
    )
```

time: 230 us -> 198 us (0.86)
  waiting for transfers between devices: 111 us -> 92.8 us
  starting transfers between devices: 54.5 us -> 40.8 us
  Pallas kernels: 28.6 us -> 39.6 us
  local copies, waits for them, and re-layouts: 23.2 us -> 17.1 us
  other arithmetic: 9.66 us -> 5.02 us
    ppermute x12 -> x14, waiting for transfers between devices: 27 us -> 6.8 us  [the longest x7 6.79 us: far(): return lax.ppermute(x, 'tile', far_pairs)]
    ppermute x12 -> x14, starting transfers between devices: 31.5 us -> 19.6 us  [the longest x7 15.2 us: far(): return lax.ppermute(x, 'tile', far_pairs)]
    pallas_call x2 -> x5, Pallas kernels: 28.6 us -> 39.6 us  [the longest x2 27.3 us: sweep(): pl.pallas_call(functools.partial(sweep_kernel, (pieces, shares, pieces_ou...]
    unnamed x38 -> x71, local copies, waits for them, and re-layouts: 14.7 us -> 6.27 us
    optimization_barrier x0 -> x2, local copies, waits for them, and re-layouts: none -> 4.66 us  [the longest x1 2.43 us: on_device(): volume, codes[0] = lax.optimization_barrier((estimate, codes[0]))]
    dynamic_update_slice x4 -> x0, local copies, waits for them, and re-layouts: 3.7 us -> none  [on_device(): lax.dynamic_update_slice_in_dim(out, piece, (view_id ^ bits) * rows_piece...]
    convert_element_type x3 -> x2, other arithmetic: 3.58 us -> 1.17 us  [the longest x1 0.6 us: on_device(): jnp.where(inside(position)[None, :], band(taps[0], wanted, position), 0.0)]
    ppermute x21 -> x18, waiting for transfers between devices: 84.1 us -> 86 us  [from_view(): return lax.ppermute(x, 'view', [(v, v ^ bits) for v in range(views)])]
  transfers between devices with their start and end apart: 33 -> 32, of which waited for: 12 -> 18; matrix products, arithmetic and copies ran while one was open for 8% -> 7% of each run, Pallas kernels for 0% -> 0%
where the time goes in v2:
time: 198 us
  waiting for transfers between devices  92.8 us (47%)
  starting transfers between devices  40.8 us (21%)
  Pallas kernels  39.6 us (20%)
  local copies, waits for them, and re-layouts  17.1 us (9%)
  other arithmetic  5.02 us (3%)
  between operations  2.46 us (1%)
    ppermute x18, waiting for transfers between devices, from_view(): return lax.ppermute(x, 'view', [(v, v ^ bits) for v in range(views)])  86 us
    pallas_call x2, Pallas kernels, sweep(): pl.pallas_call(functools.partial(sweep_kernel, (pieces, shares, pieces_ou...  27.3 us
    ppermute x18, starting transfers between devices, from_view(): return lax.ppermute(x, 'view', [(v, v ^ bits) for v in range(views)])  21.3 us
    ppermute x7, starting transfers between devices, far(): return lax.ppermute(x, 'tile', far_pairs)  15.2 us
    pallas_call x2, Pallas kernels, update(): pl.pallas_call(functools.partial(update_kernel, last, views), out_shape=s...  7.31 us
    ppermute x7, waiting for transfers between devices, far(): return lax.ppermute(x, 'tile', far_pairs)  6.79 us
    unnamed x71, local copies, waits for them, and re-layouts  6.27 us
    pallas_call x1, Pallas kernels, gather(): pl.pallas_call(functools.partial(gather_kernel, pieces, rows // views, co...  5 us
  transfers between devices with their start and end apart: 32, of which 18 were waited for; matrix products, arithmetic and copies ran while one was open for 7% of the time, Pallas kernels for 0%

profile of v2, /device:TPU:8, one launch (start us, length us, event | category | flops | bytes accessed | tf_op | source)
XLA Modules:
  0.0 198.0 jit_solution(16173249971327225321)
XLA Ops:
  0.0 1.4 constant_dynamic-slice_fusion
  1.5 1.1 copy.31
  2.6 1.9 collective-permute-start
  4.5 1.4 broadcast_select_fusion
  5.9 1.7 collective-permute-start.7
  7.6 2.2 %collective-permute-start.6 = (bf16[16,128,256]{2,1,0:T(8,128)(2,1)}, bf16[16,128,256]{2,1,0:T(8,128)(2,1)}, u32[]{:S(2)}, u32[]{:S(2)}) collective-permute-start(bf16[16,128,256]{2,1,0:T(8,128)(2,1)} %get-tuple-element.40), channel_id=1, source_target_pairs={{4,8},{8,4},{12,16},{16,12},{20,24},{24,20},{5,9},{9,5},{13,17},{1... | collective-permute-start | bytes 3145736 | tf_op jit(solution)/shard_map/ppermute | solution.py:282
  9.9 2.2 %copy.30 = bf16[32,128,256]{2,0,1:T(8,128)(2,1)S(1)} copy(f32[32,128,256]{2,1,0:T(8,128)S(1)} %copy-done.1) | data formatting | bytes 6291456 | tf_op jit(solution)/shard_map/optimization_barrier | solution.py:309
  12.1 1.6 collective-permute-start.5
  17.5 1.6 collective-permute-start.2
  19.1 1.5 collective-permute-start.1
  20.7 0.9 select_reduce_fusion.refs_17_.refs_25_
  21.6 10.1 %collective-permute-done.2.refs_4_ = bf16[32,32,256]{2,1,0:T(8,128)(2,1)S(1)} collective-permute-done((bf16[32,32,256]{2,1,0:T(8,128)(2,1)}, bf16[32,32,256]{2,1,0:T(8,128)(2,1)S(1)}, u32[]{:S(2)}, u32[]{:S(2)}) %collective-permute-start.2) | collective-permute-done | bytes 524320 | tf_op jit(solution)/shard_map/ppermute | solution.py:288
  31.7 0.8 copy-done.11
  32.5 0.7 slice.60
  33.3 1.5 collective-permute-start.4
  34.8 0.8 copy-done.12
  35.5 0.7 slice.59
  36.3 1.5 collective-permute-start.3
  37.8 0.7 select_reduce_fusion.3
  38.6 0.7 copy.16.refs_14_.refs_22_
  39.4 0.7 copy.17.refs_16_.refs_24_
  40.1 0.6 select_convert_fusion.refs_12_.refs_20_
  41.0 2.7 %collective-permute-done.3.refs_5_ = bf16[16,32,256]{2,1,0:T(8,128)(2,1)} collective-permute-done((bf16[16,32,256]{2,1,0:T(8,128)(2,1)}, bf16[16,32,256]{2,1,0:T(8,128)(2,1)}, u32[]{:S(2)}, u32[]{:S(2)}) %collective-permute-start.3) | collective-permute-done | bytes 262176 | tf_op jit(solution)/shard_map/ppermute | solution.py:288
  43.8 13.8 %sweep.2 = (s16[33,32,256]{2,1,0:T(8,128)(2,1)}, s16[33,32,256]{2,1,0:T(8,128)(2,1)}, s16[33,32,256]{2,1,0:T(8,128)(2,1)}, s16[33,32,256]{2,1,0:T(8,128)(2,1)}) custom-call(s32[1]{0:T(128)} %bitcast.refs_0_, s32[64]{0:T(128)} %get-tuple-element.37.refs_1_, bf16[32,32,256]{2,1,0:T(8,128)(2,1)} %collective-permute-done.refs_2_, ...), custom_call_target="tpu_custom_call" | custom-call | tf_op jit(solution)/shard_map/sweep/pallas_call | solution.py:161
  57.6 0.6 collective-permute-start.8
  58.3 1.5 collective-permute-start.9
  59.8 1.4 collective-permute-start.10
  61.2 2.4 %copy.18 = f32[32,128,256]{2,0,1:T(8,128)S(1)} copy(f32[32,128,256]{2,1,0:T(8,128)S(1)} %copy-done.2) | data formatting | bytes 8388608 | tf_op jit(solution)/shard_map/optimization_barrier | solution.py:354
  63.6 1.1 dynamic-slice_bitcast_fusion.refs_4_
  64.7 8.4 %collective-permute-done.8.refs_1_ = s16[33,32,256]{2,1,0:T(8,128)(2,1)S(1)} collective-permute-done((s16[33,32,256]{2,1,0:T(8,128)(2,1)}, s16[33,32,256]{2,1,0:T(8,128)(2,1)S(1)}, u32[]{:S(2)}, u32[]{:S(2)}) %collective-permute-start.8) | collective-permute-done | bytes 540704 | tf_op jit(solution)/shard_map/ppermute | solution.py:288
  73.1 8.0 %collective-permute-done.9.refs_2_ = s16[33,32,256]{2,1,0:T(8,128)(2,1)S(1)} collective-permute-done((s16[33,32,256]{2,1,0:T(8,128)(2,1)}, s16[33,32,256]{2,1,0:T(8,128)(2,1)S(1)}, u32[]{:S(2)}, u32[]{:S(2)}) %collective-permute-start.9) | collective-permute-done | bytes 540704 | tf_op jit(solution)/shard_map/ppermute | solution.py:288
  81.2 1.5 collective-permute-done.10.refs_3_
  82.7 0.8 copy-done.16
  83.5 3.7 %update.2 = (f32[32,32,256]{2,1,0:T(8,128)}, bf16[32,32,256]{2,1,0:T(8,128)(2,1)}) custom-call(s16[33,32,256]{2,1,0:T(8,128)(2,1)} %get-tuple-element.24.refs_0_, s16[33,32,256]{2,1,0:T(8,128)(2,1)} %copy-done.13, s16[33,32,256]{2,1,0:T(8,128)(2,1)} %copy-done.14, s16[33,32,256]{2,1,0:T(8,128)(2,1)} %copy-done.16, ...), custom_call_target="tpu_custom_call" | custom-call | tf_op jit(solution)/shard_map/update/pallas_call | solution.py:208
  87.2 1.6 collective-permute-start.14
  88.8 1.5 collective-permute-start.12
  90.3 2.2 %collective-permute-start.11 = (bf16[32,32,256]{2,1,0:T(8,128)(2,1)}, bf16[32,32,256]{2,1,0:T(8,128)(2,1)S(1)}, u32[]{:S(2)}, u32[]{:S(2)}) collective-permute-start(bf16[32,32,256]{2,1,0:T(8,128)(2,1)} %get-tuple-element.29.refs_7_), channel_id=1, source_target_pairs={{4,8},{8,4},{12,16},{16,12},{20,24},{24,20},{5,9},{9,5},{13,17},{1... | collective-permute-start | bytes 1572872 | tf_op jit(solution)/shard_map/ppermute | solution.py:282
  92.5 5.8 %collective-permute-done.14.refs_9_ = bf16[32,32,256]{2,1,0:T(8,128)(2,1)S(1)} collective-permute-done((bf16[32,32,256]{2,1,0:T(8,128)(2,1)}, bf16[32,32,256]{2,1,0:T(8,128)(2,1)S(1)}, u32[]{:S(2)}, u32[]{:S(2)}) %collective-permute-start.14) | collective-permute-done | bytes 524320 | tf_op jit(solution)/shard_map/ppermute | solution.py:288
  98.4 0.6 collective-permute-start.18
  99.0 2.5 %collective-permute-start.15 = (bf16[32,32,256]{2,1,0:T(8,128)(2,1)S(1)}, bf16[32,32,256]{2,1,0:T(8,128)(2,1)S(1)}, u32[]{:S(2)}, u32[]{:S(2)}) collective-permute-start(bf16[32,32,256]{2,1,0:T(8,128)(2,1)S(1)} %collective-permute-done.14.refs_9_), channel_id=1, source_target_pairs={{4,8},{8,4},{12,16},{16,12},{20,24},{24,20},{5,9},{9,5},{13,17},{1... | collective-permute-start | bytes 1572872 | tf_op jit(solution)/shard_map/ppermute | solution.py:282
  101.5 2.3 %collective-permute-done.12.refs_8_ = bf16[32,32,256]{2,1,0:T(8,128)(2,1)S(1)} collective-permute-done((bf16[32,32,256]{2,1,0:T(8,128)(2,1)}, bf16[32,32,256]{2,1,0:T(8,128)(2,1)S(1)}, u32[]{:S(2)}, u32[]{:S(2)}) %collective-permute-start.12) | collective-permute-done | bytes 524320 | tf_op jit(solution)/shard_map/ppermute | solution.py:288
  104.3 4.7 %collective-permute-done.18.refs_11_ = bf16[16,32,256]{2,1,0:T(8,128)(2,1)S(1)} collective-permute-done((bf16[16,32,256]{2,1,0:T(8,128)(2,1)S(1)}, bf16[16,32,256]{2,1,0:T(8,128)(2,1)S(1)}, u32[]{:S(2)}, u32[]{:S(2)}) %collective-permute-start.18) | collective-permute-done | bytes 262176 | tf_op jit(solution)/shard_map/ppermute | solution.py:288
  109.0 1.9 collective-permute-start.13
  110.9 1.7 collective-permute-done.16.refs_10_
  112.6 2.4 %collective-permute-start.19 = (bf16[16,32,256]{2,1,0:T(8,128)(2,1)S(1)}, bf16[16,32,256]{2,1,0:T(8,128)(2,1)S(1)}, u32[]{:S(2)}, u32[]{:S(2)}) collective-permute-start(bf16[16,32,256]{2,1,0:T(8,128)(2,1)S(1)} %collective-permute-done.18.refs_11_), channel_id=1, source_target_pairs={{4,8},{8,4},{12,16},{16,12},{20,24},{24,20},{5,9},{9,5},{13,17},{1... | collective-permute-start | bytes 786440 | tf_op jit(solution)/shard_map/ppermute | solution.py:282
  115.1 1.1 collective-permute-start.23
  116.2 2.1 %collective-permute-start.17 = (bf16[16,32,256]{2,1,0:T(8,128)(2,1)S(1)}, bf16[16,32,256]{2,1,0:T(8,128)(2,1)S(1)}, u32[]{:S(2)}, u32[]{:S(2)}) collective-permute-start(bf16[16,32,256]{2,1,0:T(8,128)(2,1)S(1)} %collective-permute-done.16.refs_10_), channel_id=1, source_target_pairs={{4,8},{8,4},{12,16},{16,12},{20,24},{24,20},{5,9},{9,5},{13,17},{1... | collective-permute-start | bytes 786440 | tf_op jit(solution)/shard_map/ppermute | solution.py:282
  118.3 1.2 collective-permute-done.13.refs_3_
  119.5 2.8 %collective-permute-done.19.refs_6_ = bf16[16,32,256]{2,1,0:T(8,128)(2,1)S(1)} collective-permute-done((bf16[16,32,256]{2,1,0:T(8,128)(2,1)S(1)}, bf16[16,32,256]{2,1,0:T(8,128)(2,1)S(1)}, u32[]{:S(2)}, u32[]{:S(2)}) %collective-permute-start.19) | collective-permute-done | bytes 262176 | tf_op jit(solution)/shard_map/ppermute | solution.py:282
  122.3 2.8 %collective-permute-done.17.refs_5_ = bf16[16,32,256]{2,1,0:T(8,128)(2,1)S(1)} collective-permute-done((bf16[16,32,256]{2,1,0:T(8,128)(2,1)S(1)}, bf16[16,32,256]{2,1,0:T(8,128)(2,1)S(1)}, u32[]{:S(2)}, u32[]{:S(2)}) %collective-permute-start.17) | collective-permute-done | bytes 262176 | tf_op jit(solution)/shard_map/ppermute | solution.py:282
  125.2 0.7 copy-done.33
  125.9 13.4 %sweep.3 = (s16[33,32,256]{2,1,0:T(8,128)(2,1)}, s16[33,32,256]{2,1,0:T(8,128)(2,1)}, s16[33,32,256]{2,1,0:T(8,128)(2,1)}, s16[33,32,256]{2,1,0:T(8,128)(2,1)}) custom-call(s32[1]{0:T(128)} %bitcast.refs_0_, s32[64]{0:T(128)} %get-tuple-element.37.refs_1_, bf16[32,32,256]{2,1,0:T(8,128)(2,1)} %copy-done.21, bf16[32,32,256]{2,1,0:T(8,128)(2,1)} %copy-done.25, ...), custom_call_target="tpu_custom_call" | custom-call | tf_op jit(solution)/shard_map/sweep/pallas_call | solution.py:161
  139.4 1.6 collective-permute-start.25
  141.4 1.5 collective-permute-start.27
  142.9 11.8 %collective-permute-done.25.refs_1_ = s16[33,32,256]{2,1,0:T(8,128)(2,1)S(1)} collective-permute-done((s16[33,32,256]{2,1,0:T(8,128)(2,1)}, s16[33,32,256]{2,1,0:T(8,128)(2,1)S(1)}, u32[]{:S(2)}, u32[]{:S(2)}) %collective-permute-start.25) | collective-permute-done | bytes 540704 | tf_op jit(solution)/shard_map/ppermute | solution.py:288
  154.8 12.0 %collective-permute-done.26.refs_2_ = s16[33,32,256]{2,1,0:T(8,128)(2,1)S(1)} collective-permute-done((s16[33,32,256]{2,1,0:T(8,128)(2,1)}, s16[33,32,256]{2,1,0:T(8,128)(2,1)S(1)}, u32[]{:S(2)}, u32[]{:S(2)}) %collective-permute-start.26) | collective-permute-done | bytes 540704 | tf_op jit(solution)/shard_map/ppermute | solution.py:288
  166.8 0.8 copy-done.17
  167.7 3.6 %update.3.refs_1_ = s16[33,32,256]{2,1,0:T(8,128)(2,1)} custom-call(s16[33,32,256]{2,1,0:T(8,128)(2,1)} %get-tuple-element.30.refs_0_, s16[33,32,256]{2,1,0:T(8,128)(2,1)} %copy-done.15, s16[33,32,256]{2,1,0:T(8,128)(2,1)} %copy-done.17, s16[33,32,256]{2,1,0:T(8,128)(2,1)} %copy-done.18, f32[32,32,256]{2,1,0:T(8,128)} %get-tuple-element.34.refs_4_), custom_call_target="tpu_custom_call" | custom-call | tf_op jit(solution)/shard_map/update/pallas_call | solution.py:208
  171.9 1.0 collective-permute-start.28
  172.9 11.8 %collective-permute-done.29.refs_3_ = s16[33,32,256]{2,1,0:T(8,128)(2,1)S(1)} collective-permute-done((s16[33,32,256]{2,1,0:T(8,128)(2,1)}, s16[33,32,256]{2,1,0:T(8,128)(2,1)S(1)}, u32[]{:S(2)}, u32[]{:S(2)}) %collective-permute-start.29) | collective-permute-done | bytes 540704 | tf_op jit(solution)/shard_map/ppermute | solution.py:288
  185.2 1.9 collective-permute-start.30
  187.1 4.3 %collective-permute-done.31.refs_5_ = s16[17,32,256]{2,1,0:T(8,128)(2,1)S(1)} collective-permute-done((s16[17,32,256]{2,1,0:T(8,128)(2,1)S(1)}, s16[17,32,256]{2,1,0:T(8,128)(2,1)S(1)}, u32[]{:S(2)}, u32[]{:S(2)}) %collective-permute-start.31) | collective-permute-done | bytes 278560 | tf_op jit(solution)/shard_map/ppermute | solution.py:288
  192.1 0.7 copy-done.27
  192.8 5.0 %gather.1 = f32[32,128,256]{2,1,0:T(8,128)} custom-call(s32[1]{0:T(128)} %bitcast.refs_0_, s16[33,32,256]{2,1,0:T(8,128)(2,1)} %update.3.refs_1_, s16[33,32,256]{2,1,0:T(8,128)(2,1)} %copy-done.8, s16[33,32,256]{2,1,0:T(8,128)(2,1)} %copy-done.7, s16[17,32,256]{2,1,0:T(8,128)(2,1)} %copy-done.27, s16[17,32,256]{2,1,0:T(8,128)(2,1)} %copy-done.26), custom_call_target="tpu_custom_call" | custom-call | tf_op jit(solution)/shard_map/gather/pallas_call | solution.py:246
  (111 shorter events, 5.5 us)
Async XLA Ops:
  0.0 14.3 %copy-start = (bf16[8,3,33]{2,0,1:T(8,128)(2,1)S(1)}, bf16[8,3,33]{2,0,1:T(8,128)(2,1)}, u32[]{:S(2)}) copy-start(bf16[8,3,33]{2,0,1:T(8,128)(2,1)} %param.7) | copy-start | bytes 4756
  0.0 4.5 %copy-start.3 = (bf16[1,32,128,256]{3,2,1,0:T(8,128)(2,1)S(1)}, bf16[1,32,128,256]{3,2,1,0:T(8,128)(2,1)}, u32[]{:S(2)}) copy-start(bf16[1,32,128,256]{3,2,1,0:T(8,128)(2,1)} %param.6) | copy-start | bytes 6291460
  2.6 15.0 %collective-permute-start = (bf16[32,32,256]{2,1,0:T(8,128)(2,1)}, bf16[32,32,256]{2,1,0:T(8,128)(2,1)}, u32[]{:S(2)}, u32[]{:S(2)}) collective-permute-start(bf16[32,32,256]{2,1,0:T(8,128)(2,1)} %bitcast.29), channel_id=1, source_target_pairs={{4,8},{8,4},{12,16},{16,12},{20,24},{24,20},{5,9},{9,5},{13,17},{1... | collective-permute-start | bytes 1572872 | tf_op jit(solution)/shard_map/ppermute | solution.py:282
  4.5 5.4 %copy-start.1 = (f32[32,128,256]{2,1,0:T(8,128)S(1)}, f32[32,128,256]{2,1,0:T(8,128)}, u32[]{:S(2)}) copy-start(f32[32,128,256]{2,1,0:T(8,128)} %param.5) | copy-start | bytes 12582916
  5.9 34.8 %collective-permute-start.7 = (bf16[16,128,256]{2,1,0:T(8,128)(2,1)}, bf16[16,128,256]{2,1,0:T(8,128)(2,1)S(1)}, u32[]{:S(2)}, u32[]{:S(2)}) collective-permute-start(bf16[16,128,256]{2,1,0:T(8,128)(2,1)} %get-tuple-element.39), channel_id=1, source_target_pairs={{0,4},{4,0},{8,12},{12,8},{16,20},{20,16},{24,28},{28,24},{1,5},{5... | collective-permute-start | bytes 3145736 | tf_op jit(solution)/shard_map/ppermute | solution.py:285
  7.6 6.9 %copy-start.34 = (s32[1,2]{1,0:T(1,128)S(1)}, s32[1,2]{1,0:T(1,128)}, u32[]{:S(2)}) copy-start(s32[1,2]{1,0:T(1,128)} %param.9) | copy-start | bytes 28
  7.6 33.1 %collective-permute-start.6 = (bf16[16,128,256]{2,1,0:T(8,128)(2,1)}, bf16[16,128,256]{2,1,0:T(8,128)(2,1)}, u32[]{:S(2)}, u32[]{:S(2)}) collective-permute-start(bf16[16,128,256]{2,1,0:T(8,128)(2,1)} %get-tuple-element.40), channel_id=1, source_target_pairs={{4,8},{8,4},{12,16},{16,12},{20,24},{24,20},{5,9},{9,5},{13,17},{1... | collective-permute-start | bytes 3145736 | tf_op jit(solution)/shard_map/ppermute | solution.py:282
  12.1 31.7 %copy-start.4 = (bf16[32,128,256]{2,0,1:T(8,128)(2,1)}, bf16[32,128,256]{2,0,1:T(8,128)(2,1)S(1)}, u32[]{:S(2)}) copy-start(bf16[32,128,256]{2,0,1:T(8,128)(2,1)S(1)} %copy.30) | copy-start | bytes 6291460
  12.1 31.6 %collective-permute-start.5 = (bf16[128,32,256]{2,1,0:T(8,128)(2,1)S(1)}, bf16[128,32,256]{2,1,0:T(8,128)(2,1)}, u32[]{:S(2)}, u32[]{:S(2)}) collective-permute-start(bf16[128,32,256]{2,1,0:T(8,128)(2,1)S(1)} %bitcast.35), channel_id=1, source_target_pairs={{0,4},{4,0},{8,12},{12,8},{16,20},{20,16},{24,28},{28,24},{1,5},{5... | collective-permute-start | bytes 6291464 | tf_op jit(solution)/shard_map/ppermute | solution.py:285
  17.5 14.2 %collective-permute-start.2 = (bf16[32,32,256]{2,1,0:T(8,128)(2,1)}, bf16[32,32,256]{2,1,0:T(8,128)(2,1)S(1)}, u32[]{:S(2)}, u32[]{:S(2)}) collective-permute-start(bf16[32,32,256]{2,1,0:T(8,128)(2,1)} %collective-permute-done.refs_2_), channel_id=1, source_target_pairs={{0,2},{1,3},{2,0},{3,1},{4,6},{5,7},{6,4},{7,5},{8,10},{9,11},{10,... | collective-permute-start | bytes 1572872 | tf_op jit(solution)/shard_map/ppermute | solution.py:288
  19.1 15.6 %collective-permute-start.1 = (bf16[32,32,256]{2,1,0:T(8,128)(2,1)}, bf16[32,32,256]{2,1,0:T(8,128)(2,1)S(1)}, u32[]{:S(2)}, u32[]{:S(2)}) collective-permute-start(bf16[32,32,256]{2,1,0:T(8,128)(2,1)} %collective-permute-done.refs_2_), channel_id=1, source_target_pairs={{0,1},{1,0},{2,3},{3,2},{4,5},{5,4},{6,7},{7,6},{8,9},{9,8},{10,11... | collective-permute-start | bytes 1572872 | tf_op jit(solution)/shard_map/ppermute | solution.py:288
  21.6 22.2 %copy-start.6 = (bf16[256,256]{1,0:T(8,128)(2,1)}, bf16[256,256]{1,0:T(8,128)(2,1)S(1)}, u32[]{:S(2)}) copy-start(bf16[256,256]{1,0:T(8,128)(2,1)S(1)} %select_reduce_fusion.refs_17_.refs_25_) | copy-start | bytes 393220
  31.7 0.8 copy-start.11
  33.3 7.8 %collective-permute-start.4 = (bf16[16,32,256]{2,1,0:T(8,128)(2,1)}, bf16[16,32,256]{2,1,0:T(8,128)(2,1)}, u32[]{:S(2)}, u32[]{:S(2)}) collective-permute-start(bf16[16,32,256]{2,1,0:T(8,128)(2,1)} %slice.60), channel_id=1, source_target_pairs={{0,1},{1,0},{2,3},{3,2},{4,5},{5,4},{6,7},{7,6},{8,9},{9,8},{10,11... | collective-permute-start | bytes 786440 | tf_op jit(solution)/shard_map/ppermute | solution.py:288
  34.7 0.8 copy-start.12
  36.3 7.5 %collective-permute-start.3 = (bf16[16,32,256]{2,1,0:T(8,128)(2,1)}, bf16[16,32,256]{2,1,0:T(8,128)(2,1)}, u32[]{:S(2)}, u32[]{:S(2)}) collective-permute-start(bf16[16,32,256]{2,1,0:T(8,128)(2,1)} %slice.59), channel_id=1, source_target_pairs={{0,2},{1,3},{2,0},{3,1},{4,6},{5,7},{6,4},{7,5},{8,10},{9,11},{10,... | collective-permute-start | bytes 786440 | tf_op jit(solution)/shard_map/ppermute | solution.py:288
  38.6 5.1 %copy-start.19 = (bf16[128,128]{0,1:T(8,128)(2,1)}, bf16[128,128]{0,1:T(8,128)(2,1)S(1)}, u32[]{:S(2)}) copy-start(bf16[128,128]{0,1:T(8,128)(2,1)S(1)} %copy.15) | copy-start | bytes 98308
  40.7 3.1 %copy-start.5 = (bf16[16,128,256]{2,1,0:T(8,128)(2,1)}, bf16[16,128,256]{2,1,0:T(8,128)(2,1)S(1)}, u32[]{:S(2)}) copy-start(bf16[16,128,256]{2,1,0:T(8,128)(2,1)S(1)} %collective-permute-done.7.refs_11_.refs_19_) | copy-start | bytes 3145732
  43.8 17.4 %copy-start.2 = (f32[32,128,256]{2,1,0:T(8,128)S(1)}, f32[32,128,256]{2,1,0:T(8,128)}, u32[]{:S(2)}) copy-start(f32[32,128,256]{2,1,0:T(8,128)} %param.5) | copy-start | bytes 12582916
  57.6 15.5 %collective-permute-start.8 = (s16[33,32,256]{2,1,0:T(8,128)(2,1)}, s16[33,32,256]{2,1,0:T(8,128)(2,1)S(1)}, u32[]{:S(2)}, u32[]{:S(2)}) collective-permute-start(s16[33,32,256]{2,1,0:T(8,128)(2,1)} %get-tuple-element.25), channel_id=1, source_target_pairs={{0,1},{1,0},{2,3},{3,2},{4,5},{5,4},{6,7},{7,6},{8,9},{9,8},{10,11... | collective-permute-start | bytes 1622024 | tf_op jit(solution)/shard_map/ppermute | solution.py:288
  58.3 22.9 %collective-permute-start.9 = (s16[33,32,256]{2,1,0:T(8,128)(2,1)}, s16[33,32,256]{2,1,0:T(8,128)(2,1)S(1)}, u32[]{:S(2)}, u32[]{:S(2)}) collective-permute-start(s16[33,32,256]{2,1,0:T(8,128)(2,1)} %get-tuple-element.26), channel_id=1, source_target_pairs={{0,2},{1,3},{2,0},{3,1},{4,6},{5,7},{6,4},{7,5},{8,10},{9,11},{10,... | collective-permute-start | bytes 1622024 | tf_op jit(solution)/shard_map/ppermute | solution.py:288
  59.8 22.9 %collective-permute-start.10 = (s16[33,32,256]{2,1,0:T(8,128)(2,1)}, s16[33,32,256]{2,1,0:T(8,128)(2,1)S(1)}, u32[]{:S(2)}, u32[]{:S(2)}) collective-permute-start(s16[33,32,256]{2,1,0:T(8,128)(2,1)} %get-tuple-element.27), channel_id=1, source_target_pairs={{0,3},{1,2},{2,1},{3,0},{4,7},{5,6},{6,5},{7,4},{8,11},{9,10},{10,... | collective-permute-start | bytes 1622024 | tf_op jit(solution)/shard_map/ppermute | solution.py:288
  73.1 9.5 %copy-start.13 = (s16[33,32,256]{2,1,0:T(8,128)(2,1)}, s16[33,32,256]{2,1,0:T(8,128)(2,1)S(1)}, u32[]{:S(2)}) copy-start(s16[33,32,256]{2,1,0:T(8,128)(2,1)S(1)} %collective-permute-done.8.refs_1_) | copy-start | bytes 1622020
  81.2 1.5 copy-start.14
  82.7 0.8 copy-start.16
  87.2 11.1 %collective-permute-start.14 = (bf16[32,32,256]{2,1,0:T(8,128)(2,1)}, bf16[32,32,256]{2,1,0:T(8,128)(2,1)S(1)}, u32[]{:S(2)}, u32[]{:S(2)}) collective-permute-start(bf16[32,32,256]{2,1,0:T(8,128)(2,1)} %get-tuple-element.29.refs_7_), channel_id=1, source_target_pairs={{0,2},{1,3},{2,0},{3,1},{4,6},{5,7},{6,4},{7,5},{8,10},{9,11},{10,... | collective-permute-start | bytes 1572872 | tf_op jit(solution)/shard_map/ppermute | solution.py:288
  88.8 10.2 %collective-permute-start.20 = (bf16[32,32,256]{2,1,0:T(8,128)(2,1)}, bf16[32,32,256]{2,1,0:T(8,128)(2,1)S(1)}, u32[]{:S(2)}, u32[]{:S(2)}) collective-permute-start(bf16[32,32,256]{2,1,0:T(8,128)(2,1)} %get-tuple-element.29.refs_7_), channel_id=1, source_target_pairs={{0,4},{4,0},{8,12},{12,8},{16,20},{20,16},{24,28},{28,24},{1,5},{5... | collective-permute-start | bytes 1572872 | tf_op jit(solution)/shard_map/ppermute | solution.py:285
  88.8 14.9 %collective-permute-start.12 = (bf16[32,32,256]{2,1,0:T(8,128)(2,1)}, bf16[32,32,256]{2,1,0:T(8,128)(2,1)S(1)}, u32[]{:S(2)}, u32[]{:S(2)}) collective-permute-start(bf16[32,32,256]{2,1,0:T(8,128)(2,1)} %get-tuple-element.29.refs_7_), channel_id=1, source_target_pairs={{0,1},{1,0},{2,3},{3,2},{4,5},{5,4},{6,7},{7,6},{8,9},{9,8},{10,11... | collective-permute-start | bytes 1572872 | tf_op jit(solution)/shard_map/ppermute | solution.py:288
  90.3 13.5 %collective-permute-start.11 = (bf16[32,32,256]{2,1,0:T(8,128)(2,1)}, bf16[32,32,256]{2,1,0:T(8,128)(2,1)S(1)}, u32[]{:S(2)}, u32[]{:S(2)}) collective-permute-start(bf16[32,32,256]{2,1,0:T(8,128)(2,1)} %get-tuple-element.29.refs_7_), channel_id=1, source_target_pairs={{4,8},{8,4},{12,16},{16,12},{20,24},{24,20},{5,9},{9,5},{13,17},{1... | collective-permute-start | bytes 1572872 | tf_op jit(solution)/shard_map/ppermute | solution.py:282
  98.3 26.8 %copy-start.9 = (bf16[32,32,256]{2,1,0:T(8,128)(2,1)}, bf16[32,32,256]{2,1,0:T(8,128)(2,1)S(1)}, u32[]{:S(2)}) copy-start(bf16[32,32,256]{2,1,0:T(8,128)(2,1)S(1)} %collective-permute-done.14.refs_9_) | copy-start | bytes 1572868
  98.4 10.6 %collective-permute-start.18 = (bf16[16,32,256]{2,1,0:T(8,128)(2,1)S(1)}, bf16[16,32,256]{2,1,0:T(8,128)(2,1)S(1)}, u32[]{:S(2)}, u32[]{:S(2)}) collective-permute-start(bf16[16,32,256]{2,1,0:T(8,128)(2,1)S(1)} %slice.62), channel_id=1, source_target_pairs={{0,1},{1,0},{2,3},{3,2},{4,5},{5,4},{6,7},{7,6},{8,9},{9,8},{10,11... | collective-permute-start | bytes 786440 | tf_op jit(solution)/shard_map/ppermute | solution.py:288
  99.0 13.6 %collective-permute-start.22 = (bf16[32,32,256]{2,1,0:T(8,128)(2,1)S(1)}, bf16[32,32,256]{2,1,0:T(8,128)(2,1)S(1)}, u32[]{:S(2)}, u32[]{:S(2)}) collective-permute-start(bf16[32,32,256]{2,1,0:T(8,128)(2,1)S(1)} %collective-permute-done.14.refs_9_), channel_id=1, source_target_pairs={{0,4},{4,0},{8,12},{12,8},{16,20},{20,16},{24,28},{28,24},{1,5},{5... | collective-permute-start | bytes 1572872 | tf_op jit(solution)/shard_map/ppermute | solution.py:285
  99.0 26.1 %copy-start.20 = (bf16[32,32,256]{2,1,0:T(8,128)(2,1)}, bf16[32,32,256]{2,1,0:T(8,128)(2,1)S(1)}, u32[]{:S(2)}) copy-start(bf16[32,32,256]{2,1,0:T(8,128)(2,1)S(1)} %collective-permute-done.20.refs_12_) | copy-start | bytes 1572868
  99.0 16.0 %collective-permute-start.15 = (bf16[32,32,256]{2,1,0:T(8,128)(2,1)S(1)}, bf16[32,32,256]{2,1,0:T(8,128)(2,1)S(1)}, u32[]{:S(2)}, u32[]{:S(2)}) collective-permute-start(bf16[32,32,256]{2,1,0:T(8,128)(2,1)S(1)} %collective-permute-done.14.refs_9_), channel_id=1, source_target_pairs={{4,8},{8,4},{12,16},{16,12},{20,24},{24,20},{5,9},{9,5},{13,17},{1... | collective-permute-start | bytes 1572872 | tf_op jit(solution)/shard_map/ppermute | solution.py:282
  103.8 21.4 %copy-start.10 = (bf16[32,32,256]{2,1,0:T(8,128)(2,1)}, bf16[32,32,256]{2,1,0:T(8,128)(2,1)S(1)}, u32[]{:S(2)}) copy-start(bf16[32,32,256]{2,1,0:T(8,128)(2,1)S(1)} %collective-permute-done.12.refs_8_) | copy-start | bytes 1572868
  103.8 12.4 %collective-permute-start.21 = (bf16[32,32,256]{2,1,0:T(8,128)(2,1)S(1)}, bf16[32,32,256]{2,1,0:T(8,128)(2,1)S(1)}, u32[]{:S(2)}, u32[]{:S(2)}) collective-permute-start(bf16[32,32,256]{2,1,0:T(8,128)(2,1)S(1)} %collective-permute-done.12.refs_8_), channel_id=1, source_target_pairs={{0,4},{4,0},{8,12},{12,8},{16,20},{20,16},{24,28},{28,24},{1,5},{5... | collective-permute-start | bytes 1572872 | tf_op jit(solution)/shard_map/ppermute | solution.py:285
  103.8 21.3 %copy-start.21 = (bf16[32,32,256]{2,1,0:T(8,128)(2,1)}, bf16[32,32,256]{2,1,0:T(8,128)(2,1)S(1)}, u32[]{:S(2)}) copy-start(bf16[32,32,256]{2,1,0:T(8,128)(2,1)S(1)} %collective-permute-done.11.refs_2_) | copy-start | bytes 1572868
  103.8 8.8 %collective-permute-start.16 = (bf16[16,32,256]{2,1,0:T(8,128)(2,1)S(1)}, bf16[16,32,256]{2,1,0:T(8,128)(2,1)S(1)}, u32[]{:S(2)}, u32[]{:S(2)}) collective-permute-start(bf16[16,32,256]{2,1,0:T(8,128)(2,1)S(1)} %slice.61), channel_id=1, source_target_pairs={{0,2},{1,3},{2,0},{3,1},{4,6},{5,7},{6,4},{7,5},{8,10},{9,11},{10,... | collective-permute-start | bytes 786440 | tf_op jit(solution)/shard_map/ppermute | solution.py:288
  109.0 16.1 %copy-start.28 = (bf16[16,32,256]{2,1,0:T(8,128)(2,1)}, bf16[16,32,256]{2,1,0:T(8,128)(2,1)S(1)}, u32[]{:S(2)}) copy-start(bf16[16,32,256]{2,1,0:T(8,128)(2,1)S(1)} %collective-permute-done.18.refs_11_) | copy-start | bytes 786436
  109.0 10.5 %collective-permute-start.13 = (bf16[32,32,256]{2,1,0:T(8,128)(2,1)S(1)}, bf16[32,32,256]{2,1,0:T(8,128)(2,1)S(1)}, u32[]{:S(2)}, u32[]{:S(2)}) collective-permute-start(bf16[32,32,256]{2,1,0:T(8,128)(2,1)S(1)} %collective-permute-done.12.refs_8_), channel_id=1, source_target_pairs={{4,8},{8,4},{12,16},{16,12},{20,24},{24,20},{5,9},{9,5},{13,17},{1... | collective-permute-start | bytes 1572872 | tf_op jit(solution)/shard_map/ppermute | solution.py:282
  112.6 12.5 %copy-start.29 = (bf16[16,32,256]{2,1,0:T(8,128)(2,1)}, bf16[16,32,256]{2,1,0:T(8,128)(2,1)S(1)}, u32[]{:S(2)}) copy-start(bf16[16,32,256]{2,1,0:T(8,128)(2,1)S(1)} %collective-permute-done.16.refs_10_) | copy-start | bytes 786436
  112.6 6.9 %collective-permute-start.24 = (bf16[16,32,256]{2,1,0:T(8,128)(2,1)S(1)}, bf16[16,32,256]{2,1,0:T(8,128)(2,1)S(1)}, u32[]{:S(2)}, u32[]{:S(2)}) collective-permute-start(bf16[16,32,256]{2,1,0:T(8,128)(2,1)S(1)} %collective-permute-done.18.refs_11_), channel_id=1, source_target_pairs={{0,4},{4,0},{8,12},{12,8},{16,20},{20,16},{24,28},{28,24},{1,5},{5... | collective-permute-start | bytes 786440 | tf_op jit(solution)/shard_map/ppermute | solution.py:285
  112.6 12.5 %copy-start.22 = (bf16[32,32,256]{2,1,0:T(8,128)(2,1)}, bf16[32,32,256]{2,1,0:T(8,128)(2,1)S(1)}, u32[]{:S(2)}) copy-start(bf16[32,32,256]{2,1,0:T(8,128)(2,1)S(1)} %collective-permute-done.22.refs_14_) | copy-start | bytes 1572868
  112.6 9.7 %collective-permute-start.19 = (bf16[16,32,256]{2,1,0:T(8,128)(2,1)S(1)}, bf16[16,32,256]{2,1,0:T(8,128)(2,1)S(1)}, u32[]{:S(2)}, u32[]{:S(2)}) collective-permute-start(bf16[16,32,256]{2,1,0:T(8,128)(2,1)S(1)} %collective-permute-done.18.refs_11_), channel_id=1, source_target_pairs={{4,8},{8,4},{12,16},{16,12},{20,24},{24,20},{5,9},{9,5},{13,17},{1... | collective-permute-start | bytes 786440 | tf_op jit(solution)/shard_map/ppermute | solution.py:282
  115.1 10.1 %copy-start.23 = (bf16[32,32,256]{2,1,0:T(8,128)(2,1)}, bf16[32,32,256]{2,1,0:T(8,128)(2,1)S(1)}, u32[]{:S(2)}) copy-start(bf16[32,32,256]{2,1,0:T(8,128)(2,1)S(1)} %collective-permute-done.15.refs_4_) | copy-start | bytes 1572868
  115.1 7.2 %collective-permute-start.23 = (bf16[16,32,256]{2,1,0:T(8,128)(2,1)S(1)}, bf16[16,32,256]{2,1,0:T(8,128)(2,1)S(1)}, u32[]{:S(2)}, u32[]{:S(2)}) collective-permute-start(bf16[16,32,256]{2,1,0:T(8,128)(2,1)S(1)} %collective-permute-done.16.refs_10_), channel_id=1, source_target_pairs={{0,4},{4,0},{8,12},{12,8},{16,20},{20,16},{24,28},{28,24},{1,5},{5... | collective-permute-start | bytes 786440 | tf_op jit(solution)/shard_map/ppermute | solution.py:285
  116.2 9.0 %copy-start.24 = (bf16[32,32,256]{2,1,0:T(8,128)(2,1)}, bf16[32,32,256]{2,1,0:T(8,128)(2,1)S(1)}, u32[]{:S(2)}) copy-start(bf16[32,32,256]{2,1,0:T(8,128)(2,1)S(1)} %collective-permute-done.21.refs_13_) | copy-start | bytes 1572868
  116.2 8.9 %collective-permute-start.17 = (bf16[16,32,256]{2,1,0:T(8,128)(2,1)S(1)}, bf16[16,32,256]{2,1,0:T(8,128)(2,1)S(1)}, u32[]{:S(2)}, u32[]{:S(2)}) collective-permute-start(bf16[16,32,256]{2,1,0:T(8,128)(2,1)S(1)} %collective-permute-done.16.refs_10_), channel_id=1, source_target_pairs={{4,8},{8,4},{12,16},{16,12},{20,24},{24,20},{5,9},{9,5},{13,17},{1... | collective-permute-start | bytes 786440 | tf_op jit(solution)/shard_map/ppermute | solution.py:282
  119.5 5.7 %copy-start.25 = (bf16[32,32,256]{2,1,0:T(8,128)(2,1)}, bf16[32,32,256]{2,1,0:T(8,128)(2,1)S(1)}, u32[]{:S(2)}) copy-start(bf16[32,32,256]{2,1,0:T(8,128)(2,1)S(1)} %collective-permute-done.13.refs_3_) | copy-start | bytes 1572868
  119.5 5.7 %copy-start.30 = (bf16[16,32,256]{2,1,0:T(8,128)(2,1)}, bf16[16,32,256]{2,1,0:T(8,128)(2,1)S(1)}, u32[]{:S(2)}) copy-start(bf16[16,32,256]{2,1,0:T(8,128)(2,1)S(1)} %collective-permute-done.24.refs_16_) | copy-start | bytes 786436
  122.3 2.9 %copy-start.31 = (bf16[16,32,256]{2,1,0:T(8,128)(2,1)}, bf16[16,32,256]{2,1,0:T(8,128)(2,1)S(1)}, u32[]{:S(2)}) copy-start(bf16[16,32,256]{2,1,0:T(8,128)(2,1)S(1)} %collective-permute-done.19.refs_6_) | copy-start | bytes 786436
  122.3 2.9 %copy-start.32 = (bf16[16,32,256]{2,1,0:T(8,128)(2,1)}, bf16[16,32,256]{2,1,0:T(8,128)(2,1)S(1)}, u32[]{:S(2)}) copy-start(bf16[16,32,256]{2,1,0:T(8,128)(2,1)S(1)} %collective-permute-done.23.refs_15_) | copy-start | bytes 786436
  139.4 15.4 %collective-permute-start.25 = (s16[33,32,256]{2,1,0:T(8,128)(2,1)}, s16[33,32,256]{2,1,0:T(8,128)(2,1)S(1)}, u32[]{:S(2)}, u32[]{:S(2)}) collective-permute-start(s16[33,32,256]{2,1,0:T(8,128)(2,1)} %get-tuple-element.31), channel_id=1, source_target_pairs={{0,1},{1,0},{2,3},{3,2},{4,5},{5,4},{6,7},{7,6},{8,9},{9,8},{10,11... | collective-permute-start | bytes 1622024 | tf_op jit(solution)/shard_map/ppermute | solution.py:288
  140.9 25.8 %collective-permute-start.26 = (s16[33,32,256]{2,1,0:T(8,128)(2,1)}, s16[33,32,256]{2,1,0:T(8,128)(2,1)S(1)}, u32[]{:S(2)}, u32[]{:S(2)}) collective-permute-start(s16[33,32,256]{2,1,0:T(8,128)(2,1)} %get-tuple-element.32), channel_id=1, source_target_pairs={{0,2},{1,3},{2,0},{3,1},{4,6},{5,7},{6,4},{7,5},{8,10},{9,11},{10,... | collective-permute-start | bytes 1622024 | tf_op jit(solution)/shard_map/ppermute | solution.py:288
  141.4 25.3 %collective-permute-start.27 = (s16[33,32,256]{2,1,0:T(8,128)(2,1)}, s16[33,32,256]{2,1,0:T(8,128)(2,1)S(1)}, u32[]{:S(2)}, u32[]{:S(2)}) collective-permute-start(s16[33,32,256]{2,1,0:T(8,128)(2,1)} %get-tuple-element.33), channel_id=1, source_target_pairs={{0,3},{1,2},{2,1},{3,0},{4,7},{5,6},{6,5},{7,4},{8,11},{9,10},{10,... | collective-permute-start | bytes 1622024 | tf_op jit(solution)/shard_map/ppermute | solution.py:288
  154.8 12.0 %copy-start.15 = (s16[33,32,256]{2,1,0:T(8,128)(2,1)}, s16[33,32,256]{2,1,0:T(8,128)(2,1)S(1)}, u32[]{:S(2)}) copy-start(s16[33,32,256]{2,1,0:T(8,128)(2,1)S(1)} %collective-permute-done.25.refs_1_) | copy-start | bytes 1622020
  166.7 0.8 copy-start.17
  166.7 1.0 copy-start.18
  171.3 13.3 %collective-permute-start.29 = (s16[33,32,256]{2,1,0:T(8,128)(2,1)}, s16[33,32,256]{2,1,0:T(8,128)(2,1)S(1)}, u32[]{:S(2)}, u32[]{:S(2)}) collective-permute-start(s16[33,32,256]{2,1,0:T(8,128)(2,1)} %update.3.refs_1_), channel_id=1, source_target_pairs={{0,2},{1,3},{2,0},{3,1},{4,6},{5,7},{6,4},{7,5},{8,10},{9,11},{10,... | collective-permute-start | bytes 1622024 | tf_op jit(solution)/shard_map/ppermute | solution.py:288
  171.9 13.3 %collective-permute-start.28 = (s16[33,32,256]{2,1,0:T(8,128)(2,1)}, s16[33,32,256]{2,1,0:T(8,128)(2,1)S(1)}, u32[]{:S(2)}, u32[]{:S(2)}) collective-permute-start(s16[33,32,256]{2,1,0:T(8,128)(2,1)} %update.3.refs_1_), channel_id=1, source_target_pairs={{0,1},{1,0},{2,3},{3,2},{4,5},{5,4},{6,7},{7,6},{8,9},{9,8},{10,11... | collective-permute-start | bytes 1622024 | tf_op jit(solution)/shard_map/ppermute | solution.py:288
  184.7 7.2 %copy-start.7 = (s16[33,32,256]{2,1,0:T(8,128)(2,1)}, s16[33,32,256]{2,1,0:T(8,128)(2,1)S(1)}, u32[]{:S(2)}) copy-start(s16[33,32,256]{2,1,0:T(8,128)(2,1)S(1)} %collective-permute-done.29.refs_3_) | copy-start | bytes 1622020
  184.7 6.7 %collective-permute-start.31 = (s16[17,32,256]{2,1,0:T(8,128)(2,1)S(1)}, s16[17,32,256]{2,1,0:T(8,128)(2,1)S(1)}, u32[]{:S(2)}, u32[]{:S(2)}) collective-permute-start(s16[17,32,256]{2,1,0:T(8,128)(2,1)S(1)} %slice.65), channel_id=1, source_target_pairs={{0,1},{1,0},{2,3},{3,2},{4,5},{5,4},{6,7},{7,6},{8,9},{9,8},{10,11... | collective-permute-start | bytes 835592 | tf_op jit(solution)/shard_map/ppermute | solution.py:288
  185.2 6.7 %copy-start.8 = (s16[33,32,256]{2,1,0:T(8,128)(2,1)}, s16[33,32,256]{2,1,0:T(8,128)(2,1)S(1)}, u32[]{:S(2)}) copy-start(s16[33,32,256]{2,1,0:T(8,128)(2,1)S(1)} %collective-permute-done.28.refs_2_) | copy-start | bytes 1622020
  185.2 6.6 %collective-permute-start.30 = (s16[17,32,256]{2,1,0:T(8,128)(2,1)S(1)}, s16[17,32,256]{2,1,0:T(8,128)(2,1)S(1)}, u32[]{:S(2)}, u32[]{:S(2)}) collective-permute-start(s16[17,32,256]{2,1,0:T(8,128)(2,1)S(1)} %pad_add_fusion), channel_id=1, source_target_pairs={{0,2},{1,3},{2,0},{3,1},{4,6},{5,7},{6,4},{7,5},{8,10},{9,11},{10,... | collective-permute-start | bytes 835592 | tf_op jit(solution)/shard_map/ppermute | solution.py:288
  (3 other events, 2.1 us)

commit v3 on v2

--- a/solution.py
+++ b/solution.py
@@ -15,6 +15,7 @@
 UNROLL = 32
 PAD = 8
 STEPS = 8.0
+LATE = 1
 ROOM = 32768.0 / 32000.0
 SMALL = 1e-30
 VMEM_LIMIT = 56 * 1024 * 1024
@@ -78,30 +79,34 @@
             copies.append(pltpu.make_async_copy(source, target, in_sem.at[part, index]))
         return copies
 
-    starts = (0, REACH, REACH + core)
-    counts = (REACH, core, REACH)
-    data_copies = [
-        pltpu.make_async_copy(
-            data_sources[i], measured.at[pl.ds(starts[i], counts[i])], data_sem.at[i]
+    data_copies = []
+    for step in range(depths // GROUP):
+        k = step * GROUP
+        which, first = (0, 0) if k < REACH else (1, k - REACH) if k < REACH + core else (2, 0)
+        data_copies.append(
+            pltpu.make_async_copy(
+                data_sources[which].at[pl.ds(first, GROUP)],
+                measured.at[pl.ds(k, GROUP)],
+                data_sem.at[step],
+            )
         )
-        for i in range(3)
-    ]
     for index in range(len(pieces)):
         for copy in block_copies(index):
             copy.start()
-    for copy in data_copies:
-        copy.start()
 
     for index, (bits, offset, count) in enumerate(pieces):
         for copy in block_copies(index):
             copy.wait()
+        if index == LATE:
+            for copy in data_copies:
+                copy.start()
         for y in range(bits * rows_out + offset, bits * rows_out + offset + count):
             for h, part in enumerate(halves(dot32(z_band[...], block[y]))):
                 by_plane[h, pl.ds(y, depths, stride=plane_rows), :] = part
-    for copy in data_copies:
-        copy.wait()
 
     def planes(step, carry):
+        arriving = measured.at[pl.ds(step * GROUP, GROUP)]
+        pltpu.make_async_copy(arriving, arriving, data_sem.at[step]).wait()
         passed = []
         for g in range(GROUP):
             start = pl.multiple_of((step * GROUP + g) * plane_rows, PAD)
@@ -171,7 +176,7 @@
             pltpu.VMEM((pieces_out, rows_out + 1, core, cols), jnp.int16),
             pltpu.VMEM((rows_out, cols), jnp.float32),
             pltpu.SemaphoreType.DMA((3, len(pieces))),
-            pltpu.SemaphoreType.DMA((3,)),
+            pltpu.SemaphoreType.DMA((depths // GROUP,)),
             pltpu.SemaphoreType.DMA((pieces_out,)),
         ],
         compiler_params=pltpu.CompilerParams(vmem_limit_bytes=VMEM_LIMIT),
@@ -217,44 +222,46 @@
 
 def gather_kernel(pieces, rows_piece, core, rows, cols, *refs):
     n = len(pieces)
-    view_ref, codes, out, planes, sem = refs[0], refs[1 : n + 1], *refs[n + 1 :]
+    view_ref, codes = refs[0], refs[1 : n + 1]
+    out, planes, sem = refs[-3:]
     plane_rows = rows + PAD
-    for code, (bits, offset, count) in zip(codes, pieces):
-        base = (view_ref[0] ^ bits) * rows_piece + offset
+    copies = []
+    for index, (code, (bits, offset, count)) in enumerate(zip(codes, pieces)):
+        base = pl.multiple_of((view_ref[0] ^ bits) * rows_piece + offset, PAD)
         scale = scale_of(code[count][0:rows_piece])
         for y in range(count):
             value = code[y].astype(jnp.float32) * scale[offset + y : offset + y + 1]
             for h, part in enumerate(halves(value)):
                 planes[h, pl.ds(base + y, core, stride=plane_rows), :] = part
-    copies = [
-        pltpu.make_async_copy(
-            planes.at[h, pl.ds(z * plane_rows, rows)],
-            out.at[z, :, pl.ds(h * LANES, LANES)],
-            sem.at[h, z],
-        )
-        for z in range(core)
-        for h in range(cols // LANES)
-    ]
-    for copy in copies:
-        copy.start()
+        for h in range(cols // LANES):
+            for z in range(core):
+                copy = pltpu.make_async_copy(
+                    planes.at[h, pl.ds(pl.multiple_of(z * plane_rows + base, PAD), count)],
+                    out.at[z, pl.ds(base, count), pl.ds(h * LANES, LANES)],
+                    sem.at[index, h, z],
+                )
+                copy.start()
+                copies.append(copy)
     for copy in copies:
         copy.wait()
 
 
-def gather(view_id, pieces, codes, rows, views):
+def gather(view_id, pieces, codes, rows, views, tile=None):
     core, cols = codes[0].shape[1:]
+    given = [] if tile is None else [tile]
     return pl.pallas_call(
         functools.partial(gather_kernel, pieces, rows // views, core, rows, cols),
         out_shape=jax.ShapeDtypeStruct((core, rows, cols), jnp.float32),
-        in_specs=[SMEM] + [VMEM] * len(codes),
+        in_specs=[SMEM] + [VMEM] * len(codes) + [ANY] * len(given),
         out_specs=ANY,
         scratch_shapes=[
             pltpu.VMEM((cols // LANES, core * (rows + PAD), LANES), jnp.float32),
-            pltpu.SemaphoreType.DMA((cols // LANES, core)),
+            pltpu.SemaphoreType.DMA((len(codes), cols // LANES, core)),
         ],
+        input_output_aliases={} if tile is None else {1 + len(codes): 0},
         compiler_params=pltpu.CompilerParams(vmem_limit_bytes=VMEM_LIMIT),
         name="gather",
-    )(view_id, *codes)
+    )(view_id, *codes, *given)
 
 
 def band(taps, row_index, col_index):
@@ -293,23 +300,30 @@
     else:
         pieces = tuple((bits, 0, rows_piece) for bits in range(views))
 
-    def share(x):
+    def share(x, send=None):
+        send = send or (lambda y: y)
+        sent = [send(x)]
         if views != 4:
-            return [x] + [from_view(x, bits) for bits in range(1, views)]
+            every = [x] + [from_view(x, bits) for bits in range(1, views)]
+            return every, sent + [send(y) for y in every[1:]]
         one, two = from_view(x, 1), from_view(x, 2)
+        sent += [send(one), send(two)]
         first, second = one[:part], two[part:]
         if x.shape[0] > rows_piece:
             first = jnp.concatenate([first, one[rows_piece:]], axis=0)
-        return [x, one, two, from_view(first, 2), from_view(second, 1)]
+        rest = [from_view(first, 2), from_view(second, 1)]
+        return [x, one, two, *rest], sent + [send(y) for y in rest]
 
     def own_rows(volume):
         return lax.dynamic_slice_in_dim(volume, view_id * rows_piece, rows_piece, axis=1)
 
     first_piece = jnp.transpose(own_rows(estimate).astype(half), (1, 0, 2))
     first_piece, volume, data = lax.optimization_barrier((first_piece, estimate, views_data[0]))
-    far_blocks = share(far(first_piece))
+    far_piece = far(first_piece)
     bottom, top = data[:REACH], data[core - REACH :]
     to_far, to_near = jnp.where(even, bottom, top), jnp.where(even, top, bottom)
+    far_piece, to_far, psf_bank = lax.optimization_barrier((far_piece, to_far, psf_bank))
+    far_blocks, _ = share(far_piece)
     measured = (far(to_far), data, near(to_near))
     start = jnp.transpose(volume.astype(half), (1, 0, 2))
     blocks = [far_blocks, [start], [near(start)]]
@@ -356,11 +370,16 @@
         arrived = [codes[0]] + [from_view(codes[bits], bits) for bits in range(1, views)]
         if it + 1 < ITERS:
             mine, rounded = update(arrived, mine, False)
-            own = share(rounded)
-            blocks = [[far(x) for x in own], own, [near(x) for x in own]]
+            own, fars = share(rounded, far)
+            blocks = [fars, own, [near(x) for x in own]]
         else:
             (code,) = update(arrived, mine, True)
-    return gather(here, pieces, share(code), rows, views)
+    codes, _ = share(code)
+    early = min(3, len(codes))
+    tile = gather(here, pieces[:early], codes[:early], rows, views)
+    if early == len(codes):
+        return tile
+    return gather(here, pieces[early:], codes[early:], rows, views, tile)
 
 
 def solution(mesh):

time: 198 us -> 194 us (0.980)
  waiting for transfers between devices: 92.8 us -> 83.2 us
  Pallas kernels: 39.6 us -> 41.8 us
    ppermute x18, waiting for transfers between devices: 86 us -> 76.7 us  [from_view(): return lax.ppermute(x, 'view', [(v, v ^ bits) for v in range(views)])]
    pallas_call x1 -> x2, Pallas kernels: 5 us -> 8.33 us  [gather(): pl.pallas_call(functools.partial(gather_kernel, pieces, rows // views, co...]
  transfers between devices with their start and end apart: 32 -> 32, of which waited for: 18 -> 15; matrix products, arithmetic and copies ran while one was open for 7% -> 9% of each run, Pallas kernels for 0% -> 3%
where the time goes in v3:
time: 194 us; the launch traced here: 193 us
  waiting for transfers between devices  83.2 us (43%)
  Pallas kernels  41.8 us (22%)
  starting transfers between devices  40.5 us (21%)
  local copies, waits for them, and re-layouts  18.4 us (9%)
  other arithmetic  6.95 us (4%)
  between operations  2.47 us (1%)
    ppermute x18, waiting for transfers between devices, from_view(): return lax.ppermute(x, 'view', [(v, v ^ bits) for v in range(views)])  76.7 us
    pallas_call x2, Pallas kernels, sweep(): pl.pallas_call(functools.partial(sweep_kernel, (pieces, shares, pieces_ou...  26.2 us
    ppermute x18, starting transfers between devices, from_view(): return lax.ppermute(x, 'view', [(v, v ^ bits) for v in range(views)])  21.2 us
    ppermute x7, starting transfers between devices, far(): return lax.ppermute(x, 'tile', far_pairs)  14.5 us
    pallas_call x2, Pallas kernels, gather(): pl.pallas_call(functools.partial(gather_kernel, pieces, rows // views, co...  8.33 us
    pallas_call x2, Pallas kernels, update(): pl.pallas_call(functools.partial(update_kernel, last, views), out_shape=s...  7.29 us
    unnamed x71, local copies, waits for them, and re-layouts  6.73 us
    ppermute x7, waiting for transfers between devices, far(): return lax.ppermute(x, 'tile', far_pairs)  6.5 us
  transfers between devices with their start and end apart: 32, of which 15 were waited for; matrix products, arithmetic and copies ran while one was open for 9% of the time, Pallas kernels for 3%

profile of v3, /device:TPU:8, one launch (start us, length us, event | category | flops | bytes accessed | tf_op | source)
XLA Modules:
  0.0 193.4 jit_solution(3065814876443848380)
XLA Ops:
  0.0 1.4 constant_dynamic-slice_fusion
  1.5 1.1 copy.32
  2.6 1.9 collective-permute-start
  4.5 1.4 broadcast_select_fusion
  5.9 1.7 collective-permute-start.7
  7.6 2.2 %copy.31 = bf16[32,128,256]{2,0,1:T(8,128)(2,1)S(1)} copy(f32[32,128,256]{2,1,0:T(8,128)S(1)} %copy-done.1) | data formatting | bytes 6291456 | tf_op jit(solution)/shard_map/optimization_barrier | solution.py:321
  9.9 1.6 collective-permute-start.5
  14.7 1.6 collective-permute-start.2
  16.3 1.5 collective-permute-start.1
  17.9 2.1 %collective-permute-start.6 = (bf16[16,128,256]{2,1,0:T(8,128)(2,1)}, bf16[16,128,256]{2,1,0:T(8,128)(2,1)}, u32[]{:S(2)}, u32[]{:S(2)}) collective-permute-start(bf16[16,128,256]{2,1,0:T(8,128)(2,1)} %get-tuple-element.27), channel_id=1, source_target_pairs={{4,8},{8,4},{12,16},{16,12},{20,24},{24,20},{5,9},{9,5},{13,17},{1... | collective-permute-start | bytes 3145736 | tf_op jit(solution)/shard_map/ppermute | solution.py:289
  20.1 0.8 select_reduce_fusion.2
  20.9 0.9 select_reduce_fusion.1
  21.7 0.9 select_reduce_fusion.refs_17_.refs_25_
  22.7 6.3 %collective-permute-done.2.refs_4_ = bf16[32,32,256]{2,1,0:T(8,128)(2,1)S(1)} collective-permute-done((bf16[32,32,256]{2,1,0:T(8,128)(2,1)}, bf16[32,32,256]{2,1,0:T(8,128)(2,1)S(1)}, u32[]{:S(2)}, u32[]{:S(2)}) %collective-permute-start.2) | collective-permute-done | bytes 524320 | tf_op jit(solution)/shard_map/ppermute | solution.py:295
  28.9 0.8 copy-done.11
  29.7 0.7 slice.60
  30.5 1.5 collective-permute-start.4
  31.9 0.8 copy-done.12
  32.7 0.7 slice.59
  33.5 1.5 collective-permute-start.3
  35.0 0.7 select_reduce_fusion.3
  35.7 0.9 copy.16
  36.6 0.7 copy.17.refs_14_.refs_22_
  37.3 0.8 copy.18.refs_16_.refs_24_
  38.1 1.3 select_convert_fusion.refs_12_.refs_20_
  39.4 1.7 collective-permute-done.3.refs_5_
  41.1 13.3 %sweep.2 = (s16[33,32,256]{2,1,0:T(8,128)(2,1)}, s16[33,32,256]{2,1,0:T(8,128)(2,1)}, s16[33,32,256]{2,1,0:T(8,128)(2,1)}, s16[33,32,256]{2,1,0:T(8,128)(2,1)}) custom-call(s32[1]{0:T(128)} %bitcast.refs_0_, s32[64]{0:T(128)} %get-tuple-element.43.refs_1_, bf16[32,32,256]{2,1,0:T(8,128)(2,1)} %collective-permute-done.refs_2_, ...), custom_call_target="tpu_custom_call" | custom-call | tf_op jit(solution)/shard_map/sweep/pallas_call | solution.py:166
  55.1 1.5 collective-permute-start.9
  56.6 1.4 collective-permute-start.10
  58.0 2.4 %copy.19 = f32[32,128,256]{2,0,1:T(8,128)S(1)} copy(f32[32,128,256]{2,1,0:T(8,128)S(1)} %copy-done.2) | data formatting | bytes 8388608 | tf_op jit(solution)/shard_map/optimization_barrier | solution.py:368
  60.4 1.1 dynamic-slice_bitcast_fusion.refs_4_
  61.5 8.4 %collective-permute-done.8.refs_1_ = s16[33,32,256]{2,1,0:T(8,128)(2,1)S(1)} collective-permute-done((s16[33,32,256]{2,1,0:T(8,128)(2,1)}, s16[33,32,256]{2,1,0:T(8,128)(2,1)S(1)}, u32[]{:S(2)}, u32[]{:S(2)}) %collective-permute-start.8) | collective-permute-done | bytes 540704 | tf_op jit(solution)/shard_map/ppermute | solution.py:295
  69.9 8.1 %collective-permute-done.9.refs_2_ = s16[33,32,256]{2,1,0:T(8,128)(2,1)S(1)} collective-permute-done((s16[33,32,256]{2,1,0:T(8,128)(2,1)}, s16[33,32,256]{2,1,0:T(8,128)(2,1)S(1)}, u32[]{:S(2)}, u32[]{:S(2)}) %collective-permute-start.9) | collective-permute-done | bytes 540704 | tf_op jit(solution)/shard_map/ppermute | solution.py:295
  78.1 1.5 collective-permute-done.10.refs_3_
  79.6 0.8 copy-done.16
  80.4 3.7 %update.2 = (f32[32,32,256]{2,1,0:T(8,128)}, bf16[32,32,256]{2,1,0:T(8,128)(2,1)}) custom-call(s16[33,32,256]{2,1,0:T(8,128)(2,1)} %get-tuple-element.30.refs_0_, s16[33,32,256]{2,1,0:T(8,128)(2,1)} %copy-done.13, s16[33,32,256]{2,1,0:T(8,128)(2,1)} %copy-done.14, s16[33,32,256]{2,1,0:T(8,128)(2,1)} %copy-done.16, ...), custom_call_target="tpu_custom_call" | custom-call | tf_op jit(solution)/shard_map/update/pallas_call | solution.py:213
  84.1 1.6 collective-permute-start.14
  85.7 1.5 collective-permute-start.12
  87.2 2.0 %collective-permute-start.11 = (bf16[32,32,256]{2,1,0:T(8,128)(2,1)}, bf16[32,32,256]{2,1,0:T(8,128)(2,1)S(1)}, u32[]{:S(2)}, u32[]{:S(2)}) collective-permute-start(bf16[32,32,256]{2,1,0:T(8,128)(2,1)} %get-tuple-element.35.refs_7_), channel_id=1, source_target_pairs={{4,8},{8,4},{12,16},{16,12},{20,24},{24,20},{5,9},{9,5},{13,17},{1... | collective-permute-start | bytes 1572872 | tf_op jit(solution)/shard_map/ppermute | solution.py:289
  89.2 6.1 %collective-permute-done.14.refs_9_ = bf16[32,32,256]{2,1,0:T(8,128)(2,1)S(1)} collective-permute-done((bf16[32,32,256]{2,1,0:T(8,128)(2,1)}, bf16[32,32,256]{2,1,0:T(8,128)(2,1)S(1)}, u32[]{:S(2)}, u32[]{:S(2)}) %collective-permute-start.14) | collective-permute-done | bytes 524320 | tf_op jit(solution)/shard_map/ppermute | solution.py:295
  96.0 2.2 %collective-permute-start.15 = (bf16[32,32,256]{2,1,0:T(8,128)(2,1)S(1)}, bf16[32,32,256]{2,1,0:T(8,128)(2,1)S(1)}, u32[]{:S(2)}, u32[]{:S(2)}) collective-permute-start(bf16[32,32,256]{2,1,0:T(8,128)(2,1)S(1)} %collective-permute-done.14.refs_9_), channel_id=1, source_target_pairs={{4,8},{8,4},{12,16},{16,12},{20,24},{24,20},{5,9},{9,5},{13,17},{1... | collective-permute-start | bytes 1572872 | tf_op jit(solution)/shard_map/ppermute | solution.py:289
  98.2 2.5 %collective-permute-done.12.refs_8_ = bf16[32,32,256]{2,1,0:T(8,128)(2,1)S(1)} collective-permute-done((bf16[32,32,256]{2,1,0:T(8,128)(2,1)}, bf16[32,32,256]{2,1,0:T(8,128)(2,1)S(1)}, u32[]{:S(2)}, u32[]{:S(2)}) %collective-permute-start.12) | collective-permute-done | bytes 524320 | tf_op jit(solution)/shard_map/ppermute | solution.py:295
  101.2 4.7 %collective-permute-done.18.refs_11_ = bf16[16,32,256]{2,1,0:T(8,128)(2,1)S(1)} collective-permute-done((bf16[16,32,256]{2,1,0:T(8,128)(2,1)S(1)}, bf16[16,32,256]{2,1,0:T(8,128)(2,1)S(1)}, u32[]{:S(2)}, u32[]{:S(2)}) %collective-permute-start.18) | collective-permute-done | bytes 262176 | tf_op jit(solution)/shard_map/ppermute | solution.py:295
  105.9 1.9 collective-permute-start.13
  107.8 1.7 collective-permute-done.16.refs_10_
  109.6 2.2 %collective-permute-start.19 = (bf16[16,32,256]{2,1,0:T(8,128)(2,1)S(1)}, bf16[16,32,256]{2,1,0:T(8,128)(2,1)S(1)}, u32[]{:S(2)}, u32[]{:S(2)}) collective-permute-start(bf16[16,32,256]{2,1,0:T(8,128)(2,1)S(1)} %collective-permute-done.18.refs_11_), channel_id=1, source_target_pairs={{4,8},{8,4},{12,16},{16,12},{20,24},{24,20},{5,9},{9,5},{13,17},{1... | collective-permute-start | bytes 786440 | tf_op jit(solution)/shard_map/ppermute | solution.py:289
  111.8 1.4 collective-permute-start.23
  113.2 2.3 %collective-permute-start.17 = (bf16[16,32,256]{2,1,0:T(8,128)(2,1)S(1)}, bf16[16,32,256]{2,1,0:T(8,128)(2,1)S(1)}, u32[]{:S(2)}, u32[]{:S(2)}) collective-permute-start(bf16[16,32,256]{2,1,0:T(8,128)(2,1)S(1)} %collective-permute-done.16.refs_10_), channel_id=1, source_target_pairs={{4,8},{8,4},{12,16},{16,12},{20,24},{24,20},{5,9},{9,5},{13,17},{1... | collective-permute-start | bytes 786440 | tf_op jit(solution)/shard_map/ppermute | solution.py:289
  115.5 0.9 collective-permute-done.13.refs_3_
  116.4 2.8 %collective-permute-done.19.refs_6_ = bf16[16,32,256]{2,1,0:T(8,128)(2,1)S(1)} collective-permute-done((bf16[16,32,256]{2,1,0:T(8,128)(2,1)S(1)}, bf16[16,32,256]{2,1,0:T(8,128)(2,1)S(1)}, u32[]{:S(2)}, u32[]{:S(2)}) %collective-permute-start.19) | collective-permute-done | bytes 262176 | tf_op jit(solution)/shard_map/ppermute | solution.py:289
  119.2 2.8 %collective-permute-done.17.refs_5_ = bf16[16,32,256]{2,1,0:T(8,128)(2,1)S(1)} collective-permute-done((bf16[16,32,256]{2,1,0:T(8,128)(2,1)S(1)}, bf16[16,32,256]{2,1,0:T(8,128)(2,1)S(1)}, u32[]{:S(2)}, u32[]{:S(2)}) %collective-permute-start.17) | collective-permute-done | bytes 262176 | tf_op jit(solution)/shard_map/ppermute | solution.py:289
  122.8 12.9 %sweep.3 = (s16[33,32,256]{2,1,0:T(8,128)(2,1)}, s16[33,32,256]{2,1,0:T(8,128)(2,1)}, s16[33,32,256]{2,1,0:T(8,128)(2,1)}, s16[33,32,256]{2,1,0:T(8,128)(2,1)}) custom-call(s32[1]{0:T(128)} %bitcast.refs_0_, s32[64]{0:T(128)} %get-tuple-element.43.refs_1_, bf16[32,32,256]{2,1,0:T(8,128)(2,1)} %copy-done.21, bf16[32,32,256]{2,1,0:T(8,128)(2,1)} %copy-done.25, ...), custom_call_target="tpu_custom_call" | custom-call | tf_op jit(solution)/shard_map/sweep/pallas_call | solution.py:166
  135.7 1.5 collective-permute-start.25
  137.8 1.5 collective-permute-start.27
  139.3 11.8 %collective-permute-done.25.refs_1_ = s16[33,32,256]{2,1,0:T(8,128)(2,1)S(1)} collective-permute-done((s16[33,32,256]{2,1,0:T(8,128)(2,1)}, s16[33,32,256]{2,1,0:T(8,128)(2,1)S(1)}, u32[]{:S(2)}, u32[]{:S(2)}) %collective-permute-start.25) | collective-permute-done | bytes 540704 | tf_op jit(solution)/shard_map/ppermute | solution.py:295
  151.1 12.0 %collective-permute-done.26.refs_2_ = s16[33,32,256]{2,1,0:T(8,128)(2,1)S(1)} collective-permute-done((s16[33,32,256]{2,1,0:T(8,128)(2,1)}, s16[33,32,256]{2,1,0:T(8,128)(2,1)S(1)}, u32[]{:S(2)}, u32[]{:S(2)}) %collective-permute-start.26) | collective-permute-done | bytes 540704 | tf_op jit(solution)/shard_map/ppermute | solution.py:295
  163.1 0.8 copy-done.17
  164.1 3.6 %update.3.refs_1_ = s16[33,32,256]{2,1,0:T(8,128)(2,1)} custom-call(s16[33,32,256]{2,1,0:T(8,128)(2,1)} %get-tuple-element.36.refs_0_, s16[33,32,256]{2,1,0:T(8,128)(2,1)} %copy-done.15, s16[33,32,256]{2,1,0:T(8,128)(2,1)} %copy-done.17, s16[33,32,256]{2,1,0:T(8,128)(2,1)} %copy-done.18, f32[32,32,256]{2,1,0:T(8,128)} %get-tuple-element.40.refs_4_), custom_call_target="tpu_custom_call" | custom-call | tf_op jit(solution)/shard_map/update/pallas_call | solution.py:213
  168.2 1.0 collective-permute-start.28
  169.2 11.8 %collective-permute-done.30.refs_3_ = s16[33,32,256]{2,1,0:T(8,128)(2,1)S(1)} collective-permute-done((s16[33,32,256]{2,1,0:T(8,128)(2,1)}, s16[33,32,256]{2,1,0:T(8,128)(2,1)S(1)}, u32[]{:S(2)}, u32[]{:S(2)}) %collective-permute-start.30) | collective-permute-done | bytes 540704 | tf_op jit(solution)/shard_map/ppermute | solution.py:295
  181.6 1.8 collective-permute-start.29
  183.4 4.9 %gather.2.refs_3_ = f32[32,128,256]{2,1,0:T(8,128)} custom-call(s32[1]{0:T(128)} %bitcast.refs_0_, s16[33,32,256]{2,1,0:T(8,128)(2,1)} %update.3.refs_1_, s16[33,32,256]{2,1,0:T(8,128)(2,1)} %copy-done.8, s16[33,32,256]{2,1,0:T(8,128)(2,1)} %copy-done.7), custom_call_target="tpu_custom_call" | custom-call | tf_op jit(solution)/shard_map/gather/pallas_call | solution.py:252
  189.1 0.7 copy-done.27
  189.8 3.4 %gather.3 = f32[32,128,256]{2,1,0:T(8,128)} custom-call(s32[1]{0:T(128)} %bitcast.refs_0_, s16[17,32,256]{2,1,0:T(8,128)(2,1)} %copy-done.27, s16[17,32,256]{2,1,0:T(8,128)(2,1)} %copy-done.26, f32[32,128,256]{2,1,0:T(8,128)} %gather.2.refs_3_), custom_call_target="tpu_custom_call", output_to_operand_aliasing={{}: (3, {})} | custom-call | tf_op jit(solution)/shard_map/gather/pallas_call | solution.py:252
  (112 shorter events, 6.7 us)
Async XLA Ops:
  0.0 17.8 %copy-start = (bf16[8,3,33]{2,0,1:T(8,128)(2,1)S(1)}, bf16[8,3,33]{2,0,1:T(8,128)(2,1)}, u32[]{:S(2)}) copy-start(bf16[8,3,33]{2,0,1:T(8,128)(2,1)} %param.7) | copy-start | bytes 4756
  0.0 4.5 %copy-start.3 = (bf16[1,32,128,256]{3,2,1,0:T(8,128)(2,1)S(1)}, bf16[1,32,128,256]{3,2,1,0:T(8,128)(2,1)}, u32[]{:S(2)}) copy-start(bf16[1,32,128,256]{3,2,1,0:T(8,128)(2,1)} %param.6) | copy-start | bytes 6291460
  2.6 12.2 %collective-permute-start = (bf16[32,32,256]{2,1,0:T(8,128)(2,1)}, bf16[32,32,256]{2,1,0:T(8,128)(2,1)}, u32[]{:S(2)}, u32[]{:S(2)}) collective-permute-start(bf16[32,32,256]{2,1,0:T(8,128)(2,1)} %bitcast.29), channel_id=1, source_target_pairs={{4,8},{8,4},{12,16},{16,12},{20,24},{24,20},{5,9},{9,5},{13,17},{1... | collective-permute-start | bytes 1572872 | tf_op jit(solution)/shard_map/ppermute | solution.py:289
  4.5 3.1 %copy-start.1 = (f32[32,128,256]{2,1,0:T(8,128)S(1)}, f32[32,128,256]{2,1,0:T(8,128)}, u32[]{:S(2)}) copy-start(f32[32,128,256]{2,1,0:T(8,128)} %param.5) | copy-start | bytes 12582916
  5.9 6.2 %copy-start.34 = (s32[1,2]{1,0:T(1,128)S(1)}, s32[1,2]{1,0:T(1,128)}, u32[]{:S(2)}) copy-start(s32[1,2]{1,0:T(1,128)} %param.9) | copy-start | bytes 28
  5.9 33.4 %collective-permute-start.7 = (bf16[16,128,256]{2,1,0:T(8,128)(2,1)}, bf16[16,128,256]{2,1,0:T(8,128)(2,1)S(1)}, u32[]{:S(2)}, u32[]{:S(2)}) collective-permute-start(bf16[16,128,256]{2,1,0:T(8,128)(2,1)} %get-tuple-element.45), channel_id=1, source_target_pairs={{0,4},{4,0},{8,12},{12,8},{16,20},{20,16},{24,28},{28,24},{1,5},{5... | collective-permute-start | bytes 3145736 | tf_op jit(solution)/shard_map/ppermute | solution.py:292
  9.9 31.2 %copy-start.4 = (bf16[32,128,256]{2,0,1:T(8,128)(2,1)}, bf16[32,128,256]{2,0,1:T(8,128)(2,1)S(1)}, u32[]{:S(2)}) copy-start(bf16[32,128,256]{2,0,1:T(8,128)(2,1)S(1)} %copy.31) | copy-start | bytes 6291460
  9.9 31.2 %collective-permute-start.5 = (bf16[128,32,256]{2,1,0:T(8,128)(2,1)S(1)}, bf16[128,32,256]{2,1,0:T(8,128)(2,1)}, u32[]{:S(2)}, u32[]{:S(2)}) collective-permute-start(bf16[128,32,256]{2,1,0:T(8,128)(2,1)S(1)} %bitcast.35), channel_id=1, source_target_pairs={{0,4},{4,0},{8,12},{12,8},{16,20},{20,16},{24,28},{28,24},{1,5},{5... | collective-permute-start | bytes 6291464 | tf_op jit(solution)/shard_map/ppermute | solution.py:292
  14.7 14.2 %collective-permute-start.2 = (bf16[32,32,256]{2,1,0:T(8,128)(2,1)}, bf16[32,32,256]{2,1,0:T(8,128)(2,1)S(1)}, u32[]{:S(2)}, u32[]{:S(2)}) collective-permute-start(bf16[32,32,256]{2,1,0:T(8,128)(2,1)} %collective-permute-done.refs_2_), channel_id=1, source_target_pairs={{0,2},{1,3},{2,0},{3,1},{4,6},{5,7},{6,4},{7,5},{8,10},{9,11},{10,... | collective-permute-start | bytes 1572872 | tf_op jit(solution)/shard_map/ppermute | solution.py:295
  16.3 15.6 %collective-permute-start.1 = (bf16[32,32,256]{2,1,0:T(8,128)(2,1)}, bf16[32,32,256]{2,1,0:T(8,128)(2,1)S(1)}, u32[]{:S(2)}, u32[]{:S(2)}) collective-permute-start(bf16[32,32,256]{2,1,0:T(8,128)(2,1)} %collective-permute-done.refs_2_), channel_id=1, source_target_pairs={{0,1},{1,0},{2,3},{3,2},{4,5},{5,4},{6,7},{7,6},{8,9},{9,8},{10,11... | collective-permute-start | bytes 1572872 | tf_op jit(solution)/shard_map/ppermute | solution.py:295
  17.9 23.1 %collective-permute-start.6 = (bf16[16,128,256]{2,1,0:T(8,128)(2,1)}, bf16[16,128,256]{2,1,0:T(8,128)(2,1)}, u32[]{:S(2)}, u32[]{:S(2)}) collective-permute-start(bf16[16,128,256]{2,1,0:T(8,128)(2,1)} %get-tuple-element.27), channel_id=1, source_target_pairs={{4,8},{8,4},{12,16},{16,12},{20,24},{24,20},{5,9},{9,5},{13,17},{1... | collective-permute-start | bytes 3145736 | tf_op jit(solution)/shard_map/ppermute | solution.py:289
  22.7 18.4 %copy-start.6 = (bf16[256,256]{1,0:T(8,128)(2,1)}, bf16[256,256]{1,0:T(8,128)(2,1)S(1)}, u32[]{:S(2)}) copy-start(bf16[256,256]{1,0:T(8,128)(2,1)S(1)} %select_reduce_fusion.refs_17_.refs_25_) | copy-start | bytes 393220
  28.9 0.8 copy-start.11
  30.5 8.9 %collective-permute-start.4 = (bf16[16,32,256]{2,1,0:T(8,128)(2,1)}, bf16[16,32,256]{2,1,0:T(8,128)(2,1)}, u32[]{:S(2)}, u32[]{:S(2)}) collective-permute-start(bf16[16,32,256]{2,1,0:T(8,128)(2,1)} %slice.60), channel_id=1, source_target_pairs={{0,1},{1,0},{2,3},{3,2},{4,5},{5,4},{6,7},{7,6},{8,9},{9,8},{10,11... | collective-permute-start | bytes 786440 | tf_op jit(solution)/shard_map/ppermute | solution.py:295
  31.9 0.8 copy-start.12
  33.5 7.6 %collective-permute-start.3 = (bf16[16,32,256]{2,1,0:T(8,128)(2,1)}, bf16[16,32,256]{2,1,0:T(8,128)(2,1)}, u32[]{:S(2)}, u32[]{:S(2)}) collective-permute-start(bf16[16,32,256]{2,1,0:T(8,128)(2,1)} %slice.59), channel_id=1, source_target_pairs={{0,2},{1,3},{2,0},{3,1},{4,6},{5,7},{6,4},{7,5},{8,10},{9,11},{10,... | collective-permute-start | bytes 786440 | tf_op jit(solution)/shard_map/ppermute | solution.py:295
  36.6 4.5 %copy-start.19 = (bf16[128,128]{0,1:T(8,128)(2,1)}, bf16[128,128]{0,1:T(8,128)(2,1)S(1)}, u32[]{:S(2)}) copy-start(bf16[128,128]{0,1:T(8,128)(2,1)S(1)} %copy.16) | copy-start | bytes 98308
  39.4 1.7 copy-start.5
  41.1 16.9 %copy-start.2 = (f32[32,128,256]{2,1,0:T(8,128)S(1)}, f32[32,128,256]{2,1,0:T(8,128)}, u32[]{:S(2)}) copy-start(f32[32,128,256]{2,1,0:T(8,128)} %param.5) | copy-start | bytes 12582916
  54.5 15.5 %collective-permute-start.8 = (s16[33,32,256]{2,1,0:T(8,128)(2,1)}, s16[33,32,256]{2,1,0:T(8,128)(2,1)S(1)}, u32[]{:S(2)}, u32[]{:S(2)}) collective-permute-start(s16[33,32,256]{2,1,0:T(8,128)(2,1)} %get-tuple-element.31), channel_id=1, source_target_pairs={{0,1},{1,0},{2,3},{3,2},{4,5},{5,4},{6,7},{7,6},{8,9},{9,8},{10,11... | collective-permute-start | bytes 1622024 | tf_op jit(solution)/shard_map/ppermute | solution.py:295
  55.1 23.0 %collective-permute-start.9 = (s16[33,32,256]{2,1,0:T(8,128)(2,1)}, s16[33,32,256]{2,1,0:T(8,128)(2,1)S(1)}, u32[]{:S(2)}, u32[]{:S(2)}) collective-permute-start(s16[33,32,256]{2,1,0:T(8,128)(2,1)} %get-tuple-element.32), channel_id=1, source_target_pairs={{0,2},{1,3},{2,0},{3,1},{4,6},{5,7},{6,4},{7,5},{8,10},{9,11},{10,... | collective-permute-start | bytes 1622024 | tf_op jit(solution)/shard_map/ppermute | solution.py:295
  56.6 23.0 %collective-permute-start.10 = (s16[33,32,256]{2,1,0:T(8,128)(2,1)}, s16[33,32,256]{2,1,0:T(8,128)(2,1)S(1)}, u32[]{:S(2)}, u32[]{:S(2)}) collective-permute-start(s16[33,32,256]{2,1,0:T(8,128)(2,1)} %get-tuple-element.33), channel_id=1, source_target_pairs={{0,3},{1,2},{2,1},{3,0},{4,7},{5,6},{6,5},{7,4},{8,11},{9,10},{10,... | collective-permute-start | bytes 1622024 | tf_op jit(solution)/shard_map/ppermute | solution.py:295
  69.9 9.6 %copy-start.13 = (s16[33,32,256]{2,1,0:T(8,128)(2,1)}, s16[33,32,256]{2,1,0:T(8,128)(2,1)S(1)}, u32[]{:S(2)}) copy-start(s16[33,32,256]{2,1,0:T(8,128)(2,1)S(1)} %collective-permute-done.8.refs_1_) | copy-start | bytes 1622020
  78.1 1.5 copy-start.14
  79.6 0.8 copy-start.16
  84.1 11.3 %collective-permute-start.14 = (bf16[32,32,256]{2,1,0:T(8,128)(2,1)}, bf16[32,32,256]{2,1,0:T(8,128)(2,1)S(1)}, u32[]{:S(2)}, u32[]{:S(2)}) collective-permute-start(bf16[32,32,256]{2,1,0:T(8,128)(2,1)} %get-tuple-element.35.refs_7_), channel_id=1, source_target_pairs={{0,2},{1,3},{2,0},{3,1},{4,6},{5,7},{6,4},{7,5},{8,10},{9,11},{10,... | collective-permute-start | bytes 1572872 | tf_op jit(solution)/shard_map/ppermute | solution.py:295
  85.7 10.3 %collective-permute-start.20 = (bf16[32,32,256]{2,1,0:T(8,128)(2,1)}, bf16[32,32,256]{2,1,0:T(8,128)(2,1)S(1)}, u32[]{:S(2)}, u32[]{:S(2)}) collective-permute-start(bf16[32,32,256]{2,1,0:T(8,128)(2,1)} %get-tuple-element.35.refs_7_), channel_id=1, source_target_pairs={{0,4},{4,0},{8,12},{12,8},{16,20},{20,16},{24,28},{28,24},{1,5},{5... | collective-permute-start | bytes 1572872 | tf_op jit(solution)/shard_map/ppermute | solution.py:292
  85.7 14.9 %collective-permute-start.12 = (bf16[32,32,256]{2,1,0:T(8,128)(2,1)}, bf16[32,32,256]{2,1,0:T(8,128)(2,1)S(1)}, u32[]{:S(2)}, u32[]{:S(2)}) collective-permute-start(bf16[32,32,256]{2,1,0:T(8,128)(2,1)} %get-tuple-element.35.refs_7_), channel_id=1, source_target_pairs={{0,1},{1,0},{2,3},{3,2},{4,5},{5,4},{6,7},{7,6},{8,9},{9,8},{10,11... | collective-permute-start | bytes 1572872 | tf_op jit(solution)/shard_map/ppermute | solution.py:295
  87.2 13.5 %collective-permute-start.11 = (bf16[32,32,256]{2,1,0:T(8,128)(2,1)}, bf16[32,32,256]{2,1,0:T(8,128)(2,1)S(1)}, u32[]{:S(2)}, u32[]{:S(2)}) collective-permute-start(bf16[32,32,256]{2,1,0:T(8,128)(2,1)} %get-tuple-element.35.refs_7_), channel_id=1, source_target_pairs={{4,8},{8,4},{12,16},{16,12},{20,24},{24,20},{5,9},{9,5},{13,17},{1... | collective-permute-start | bytes 1572872 | tf_op jit(solution)/shard_map/ppermute | solution.py:289
  95.4 26.7 %copy-start.9 = (bf16[32,32,256]{2,1,0:T(8,128)(2,1)}, bf16[32,32,256]{2,1,0:T(8,128)(2,1)S(1)}, u32[]{:S(2)}) copy-start(bf16[32,32,256]{2,1,0:T(8,128)(2,1)S(1)} %collective-permute-done.14.refs_9_) | copy-start | bytes 1572868
  95.4 10.5 %collective-permute-start.18 = (bf16[16,32,256]{2,1,0:T(8,128)(2,1)S(1)}, bf16[16,32,256]{2,1,0:T(8,128)(2,1)S(1)}, u32[]{:S(2)}, u32[]{:S(2)}) collective-permute-start(bf16[16,32,256]{2,1,0:T(8,128)(2,1)S(1)} %slice.62), channel_id=1, source_target_pairs={{0,1},{1,0},{2,3},{3,2},{4,5},{5,4},{6,7},{7,6},{8,9},{9,8},{10,11... | collective-permute-start | bytes 786440 | tf_op jit(solution)/shard_map/ppermute | solution.py:295
  96.0 13.6 %collective-permute-start.22 = (bf16[32,32,256]{2,1,0:T(8,128)(2,1)S(1)}, bf16[32,32,256]{2,1,0:T(8,128)(2,1)S(1)}, u32[]{:S(2)}, u32[]{:S(2)}) collective-permute-start(bf16[32,32,256]{2,1,0:T(8,128)(2,1)S(1)} %collective-permute-done.14.refs_9_), channel_id=1, source_target_pairs={{0,4},{4,0},{8,12},{12,8},{16,20},{20,16},{24,28},{28,24},{1,5},{5... | collective-permute-start | bytes 1572872 | tf_op jit(solution)/shard_map/ppermute | solution.py:292
  96.0 26.0 %copy-start.20 = (bf16[32,32,256]{2,1,0:T(8,128)(2,1)}, bf16[32,32,256]{2,1,0:T(8,128)(2,1)S(1)}, u32[]{:S(2)}) copy-start(bf16[32,32,256]{2,1,0:T(8,128)(2,1)S(1)} %collective-permute-done.20.refs_12_) | copy-start | bytes 1572868
  96.0 15.7 %collective-permute-start.15 = (bf16[32,32,256]{2,1,0:T(8,128)(2,1)S(1)}, bf16[32,32,256]{2,1,0:T(8,128)(2,1)S(1)}, u32[]{:S(2)}, u32[]{:S(2)}) collective-permute-start(bf16[32,32,256]{2,1,0:T(8,128)(2,1)S(1)} %collective-permute-done.14.refs_9_), channel_id=1, source_target_pairs={{4,8},{8,4},{12,16},{16,12},{20,24},{24,20},{5,9},{9,5},{13,17},{1... | collective-permute-start | bytes 1572872 | tf_op jit(solution)/shard_map/ppermute | solution.py:289
  100.7 21.4 %copy-start.10 = (bf16[32,32,256]{2,1,0:T(8,128)(2,1)}, bf16[32,32,256]{2,1,0:T(8,128)(2,1)S(1)}, u32[]{:S(2)}) copy-start(bf16[32,32,256]{2,1,0:T(8,128)(2,1)S(1)} %collective-permute-done.12.refs_8_) | copy-start | bytes 1572868
  100.7 12.6 %collective-permute-start.21 = (bf16[32,32,256]{2,1,0:T(8,128)(2,1)S(1)}, bf16[32,32,256]{2,1,0:T(8,128)(2,1)S(1)}, u32[]{:S(2)}, u32[]{:S(2)}) collective-permute-start(bf16[32,32,256]{2,1,0:T(8,128)(2,1)S(1)} %collective-permute-done.12.refs_8_), channel_id=1, source_target_pairs={{0,4},{4,0},{8,12},{12,8},{16,20},{20,16},{24,28},{28,24},{1,5},{5... | collective-permute-start | bytes 1572872 | tf_op jit(solution)/shard_map/ppermute | solution.py:292
  100.7 21.3 %copy-start.21 = (bf16[32,32,256]{2,1,0:T(8,128)(2,1)}, bf16[32,32,256]{2,1,0:T(8,128)(2,1)S(1)}, u32[]{:S(2)}) copy-start(bf16[32,32,256]{2,1,0:T(8,128)(2,1)S(1)} %collective-permute-done.11.refs_2_) | copy-start | bytes 1572868
  100.7 8.8 %collective-permute-start.16 = (bf16[16,32,256]{2,1,0:T(8,128)(2,1)S(1)}, bf16[16,32,256]{2,1,0:T(8,128)(2,1)S(1)}, u32[]{:S(2)}, u32[]{:S(2)}) collective-permute-start(bf16[16,32,256]{2,1,0:T(8,128)(2,1)S(1)} %slice.61), channel_id=1, source_target_pairs={{0,2},{1,3},{2,0},{3,1},{4,6},{5,7},{6,4},{7,5},{8,10},{9,11},{10,... | collective-permute-start | bytes 786440 | tf_op jit(solution)/shard_map/ppermute | solution.py:295
  105.9 16.1 %copy-start.28 = (bf16[16,32,256]{2,1,0:T(8,128)(2,1)}, bf16[16,32,256]{2,1,0:T(8,128)(2,1)S(1)}, u32[]{:S(2)}) copy-start(bf16[16,32,256]{2,1,0:T(8,128)(2,1)S(1)} %collective-permute-done.18.refs_11_) | copy-start | bytes 786436
  105.9 10.5 %collective-permute-start.13 = (bf16[32,32,256]{2,1,0:T(8,128)(2,1)S(1)}, bf16[32,32,256]{2,1,0:T(8,128)(2,1)S(1)}, u32[]{:S(2)}, u32[]{:S(2)}) collective-permute-start(bf16[32,32,256]{2,1,0:T(8,128)(2,1)S(1)} %collective-permute-done.12.refs_8_), channel_id=1, source_target_pairs={{4,8},{8,4},{12,16},{16,12},{20,24},{24,20},{5,9},{9,5},{13,17},{1... | collective-permute-start | bytes 1572872 | tf_op jit(solution)/shard_map/ppermute | solution.py:289
  109.5 12.5 %copy-start.29 = (bf16[16,32,256]{2,1,0:T(8,128)(2,1)}, bf16[16,32,256]{2,1,0:T(8,128)(2,1)S(1)}, u32[]{:S(2)}) copy-start(bf16[16,32,256]{2,1,0:T(8,128)(2,1)S(1)} %collective-permute-done.16.refs_10_) | copy-start | bytes 786436
  109.5 6.9 %collective-permute-start.24 = (bf16[16,32,256]{2,1,0:T(8,128)(2,1)S(1)}, bf16[16,32,256]{2,1,0:T(8,128)(2,1)S(1)}, u32[]{:S(2)}, u32[]{:S(2)}) collective-permute-start(bf16[16,32,256]{2,1,0:T(8,128)(2,1)S(1)} %collective-permute-done.18.refs_11_), channel_id=1, source_target_pairs={{0,4},{4,0},{8,12},{12,8},{16,20},{20,16},{24,28},{28,24},{1,5},{5... | collective-permute-start | bytes 786440 | tf_op jit(solution)/shard_map/ppermute | solution.py:292
  109.6 12.5 %copy-start.22 = (bf16[32,32,256]{2,1,0:T(8,128)(2,1)}, bf16[32,32,256]{2,1,0:T(8,128)(2,1)S(1)}, u32[]{:S(2)}) copy-start(bf16[32,32,256]{2,1,0:T(8,128)(2,1)S(1)} %collective-permute-done.22.refs_14_) | copy-start | bytes 1572868
  109.6 9.6 %collective-permute-start.19 = (bf16[16,32,256]{2,1,0:T(8,128)(2,1)S(1)}, bf16[16,32,256]{2,1,0:T(8,128)(2,1)S(1)}, u32[]{:S(2)}, u32[]{:S(2)}) collective-permute-start(bf16[16,32,256]{2,1,0:T(8,128)(2,1)S(1)} %collective-permute-done.18.refs_11_), channel_id=1, source_target_pairs={{4,8},{8,4},{12,16},{16,12},{20,24},{24,20},{5,9},{9,5},{13,17},{1... | collective-permute-start | bytes 786440 | tf_op jit(solution)/shard_map/ppermute | solution.py:289
  111.8 10.3 %copy-start.23 = (bf16[32,32,256]{2,1,0:T(8,128)(2,1)}, bf16[32,32,256]{2,1,0:T(8,128)(2,1)S(1)}, u32[]{:S(2)}) copy-start(bf16[32,32,256]{2,1,0:T(8,128)(2,1)S(1)} %collective-permute-done.15.refs_4_) | copy-start | bytes 1572868
  111.8 7.4 %collective-permute-start.23 = (bf16[16,32,256]{2,1,0:T(8,128)(2,1)S(1)}, bf16[16,32,256]{2,1,0:T(8,128)(2,1)S(1)}, u32[]{:S(2)}, u32[]{:S(2)}) collective-permute-start(bf16[16,32,256]{2,1,0:T(8,128)(2,1)S(1)} %collective-permute-done.16.refs_10_), channel_id=1, source_target_pairs={{0,4},{4,0},{8,12},{12,8},{16,20},{20,16},{24,28},{28,24},{1,5},{5... | collective-permute-start | bytes 786440 | tf_op jit(solution)/shard_map/ppermute | solution.py:292
  113.2 8.9 %copy-start.24 = (bf16[32,32,256]{2,1,0:T(8,128)(2,1)}, bf16[32,32,256]{2,1,0:T(8,128)(2,1)S(1)}, u32[]{:S(2)}) copy-start(bf16[32,32,256]{2,1,0:T(8,128)(2,1)S(1)} %collective-permute-done.21.refs_13_) | copy-start | bytes 1572868
  113.2 8.8 %collective-permute-start.17 = (bf16[16,32,256]{2,1,0:T(8,128)(2,1)S(1)}, bf16[16,32,256]{2,1,0:T(8,128)(2,1)S(1)}, u32[]{:S(2)}, u32[]{:S(2)}) collective-permute-start(bf16[16,32,256]{2,1,0:T(8,128)(2,1)S(1)} %collective-permute-done.16.refs_10_), channel_id=1, source_target_pairs={{4,8},{8,4},{12,16},{16,12},{20,24},{24,20},{5,9},{9,5},{13,17},{1... | collective-permute-start | bytes 786440 | tf_op jit(solution)/shard_map/ppermute | solution.py:289
  116.4 5.7 %copy-start.25 = (bf16[32,32,256]{2,1,0:T(8,128)(2,1)}, bf16[32,32,256]{2,1,0:T(8,128)(2,1)S(1)}, u32[]{:S(2)}) copy-start(bf16[32,32,256]{2,1,0:T(8,128)(2,1)S(1)} %collective-permute-done.13.refs_3_) | copy-start | bytes 1572868
  116.4 5.7 %copy-start.30 = (bf16[16,32,256]{2,1,0:T(8,128)(2,1)}, bf16[16,32,256]{2,1,0:T(8,128)(2,1)S(1)}, u32[]{:S(2)}) copy-start(bf16[16,32,256]{2,1,0:T(8,128)(2,1)S(1)} %collective-permute-done.24.refs_16_) | copy-start | bytes 786436
  119.2 2.9 %copy-start.31 = (bf16[16,32,256]{2,1,0:T(8,128)(2,1)}, bf16[16,32,256]{2,1,0:T(8,128)(2,1)S(1)}, u32[]{:S(2)}) copy-start(bf16[16,32,256]{2,1,0:T(8,128)(2,1)S(1)} %collective-permute-done.19.refs_6_) | copy-start | bytes 786436
  119.2 2.9 %copy-start.32 = (bf16[16,32,256]{2,1,0:T(8,128)(2,1)}, bf16[16,32,256]{2,1,0:T(8,128)(2,1)S(1)}, u32[]{:S(2)}) copy-start(bf16[16,32,256]{2,1,0:T(8,128)(2,1)S(1)} %collective-permute-done.23.refs_15_) | copy-start | bytes 786436
  135.7 15.4 %collective-permute-start.25 = (s16[33,32,256]{2,1,0:T(8,128)(2,1)}, s16[33,32,256]{2,1,0:T(8,128)(2,1)S(1)}, u32[]{:S(2)}, u32[]{:S(2)}) collective-permute-start(s16[33,32,256]{2,1,0:T(8,128)(2,1)} %get-tuple-element.37), channel_id=1, source_target_pairs={{0,1},{1,0},{2,3},{3,2},{4,5},{5,4},{6,7},{7,6},{8,9},{9,8},{10,11... | collective-permute-start | bytes 1622024 | tf_op jit(solution)/shard_map/ppermute | solution.py:295
  137.3 25.8 %collective-permute-start.26 = (s16[33,32,256]{2,1,0:T(8,128)(2,1)}, s16[33,32,256]{2,1,0:T(8,128)(2,1)S(1)}, u32[]{:S(2)}, u32[]{:S(2)}) collective-permute-start(s16[33,32,256]{2,1,0:T(8,128)(2,1)} %get-tuple-element.38), channel_id=1, source_target_pairs={{0,2},{1,3},{2,0},{3,1},{4,6},{5,7},{6,4},{7,5},{8,10},{9,11},{10,... | collective-permute-start | bytes 1622024 | tf_op jit(solution)/shard_map/ppermute | solution.py:295
  137.8 25.3 %collective-permute-start.27 = (s16[33,32,256]{2,1,0:T(8,128)(2,1)}, s16[33,32,256]{2,1,0:T(8,128)(2,1)S(1)}, u32[]{:S(2)}, u32[]{:S(2)}) collective-permute-start(s16[33,32,256]{2,1,0:T(8,128)(2,1)} %get-tuple-element.39), channel_id=1, source_target_pairs={{0,3},{1,2},{2,1},{3,0},{4,7},{5,6},{6,5},{7,4},{8,11},{9,10},{10,... | collective-permute-start | bytes 1622024 | tf_op jit(solution)/shard_map/ppermute | solution.py:295
  151.1 12.0 %copy-start.15 = (s16[33,32,256]{2,1,0:T(8,128)(2,1)}, s16[33,32,256]{2,1,0:T(8,128)(2,1)S(1)}, u32[]{:S(2)}) copy-start(s16[33,32,256]{2,1,0:T(8,128)(2,1)S(1)} %collective-permute-done.25.refs_1_) | copy-start | bytes 1622020
  163.1 0.8 copy-start.17
  163.1 1.0 copy-start.18
  167.7 13.4 %collective-permute-start.30 = (s16[33,32,256]{2,1,0:T(8,128)(2,1)}, s16[33,32,256]{2,1,0:T(8,128)(2,1)S(1)}, u32[]{:S(2)}, u32[]{:S(2)}) collective-permute-start(s16[33,32,256]{2,1,0:T(8,128)(2,1)} %update.3.refs_1_), channel_id=1, source_target_pairs={{0,2},{1,3},{2,0},{3,1},{4,6},{5,7},{6,4},{7,5},{8,10},{9,11},{10,... | collective-permute-start | bytes 1622024 | tf_op jit(solution)/shard_map/ppermute | solution.py:295
  168.2 13.3 %collective-permute-start.28 = (s16[33,32,256]{2,1,0:T(8,128)(2,1)}, s16[33,32,256]{2,1,0:T(8,128)(2,1)S(1)}, u32[]{:S(2)}, u32[]{:S(2)}) collective-permute-start(s16[33,32,256]{2,1,0:T(8,128)(2,1)} %update.3.refs_1_), channel_id=1, source_target_pairs={{0,1},{1,0},{2,3},{3,2},{4,5},{5,4},{6,7},{7,6},{8,9},{9,8},{10,11... | collective-permute-start | bytes 1622024 | tf_op jit(solution)/shard_map/ppermute | solution.py:295
  181.1 2.4 %copy-start.7 = (s16[33,32,256]{2,1,0:T(8,128)(2,1)}, s16[33,32,256]{2,1,0:T(8,128)(2,1)S(1)}, u32[]{:S(2)}) copy-start(s16[33,32,256]{2,1,0:T(8,128)(2,1)S(1)} %collective-permute-done.30.refs_3_) | copy-start | bytes 1622020
  181.1 7.3 %collective-permute-start.31 = (s16[17,32,256]{2,1,0:T(8,128)(2,1)S(1)}, s16[17,32,256]{2,1,0:T(8,128)(2,1)S(1)}, u32[]{:S(2)}, u32[]{:S(2)}) collective-permute-start(s16[17,32,256]{2,1,0:T(8,128)(2,1)S(1)} %slice.65), channel_id=1, source_target_pairs={{0,1},{1,0},{2,3},{3,2},{4,5},{5,4},{6,7},{7,6},{8,9},{9,8},{10,11... | collective-permute-start | bytes 835592 | tf_op jit(solution)/shard_map/ppermute | solution.py:295
  181.5 1.9 copy-start.8
  181.6 6.8 %collective-permute-start.29 = (s16[17,32,256]{2,1,0:T(8,128)(2,1)S(1)}, s16[17,32,256]{2,1,0:T(8,128)(2,1)S(1)}, u32[]{:S(2)}, u32[]{:S(2)}) collective-permute-start(s16[17,32,256]{2,1,0:T(8,128)(2,1)S(1)} %pad_add_fusion), channel_id=1, source_target_pairs={{0,2},{1,3},{2,0},{3,1},{4,6},{5,7},{6,4},{7,5},{8,10},{9,11},{10,... | collective-permute-start | bytes 835592 | tf_op jit(solution)/shard_map/ppermute | solution.py:295
  (3 other events, 2.1 us)

commit v4 on v3

--- a/solution.py
+++ b/solution.py
@@ -16,10 +16,11 @@
 PAD = 8
 STEPS = 8.0
 LATE = 1
+BLOCKS = 4
 ROOM = 32768.0 / 32000.0
 SMALL = 1e-30
 VMEM_LIMIT = 56 * 1024 * 1024
-ANY = pl.BlockSpec(memory_space=pl.ANY)
+ANY = pl.BlockSpec(memory_space=pltpu.HBM)
 VMEM = pl.BlockSpec(memory_space=pltpu.VMEM)
 SMEM = pl.BlockSpec(memory_space=pltpu.SMEM)
 
@@ -70,7 +71,9 @@
         bits, offset, count = pieces[index]
         copies = []
         for part, given in enumerate(sources):
-            if len(given) == 1:
+            if len(given) == pieces_out and len(pieces) != pieces_out:
+                source = given[bits].at[pl.ds(offset, count)]
+            elif len(given) == 1:
                 first = (view_ref[0] ^ bits) * rows_out + offset
                 source = given[0].at[pl.ds(first, count)]
             else:
@@ -185,23 +188,54 @@
 
 
 def update_kernel(last, views, *refs):
-    codes, mine, outs = refs[:views], refs[views], refs[views + 1 :]
-    count = mine.shape[0]
+    count, kinds = refs[views].shape[0], 1 if last else 2
+    given, outs = refs[: views + 1], refs[views + 1 : views + 1 + kinds]
+    held, made = refs[views + 1 + kinds : 2 * views + 2 + kinds], refs[2 * views + 2 + kinds : -3]
+    slab_sem, in_sem, out_sem = refs[-3:]
+    codes, mine = held[:views], held[views]
+    size = count // BLOCKS
+
+    def loads(c):
+        rows = pl.ds(c * size, size)
+        pairs = enumerate(zip(given, held))
+        return [pltpu.make_async_copy(a.at[rows], b.at[rows], in_sem.at[c, i]) for i, (a, b) in pairs]
+
+    def stores(c):
+        rows = pl.ds(c * size, size + 1 if last and c == BLOCKS - 1 else size)
+        pairs = enumerate(zip(made, outs))
+        return [pltpu.make_async_copy(a.at[rows], b.at[rows], out_sem.at[c, i]) for i, (a, b) in pairs]
+
+    slabs = [
+        pltpu.make_async_copy(given[v].at[count], codes[v].at[count], slab_sem.at[v])
+        for v in range(views)
+    ]
+    for copy in slabs + [copy for c in range(BLOCKS) for copy in loads(c)]:
+        copy.start()
+    for copy in slabs:
+        copy.wait()
     scales = [scale_of(code[count][0:count]) for code in codes]
     powers = []
-    for y in range(count):
-        total = sum(
-            code[y].astype(jnp.float32) * scale[y : y + 1] for code, scale in zip(codes, scales)
-        )
-        value = mine[y] * total * jnp.float32(1.0 / views)
-        if last:
-            outs[0][y], power = encode(value)
-            powers.append(power)
-        else:
-            outs[0][y] = value
-            outs[1][y] = value.astype(jnp.bfloat16)
-    if last:
-        put_powers(outs[0].at[count], jnp.concatenate(powers, axis=0))
+    for c in range(BLOCKS):
+        for copy in loads(c):
+            copy.wait()
+        for y in range(c * size, c * size + size):
+            total = sum(
+                code[y].astype(jnp.float32) * scale[y : y + 1] for code, scale in zip(codes, scales)
+            )
+            value = mine[y] * total * jnp.float32(1.0 / views)
+            if last:
+                made[0][y], power = encode(value)
+                powers.append(power)
+            else:
+                made[0][y] = value
+                made[1][y] = value.astype(jnp.bfloat16)
+        if last and c == BLOCKS - 1:
+            put_powers(made[0].at[count], jnp.concatenate(powers, axis=0))
+        for copy in stores(c):
+            copy.start()
+    for c in range(BLOCKS):
+        for copy in stores(c):
+            copy.wait()
 
 
 def update(codes, mine, last):
@@ -213,8 +247,14 @@
     return pl.pallas_call(
         functools.partial(update_kernel, last, views),
         out_shape=shapes,
-        in_specs=[VMEM] * (views + 1),
-        out_specs=[VMEM] * len(shapes),
+        in_specs=[ANY] * (views + 1),
+        out_specs=[ANY] * len(shapes),
+        scratch_shapes=[pltpu.VMEM(x.shape, x.dtype) for x in (*codes, mine, *shapes)]
+        + [
+            pltpu.SemaphoreType.DMA((views,)),
+            pltpu.SemaphoreType.DMA((BLOCKS, views + 1)),
+            pltpu.SemaphoreType.DMA((BLOCKS, len(shapes))),
+        ],
         compiler_params=pltpu.CompilerParams(vmem_limit_bytes=VMEM_LIMIT),
         name="update",
     )(*codes, mine)
@@ -234,14 +274,13 @@
             for h, part in enumerate(halves(value)):
                 planes[h, pl.ds(base + y, core, stride=plane_rows), :] = part
         for h in range(cols // LANES):
-            for z in range(core):
-                copy = pltpu.make_async_copy(
-                    planes.at[h, pl.ds(pl.multiple_of(z * plane_rows + base, PAD), count)],
-                    out.at[z, pl.ds(base, count), pl.ds(h * LANES, LANES)],
-                    sem.at[index, h, z],
-                )
-                copy.start()
-                copies.append(copy)
+            copy = pltpu.make_async_copy(
+                planes.at[h].reshape(core, plane_rows, LANES).at[:, pl.ds(base, count)],
+                out.at[:, pl.ds(base, count), pl.ds(h * LANES, LANES)],
+                sem.at[index, h],
+            )
+            copy.start()
+            copies.append(copy)
     for copy in copies:
         copy.wait()
 
@@ -256,7 +295,7 @@
         out_specs=ANY,
         scratch_shapes=[
             pltpu.VMEM((cols // LANES, core * (rows + PAD), LANES), jnp.float32),
-            pltpu.SemaphoreType.DMA((len(codes), cols // LANES, core)),
+            pltpu.SemaphoreType.DMA((len(codes), cols // LANES)),
         ],
         input_output_aliases={} if tile is None else {1 + len(codes): 0},
         compiler_params=pltpu.CompilerParams(vmem_limit_bytes=VMEM_LIMIT),
@@ -312,7 +351,7 @@
         if x.shape[0] > rows_piece:
             first = jnp.concatenate([first, one[rows_piece:]], axis=0)
         rest = [from_view(first, 2), from_view(second, 1)]
-        return [x, one, two, *rest], sent + [send(y) for y in rest]
+        return [x, one, two, *rest], sent + [send(jnp.concatenate(rest, axis=0))]
 
     def own_rows(volume):
         return lax.dynamic_slice_in_dim(volume, view_id * rows_piece, rows_piece, axis=1)
@@ -371,7 +410,7 @@
         if it + 1 < ITERS:
             mine, rounded = update(arrived, mine, False)
             own, fars = share(rounded, far)
-            blocks = [fars, own, [near(x) for x in own]]
+            blocks = [fars, own, [near(x) for x in lax.optimization_barrier(tuple(own))]]
         else:
             (code,) = update(arrived, mine, True)
     codes, _ = share(code)

time: 194 us -> 192 us (0.990)
  Pallas kernels: 41.8 us -> 38 us
    ppermute x7 -> x6, waiting for transfers between devices: 6.5 us -> 3.59 us  [far(): return lax.ppermute(x, 'tile', far_pairs)]
    pallas_call x2, Pallas kernels: 8.33 us -> 5.48 us  [gather(): pl.pallas_call(functools.partial(gather_kernel, pieces, rows // views, co...]
    ppermute x7, waiting for transfers between devices: 0.02 us -> 2.81 us  [near(): return lax.ppermute(x, 'tile', near_pairs)]
    ppermute x7 -> x6, starting transfers between devices: 14.5 us -> 13.6 us  [far(): return lax.ppermute(x, 'tile', far_pairs)]
    unnamed x71 -> x69, local copies, waits for them, and re-layouts: 6.73 us -> 7.59 us
  transfers between devices with their start and end apart: 32 -> 31, of which waited for: 15 -> 15; matrix products, arithmetic and copies ran while one was open for 9% -> 9% of each run, Pallas kernels for 3% -> 2%
where the time goes in v4:
time: 192 us; the launch traced here: 191 us
  waiting for transfers between devices  84.3 us (44%)
  starting transfers between devices  40.1 us (21%)
  Pallas kernels  38 us (20%)
  local copies, waits for them, and re-layouts  19.2 us (10%)
  other arithmetic  7.1 us (4%)
  between operations  2.49 us (1%)
    ppermute x18, waiting for transfers between devices, from_view(): return lax.ppermute(x, 'view', [(v, v ^ bits) for v in range(views)])  77.9 us
    pallas_call x2, Pallas kernels, sweep(): pl.pallas_call(functools.partial(sweep_kernel, (pieces, shares, pieces_ou...  26.2 us
    ppermute x18, starting transfers between devices, from_view(): return lax.ppermute(x, 'view', [(v, v ^ bits) for v in range(views)])  21.4 us
    ppermute x6, starting transfers between devices, far(): return lax.ppermute(x, 'tile', far_pairs)  13.6 us
    unnamed x69, local copies, waits for them, and re-layouts  7.59 us
    pallas_call x2, Pallas kernels, update(): pl.pallas_call(functools.partial(update_kernel, last, views), out_shape=s...  6.33 us
    pallas_call x2, Pallas kernels, gather(): pl.pallas_call(functools.partial(gather_kernel, pieces, rows // views, co...  5.48 us
    ppermute x7, starting transfers between devices, near(): return lax.ppermute(x, 'tile', near_pairs)  5.14 us
  transfers between devices with their start and end apart: 31, of which 15 were waited for; matrix products, arithmetic and copies ran while one was open for 9% of the time, Pallas kernels for 2%

profile of v4, /device:TPU:8, one launch (start us, length us, event | category | flops | bytes accessed | tf_op | source)
XLA Modules:
  0.0 191.2 jit_solution(3433993495124186400)
XLA Ops:
  0.0 1.4 constant_dynamic-slice_fusion
  1.5 1.1 copy.32
  2.5 1.9 collective-permute-start
  4.5 1.5 broadcast_select_fusion
  6.0 1.7 collective-permute-start.7
  7.7 2.2 %copy.31 = bf16[32,128,256]{2,0,1:T(8,128)(2,1)S(1)} copy(f32[32,128,256]{2,1,0:T(8,128)S(1)} %copy-done.1) | data formatting | bytes 6291456 | tf_op jit(solution)/shard_map/optimization_barrier | solution.py:360
  9.9 1.5 collective-permute-start.5
  14.8 1.6 collective-permute-start.2
  16.4 1.5 collective-permute-start.1
  18.0 2.1 %collective-permute-start.6 = (bf16[16,128,256]{2,1,0:T(8,128)(2,1)}, bf16[16,128,256]{2,1,0:T(8,128)(2,1)}, u32[]{:S(2)}, u32[]{:S(2)}) collective-permute-start(bf16[16,128,256]{2,1,0:T(8,128)(2,1)} %get-tuple-element.32), channel_id=1, source_target_pairs={{4,8},{8,4},{12,16},{16,12},{20,24},{24,20},{5,9},{9,5},{13,17},{1... | collective-permute-start | bytes 3145736 | tf_op jit(solution)/shard_map/ppermute | solution.py:328
  20.1 0.8 select_reduce_fusion.2
  20.9 0.9 select_reduce_fusion.1
  21.8 0.9 select_reduce_fusion.refs_17_.refs_24_
  22.7 6.3 %collective-permute-done.2.refs_4_ = bf16[32,32,256]{2,1,0:T(8,128)(2,1)S(1)} collective-permute-done((bf16[32,32,256]{2,1,0:T(8,128)(2,1)}, bf16[32,32,256]{2,1,0:T(8,128)(2,1)S(1)}, u32[]{:S(2)}, u32[]{:S(2)}) %collective-permute-start.2) | collective-permute-done | bytes 524320 | tf_op jit(solution)/shard_map/ppermute | solution.py:334
  29.0 0.8 copy-done.11
  29.7 0.7 slice.60
  30.5 1.5 collective-permute-start.4
  32.0 0.8 copy-done.12
  32.8 0.7 slice.59
  33.5 1.5 collective-permute-start.3
  35.0 0.7 select_reduce_fusion.3
  35.8 0.9 copy.16
  36.6 0.7 copy.17.refs_14_.refs_21_
  37.4 0.8 copy.18.refs_16_.refs_23_
  38.1 1.3 select_convert_fusion.refs_12_.refs_19_
  39.4 1.7 collective-permute-done.3.refs_5_
  41.2 13.3 %sweep.2 = (s16[33,32,256]{2,1,0:T(8,128)(2,1)}, s16[33,32,256]{2,1,0:T(8,128)(2,1)}, s16[33,32,256]{2,1,0:T(8,128)(2,1)}, s16[33,32,256]{2,1,0:T(8,128)(2,1)}) custom-call(s32[1]{0:T(128)} %bitcast.refs_0_, s32[64]{0:T(128)} %get-tuple-element.53.refs_1_, bf16[32,32,256]{2,1,0:T(8,128)(2,1)} %collective-permute-done.refs_2_, ...), custom_call_target="tpu_custom_call" | custom-call | tf_op jit(solution)/shard_map/sweep/pallas_call | solution.py:169
  55.0 1.5 collective-permute-start.9
  56.6 1.4 collective-permute-start.10
  58.0 2.4 %copy.19 = f32[32,128,256]{2,0,1:T(8,128)S(1)} copy(f32[32,128,256]{2,1,0:T(8,128)S(1)} %copy-done.2) | data formatting | bytes 8388608 | tf_op jit(solution)/shard_map/optimization_barrier | solution.py:407
  60.4 1.1 dynamic-slice_bitcast_fusion.refs_4_
  61.5 8.4 %collective-permute-done.8.refs_1_ = s16[33,32,256]{2,1,0:T(8,128)(2,1)S(1)} collective-permute-done((s16[33,32,256]{2,1,0:T(8,128)(2,1)}, s16[33,32,256]{2,1,0:T(8,128)(2,1)S(1)}, u32[]{:S(2)}, u32[]{:S(2)}) %collective-permute-start.8) | collective-permute-done | bytes 540704 | tf_op jit(solution)/shard_map/ppermute | solution.py:334
  69.9 8.1 %collective-permute-done.9.refs_2_ = s16[33,32,256]{2,1,0:T(8,128)(2,1)S(1)} collective-permute-done((s16[33,32,256]{2,1,0:T(8,128)(2,1)}, s16[33,32,256]{2,1,0:T(8,128)(2,1)S(1)}, u32[]{:S(2)}, u32[]{:S(2)}) %collective-permute-start.9) | collective-permute-done | bytes 540704 | tf_op jit(solution)/shard_map/ppermute | solution.py:334
  78.0 1.5 collective-permute-done.10.refs_3_
  79.6 0.8 copy-done.18
  80.4 3.2 %update.2 = (f32[32,32,256]{2,1,0:T(8,128)}, bf16[32,32,256]{2,1,0:T(8,128)(2,1)}) custom-call(s16[33,32,256]{2,1,0:T(8,128)(2,1)} %get-tuple-element.35.refs_0_, s16[33,32,256]{2,1,0:T(8,128)(2,1)} %copy-done.15, s16[33,32,256]{2,1,0:T(8,128)(2,1)} %copy-done.16, s16[33,32,256]{2,1,0:T(8,128)(2,1)} %copy-done.18, ...), custom_call_target="tpu_custom_call" | custom-call | tf_op jit(solution)/shard_map/update/pallas_call | solution.py:247
  83.6 1.7 collective-permute-start.14
  85.2 1.5 collective-permute-start.12
  86.7 1.9 collective-permute-start.11
  88.7 6.2 %collective-permute-done.14.refs_8_ = bf16[32,32,256]{2,1,0:T(8,128)(2,1)S(1)} collective-permute-done((bf16[32,32,256]{2,1,0:T(8,128)(2,1)}, bf16[32,32,256]{2,1,0:T(8,128)(2,1)S(1)}, u32[]{:S(2)}, u32[]{:S(2)}) %collective-permute-start.14) | collective-permute-done | bytes 524320 | tf_op jit(solution)/shard_map/ppermute | solution.py:334
  94.9 1.9 collective-permute-start.15
  96.8 3.6 %collective-permute-start.13 = (bf16[32,32,256]{2,1,0:T(8,128)(2,1)S(1)}, bf16[32,32,256]{2,1,0:T(8,128)(2,1)S(1)}, u32[]{:S(2)}, u32[]{:S(2)}) collective-permute-start(bf16[32,32,256]{2,1,0:T(8,128)(2,1)S(1)} %collective-permute-done.12.refs_7_), channel_id=1, source_target_pairs={{4,8},{8,4},{12,16},{16,12},{20,24},{24,20},{5,9},{9,5},{13,17},{1... | collective-permute-start | bytes 1572872 | tf_op jit(solution)/shard_map/ppermute | solution.py:328
  101.2 0.7 collective-permute-start.16
  101.9 6.8 %collective-permute-done.17.refs_10_ = bf16[16,32,256]{2,1,0:T(8,128)(2,1)S(1)} collective-permute-done((bf16[16,32,256]{2,1,0:T(8,128)(2,1)S(1)}, bf16[16,32,256]{2,1,0:T(8,128)(2,1)S(1)}, u32[]{:S(2)}, u32[]{:S(2)}) %collective-permute-start.17) | collective-permute-done | bytes 262176 | tf_op jit(solution)/shard_map/ppermute | solution.py:334
  109.2 2.1 %collective-permute-start.18 = (bf16[32,32,256]{2,1,0:T(8,128)(2,1)S(1)}, bf16[32,32,256]{2,1,0:T(8,128)(2,1)S(1)}, u32[]{:S(2)}, u32[]{:S(2)}) collective-permute-start(bf16[32,32,256]{2,1,0:T(8,128)(2,1)S(1)} %pad_maximum_fusion), channel_id=1, source_target_pairs={{4,8},{8,4},{12,16},{16,12},{20,24},{24,20},{5,9},{9,5},{13,17},{1... | collective-permute-start | bytes 1572872 | tf_op jit(solution)/shard_map/ppermute | solution.py:328
  111.3 1.3 collective-permute-start.19
  113.3 2.8 %collective-permute-done.23.refs_15_ = bf16[16,32,256]{2,1,0:T(8,128)(2,1)S(1)} collective-permute-done((bf16[16,32,256]{2,1,0:T(8,128)(2,1)S(1)}, bf16[16,32,256]{2,1,0:T(8,128)(2,1)S(1)}, u32[]{:S(2)}, u32[]{:S(2)}) %collective-permute-start.23) | collective-permute-done | bytes 262176 | tf_op jit(solution)/shard_map/ppermute | solution.py:331
  116.1 3.6 %collective-permute-done.18.refs_5_ = bf16[32,32,256]{2,1,0:T(8,128)(2,1)S(1)} collective-permute-done((bf16[32,32,256]{2,1,0:T(8,128)(2,1)S(1)}, bf16[32,32,256]{2,1,0:T(8,128)(2,1)S(1)}, u32[]{:S(2)}, u32[]{:S(2)}) %collective-permute-start.18) | collective-permute-done | bytes 524320 | tf_op jit(solution)/shard_map/ppermute | solution.py:328
  119.8 0.7 copy-done.25
  120.8 0.8 copy-done.28
  121.7 12.9 %sweep.3 = (s16[33,32,256]{2,1,0:T(8,128)(2,1)}, s16[33,32,256]{2,1,0:T(8,128)(2,1)}, s16[33,32,256]{2,1,0:T(8,128)(2,1)}, s16[33,32,256]{2,1,0:T(8,128)(2,1)}) custom-call(s32[1]{0:T(128)} %bitcast.refs_0_, s32[64]{0:T(128)} %get-tuple-element.53.refs_1_, bf16[32,32,256]{2,1,0:T(8,128)(2,1)} %copy-done.22, bf16[32,32,256]{2,1,0:T(8,128)(2,1)} %copy-done.24, ...), custom_call_target="tpu_custom_call" | custom-call | tf_op jit(solution)/shard_map/sweep/pallas_call | solution.py:169
  134.6 1.5 collective-permute-start.24
  136.7 1.5 collective-permute-start.26
  138.1 11.8 %collective-permute-done.24.refs_1_ = s16[33,32,256]{2,1,0:T(8,128)(2,1)S(1)} collective-permute-done((s16[33,32,256]{2,1,0:T(8,128)(2,1)}, s16[33,32,256]{2,1,0:T(8,128)(2,1)S(1)}, u32[]{:S(2)}, u32[]{:S(2)}) %collective-permute-start.24) | collective-permute-done | bytes 540704 | tf_op jit(solution)/shard_map/ppermute | solution.py:334
  149.9 12.4 %collective-permute-done.25.refs_2_ = s16[33,32,256]{2,1,0:T(8,128)(2,1)S(1)} collective-permute-done((s16[33,32,256]{2,1,0:T(8,128)(2,1)}, s16[33,32,256]{2,1,0:T(8,128)(2,1)S(1)}, u32[]{:S(2)}, u32[]{:S(2)}) %collective-permute-start.25) | collective-permute-done | bytes 540704 | tf_op jit(solution)/shard_map/ppermute | solution.py:334
  162.3 0.8 copy-done.19
  163.3 3.1 %update.3.refs_1_ = s16[33,32,256]{2,1,0:T(8,128)(2,1)} custom-call(s16[33,32,256]{2,1,0:T(8,128)(2,1)} %get-tuple-element.46.refs_0_, s16[33,32,256]{2,1,0:T(8,128)(2,1)} %copy-done.17, s16[33,32,256]{2,1,0:T(8,128)(2,1)} %copy-done.19, s16[33,32,256]{2,1,0:T(8,128)(2,1)} %copy-done.20, f32[32,32,256]{2,1,0:T(8,128)} %get-tuple-element.50.refs_4_), custom_call_target="tpu_custom_call" | custom-call | tf_op jit(solution)/shard_map/update/pallas_call | solution.py:247
  167.1 1.0 collective-permute-start.27
  168.1 12.2 %collective-permute-done.29.refs_3_ = s16[33,32,256]{2,1,0:T(8,128)(2,1)S(1)} collective-permute-done((s16[33,32,256]{2,1,0:T(8,128)(2,1)}, s16[33,32,256]{2,1,0:T(8,128)(2,1)S(1)}, u32[]{:S(2)}, u32[]{:S(2)}) %collective-permute-start.29) | collective-permute-done | bytes 540704 | tf_op jit(solution)/shard_map/ppermute | solution.py:334
  180.9 1.5 collective-permute-start.28
  182.4 3.3 %gather.2.refs_3_ = f32[32,128,256]{2,1,0:T(8,128)} custom-call(s32[1]{0:T(128)} %bitcast.refs_0_, s16[33,32,256]{2,1,0:T(8,128)(2,1)} %update.3.refs_1_, s16[33,32,256]{2,1,0:T(8,128)(2,1)} %copy-done.8, s16[33,32,256]{2,1,0:T(8,128)(2,1)} %copy-done.7), custom_call_target="tpu_custom_call" | custom-call | tf_op jit(solution)/shard_map/gather/pallas_call | solution.py:291
  185.7 1.7 collective-permute-done.30.refs_2_
  188.2 0.7 copy-done.30
  188.9 2.2 %gather.3 = f32[32,128,256]{2,1,0:T(8,128)} custom-call(s32[1]{0:T(128)} %bitcast.refs_0_, s16[17,32,256]{2,1,0:T(8,128)(2,1)} %copy-done.30, s16[17,32,256]{2,1,0:T(8,128)(2,1)} %copy-done.29, f32[32,128,256]{2,1,0:T(8,128)} %gather.2.refs_3_), custom_call_target="tpu_custom_call", output_to_operand_aliasing={{}: (3, {})} | custom-call | tf_op jit(solution)/shard_map/gather/pallas_call | solution.py:291
  (109 shorter events, 7.0 us)
Async XLA Ops:
  0.0 17.9 %copy-start = (bf16[8,3,33]{2,0,1:T(8,128)(2,1)S(1)}, bf16[8,3,33]{2,0,1:T(8,128)(2,1)}, u32[]{:S(2)}) copy-start(bf16[8,3,33]{2,0,1:T(8,128)(2,1)} %param.7) | copy-start | bytes 4756
  0.0 4.5 %copy-start.3 = (bf16[1,32,128,256]{3,2,1,0:T(8,128)(2,1)S(1)}, bf16[1,32,128,256]{3,2,1,0:T(8,128)(2,1)}, u32[]{:S(2)}) copy-start(bf16[1,32,128,256]{3,2,1,0:T(8,128)(2,1)} %param.6) | copy-start | bytes 6291460
  2.5 12.2 %collective-permute-start = (bf16[32,32,256]{2,1,0:T(8,128)(2,1)}, bf16[32,32,256]{2,1,0:T(8,128)(2,1)}, u32[]{:S(2)}, u32[]{:S(2)}) collective-permute-start(bf16[32,32,256]{2,1,0:T(8,128)(2,1)} %bitcast.29), channel_id=1, source_target_pairs={{4,8},{8,4},{12,16},{16,12},{20,24},{24,20},{5,9},{9,5},{13,17},{1... | collective-permute-start | bytes 1572872 | tf_op jit(solution)/shard_map/ppermute | solution.py:328
  4.5 3.2 %copy-start.1 = (f32[32,128,256]{2,1,0:T(8,128)S(1)}, f32[32,128,256]{2,1,0:T(8,128)}, u32[]{:S(2)}) copy-start(f32[32,128,256]{2,1,0:T(8,128)} %param.5) | copy-start | bytes 12582916
  6.0 6.1 %copy-start.33 = (s32[1,2]{1,0:T(1,128)S(1)}, s32[1,2]{1,0:T(1,128)}, u32[]{:S(2)}) copy-start(s32[1,2]{1,0:T(1,128)} %param.9) | copy-start | bytes 28
  6.0 33.4 %collective-permute-start.7 = (bf16[16,128,256]{2,1,0:T(8,128)(2,1)}, bf16[16,128,256]{2,1,0:T(8,128)(2,1)S(1)}, u32[]{:S(2)}, u32[]{:S(2)}) collective-permute-start(bf16[16,128,256]{2,1,0:T(8,128)(2,1)} %get-tuple-element.55), channel_id=1, source_target_pairs={{0,4},{4,0},{8,12},{12,8},{16,20},{20,16},{24,28},{28,24},{1,5},{5... | collective-permute-start | bytes 3145736 | tf_op jit(solution)/shard_map/ppermute | solution.py:331
  9.9 31.2 %copy-start.4 = (bf16[32,128,256]{2,0,1:T(8,128)(2,1)}, bf16[32,128,256]{2,0,1:T(8,128)(2,1)S(1)}, u32[]{:S(2)}) copy-start(bf16[32,128,256]{2,0,1:T(8,128)(2,1)S(1)} %copy.31) | copy-start | bytes 6291460
  9.9 31.2 %collective-permute-start.5 = (bf16[128,32,256]{2,1,0:T(8,128)(2,1)S(1)}, bf16[128,32,256]{2,1,0:T(8,128)(2,1)}, u32[]{:S(2)}, u32[]{:S(2)}) collective-permute-start(bf16[128,32,256]{2,1,0:T(8,128)(2,1)S(1)} %bitcast.35), channel_id=1, source_target_pairs={{0,4},{4,0},{8,12},{12,8},{16,20},{20,16},{24,28},{28,24},{1,5},{5... | collective-permute-start | bytes 6291464 | tf_op jit(solution)/shard_map/ppermute | solution.py:331
  14.8 14.2 %collective-permute-start.2 = (bf16[32,32,256]{2,1,0:T(8,128)(2,1)}, bf16[32,32,256]{2,1,0:T(8,128)(2,1)S(1)}, u32[]{:S(2)}, u32[]{:S(2)}) collective-permute-start(bf16[32,32,256]{2,1,0:T(8,128)(2,1)} %collective-permute-done.refs_2_), channel_id=1, source_target_pairs={{0,2},{1,3},{2,0},{3,1},{4,6},{5,7},{6,4},{7,5},{8,10},{9,11},{10,... | collective-permute-start | bytes 1572872 | tf_op jit(solution)/shard_map/ppermute | solution.py:334
  16.4 15.6 %collective-permute-start.1 = (bf16[32,32,256]{2,1,0:T(8,128)(2,1)}, bf16[32,32,256]{2,1,0:T(8,128)(2,1)S(1)}, u32[]{:S(2)}, u32[]{:S(2)}) collective-permute-start(bf16[32,32,256]{2,1,0:T(8,128)(2,1)} %collective-permute-done.refs_2_), channel_id=1, source_target_pairs={{0,1},{1,0},{2,3},{3,2},{4,5},{5,4},{6,7},{7,6},{8,9},{9,8},{10,11... | collective-permute-start | bytes 1572872 | tf_op jit(solution)/shard_map/ppermute | solution.py:334
  18.0 23.1 %collective-permute-start.6 = (bf16[16,128,256]{2,1,0:T(8,128)(2,1)}, bf16[16,128,256]{2,1,0:T(8,128)(2,1)}, u32[]{:S(2)}, u32[]{:S(2)}) collective-permute-start(bf16[16,128,256]{2,1,0:T(8,128)(2,1)} %get-tuple-element.32), channel_id=1, source_target_pairs={{4,8},{8,4},{12,16},{16,12},{20,24},{24,20},{5,9},{9,5},{13,17},{1... | collective-permute-start | bytes 3145736 | tf_op jit(solution)/shard_map/ppermute | solution.py:328
  22.7 18.4 %copy-start.6 = (bf16[256,256]{1,0:T(8,128)(2,1)}, bf16[256,256]{1,0:T(8,128)(2,1)S(1)}, u32[]{:S(2)}) copy-start(bf16[256,256]{1,0:T(8,128)(2,1)S(1)} %select_reduce_fusion.refs_17_.refs_24_) | copy-start | bytes 393220
  29.0 0.8 copy-start.11
  30.5 9.0 %collective-permute-start.4 = (bf16[16,32,256]{2,1,0:T(8,128)(2,1)}, bf16[16,32,256]{2,1,0:T(8,128)(2,1)}, u32[]{:S(2)}, u32[]{:S(2)}) collective-permute-start(bf16[16,32,256]{2,1,0:T(8,128)(2,1)} %slice.60), channel_id=1, source_target_pairs={{0,1},{1,0},{2,3},{3,2},{4,5},{5,4},{6,7},{7,6},{8,9},{9,8},{10,11... | collective-permute-start | bytes 786440 | tf_op jit(solution)/shard_map/ppermute | solution.py:334
  32.0 0.8 copy-start.12
  33.5 7.6 %collective-permute-start.3 = (bf16[16,32,256]{2,1,0:T(8,128)(2,1)}, bf16[16,32,256]{2,1,0:T(8,128)(2,1)}, u32[]{:S(2)}, u32[]{:S(2)}) collective-permute-start(bf16[16,32,256]{2,1,0:T(8,128)(2,1)} %slice.59), channel_id=1, source_target_pairs={{0,2},{1,3},{2,0},{3,1},{4,6},{5,7},{6,4},{7,5},{8,10},{9,11},{10,... | collective-permute-start | bytes 786440 | tf_op jit(solution)/shard_map/ppermute | solution.py:334
  36.6 4.5 %copy-start.21 = (bf16[128,128]{0,1:T(8,128)(2,1)}, bf16[128,128]{0,1:T(8,128)(2,1)S(1)}, u32[]{:S(2)}) copy-start(bf16[128,128]{0,1:T(8,128)(2,1)S(1)} %copy.16) | copy-start | bytes 98308
  39.4 1.7 copy-start.5
  41.1 16.9 %copy-start.2 = (f32[32,128,256]{2,1,0:T(8,128)S(1)}, f32[32,128,256]{2,1,0:T(8,128)}, u32[]{:S(2)}) copy-start(f32[32,128,256]{2,1,0:T(8,128)} %param.5) | copy-start | bytes 12582916
  54.4 15.5 %collective-permute-start.8 = (s16[33,32,256]{2,1,0:T(8,128)(2,1)}, s16[33,32,256]{2,1,0:T(8,128)(2,1)S(1)}, u32[]{:S(2)}, u32[]{:S(2)}) collective-permute-start(s16[33,32,256]{2,1,0:T(8,128)(2,1)} %get-tuple-element.36), channel_id=1, source_target_pairs={{0,1},{1,0},{2,3},{3,2},{4,5},{5,4},{6,7},{7,6},{8,9},{9,8},{10,11... | collective-permute-start | bytes 1622024 | tf_op jit(solution)/shard_map/ppermute | solution.py:334
  55.0 23.0 %collective-permute-start.9 = (s16[33,32,256]{2,1,0:T(8,128)(2,1)}, s16[33,32,256]{2,1,0:T(8,128)(2,1)S(1)}, u32[]{:S(2)}, u32[]{:S(2)}) collective-permute-start(s16[33,32,256]{2,1,0:T(8,128)(2,1)} %get-tuple-element.37), channel_id=1, source_target_pairs={{0,2},{1,3},{2,0},{3,1},{4,6},{5,7},{6,4},{7,5},{8,10},{9,11},{10,... | collective-permute-start | bytes 1622024 | tf_op jit(solution)/shard_map/ppermute | solution.py:334
  56.6 23.0 %collective-permute-start.10 = (s16[33,32,256]{2,1,0:T(8,128)(2,1)}, s16[33,32,256]{2,1,0:T(8,128)(2,1)S(1)}, u32[]{:S(2)}, u32[]{:S(2)}) collective-permute-start(s16[33,32,256]{2,1,0:T(8,128)(2,1)} %get-tuple-element.38), channel_id=1, source_target_pairs={{0,3},{1,2},{2,1},{3,0},{4,7},{5,6},{6,5},{7,4},{8,11},{9,10},{10,... | collective-permute-start | bytes 1622024 | tf_op jit(solution)/shard_map/ppermute | solution.py:334
  69.9 9.6 %copy-start.15 = (s16[33,32,256]{2,1,0:T(8,128)(2,1)}, s16[33,32,256]{2,1,0:T(8,128)(2,1)S(1)}, u32[]{:S(2)}) copy-start(s16[33,32,256]{2,1,0:T(8,128)(2,1)S(1)} %collective-permute-done.8.refs_1_) | copy-start | bytes 1622020
  78.0 1.5 copy-start.16
  79.6 0.8 copy-start.18
  83.6 11.3 %collective-permute-start.14 = (bf16[32,32,256]{2,1,0:T(8,128)(2,1)}, bf16[32,32,256]{2,1,0:T(8,128)(2,1)S(1)}, u32[]{:S(2)}, u32[]{:S(2)}) collective-permute-start(bf16[32,32,256]{2,1,0:T(8,128)(2,1)} %get-tuple-element.41.refs_6_), channel_id=1, source_target_pairs={{0,2},{1,3},{2,0},{3,1},{4,6},{5,7},{6,4},{7,5},{8,10},{9,11},{10,... | collective-permute-start | bytes 1572872 | tf_op jit(solution)/shard_map/ppermute | solution.py:334
  85.2 11.6 %collective-permute-start.12 = (bf16[32,32,256]{2,1,0:T(8,128)(2,1)}, bf16[32,32,256]{2,1,0:T(8,128)(2,1)S(1)}, u32[]{:S(2)}, u32[]{:S(2)}) collective-permute-start(bf16[32,32,256]{2,1,0:T(8,128)(2,1)} %get-tuple-element.41.refs_6_), channel_id=1, source_target_pairs={{0,1},{1,0},{2,3},{3,2},{4,5},{5,4},{6,7},{7,6},{8,9},{9,8},{10,11... | collective-permute-start | bytes 1572872 | tf_op jit(solution)/shard_map/ppermute | solution.py:334
  86.7 24.6 %collective-permute-start.11 = (bf16[32,32,256]{2,1,0:T(8,128)(2,1)}, bf16[32,32,256]{2,1,0:T(8,128)(2,1)S(1)}, u32[]{:S(2)}, u32[]{:S(2)}) collective-permute-start(bf16[32,32,256]{2,1,0:T(8,128)(2,1)} %get-tuple-element.41.refs_6_), channel_id=1, source_target_pairs={{4,8},{8,4},{12,16},{16,12},{20,24},{24,20},{5,9},{9,5},{13,17},{1... | collective-permute-start | bytes 1572872 | tf_op jit(solution)/shard_map/ppermute | solution.py:328
  94.9 24.8 %copy-start.9 = (bf16[32,32,256]{2,1,0:T(8,128)(2,1)}, bf16[32,32,256]{2,1,0:T(8,128)(2,1)S(1)}, u32[]{:S(2)}) copy-start(bf16[32,32,256]{2,1,0:T(8,128)(2,1)S(1)} %collective-permute-done.14.refs_8_) | copy-start | bytes 1572868
  94.9 17.8 %collective-permute-start.15 = (bf16[32,32,256]{2,1,0:T(8,128)(2,1)S(1)}, bf16[32,32,256]{2,1,0:T(8,128)(2,1)S(1)}, u32[]{:S(2)}, u32[]{:S(2)}) collective-permute-start(bf16[32,32,256]{2,1,0:T(8,128)(2,1)S(1)} %collective-permute-done.14.refs_8_), channel_id=1, source_target_pairs={{4,8},{8,4},{12,16},{16,12},{20,24},{24,20},{5,9},{9,5},{13,17},{1... | collective-permute-start | bytes 1572872 | tf_op jit(solution)/shard_map/ppermute | solution.py:328
  96.8 22.9 %copy-start.10 = (bf16[32,32,256]{2,1,0:T(8,128)(2,1)}, bf16[32,32,256]{2,1,0:T(8,128)(2,1)S(1)}, u32[]{:S(2)}) copy-start(bf16[32,32,256]{2,1,0:T(8,128)(2,1)S(1)} %collective-permute-done.12.refs_7_) | copy-start | bytes 1572868
  96.8 15.9 %collective-permute-start.13 = (bf16[32,32,256]{2,1,0:T(8,128)(2,1)S(1)}, bf16[32,32,256]{2,1,0:T(8,128)(2,1)S(1)}, u32[]{:S(2)}, u32[]{:S(2)}) collective-permute-start(bf16[32,32,256]{2,1,0:T(8,128)(2,1)S(1)} %collective-permute-done.12.refs_7_), channel_id=1, source_target_pairs={{4,8},{8,4},{12,16},{16,12},{20,24},{24,20},{5,9},{9,5},{13,17},{1... | collective-permute-start | bytes 1572872 | tf_op jit(solution)/shard_map/ppermute | solution.py:328
  100.5 8.2 %collective-permute-start.17 = (bf16[16,32,256]{2,1,0:T(8,128)(2,1)S(1)}, bf16[16,32,256]{2,1,0:T(8,128)(2,1)S(1)}, u32[]{:S(2)}, u32[]{:S(2)}) collective-permute-start(bf16[16,32,256]{2,1,0:T(8,128)(2,1)S(1)} %slice.62), channel_id=1, source_target_pairs={{0,1},{1,0},{2,3},{3,2},{4,5},{5,4},{6,7},{7,6},{8,9},{9,8},{10,11... | collective-permute-start | bytes 786440 | tf_op jit(solution)/shard_map/ppermute | solution.py:334
  101.2 7.9 %collective-permute-start.16 = (bf16[16,32,256]{2,1,0:T(8,128)(2,1)S(1)}, bf16[16,32,256]{2,1,0:T(8,128)(2,1)S(1)}, u32[]{:S(2)}, u32[]{:S(2)}) collective-permute-start(bf16[16,32,256]{2,1,0:T(8,128)(2,1)S(1)} %slice.61), channel_id=1, source_target_pairs={{0,2},{1,3},{2,0},{3,1},{4,6},{5,7},{6,4},{7,5},{8,10},{9,11},{10,... | collective-permute-start | bytes 786440 | tf_op jit(solution)/shard_map/ppermute | solution.py:334
  108.7 11.0 %copy-start.13 = (bf16[16,32,256]{2,1,0:T(8,128)(2,1)}, bf16[16,32,256]{2,1,0:T(8,128)(2,1)S(1)}, u32[]{:S(2)}) copy-start(bf16[16,32,256]{2,1,0:T(8,128)(2,1)S(1)} %collective-permute-done.17.refs_10_) | copy-start | bytes 786436
  109.1 10.6 %copy-start.14 = (bf16[16,32,256]{2,1,0:T(8,128)(2,1)}, bf16[16,32,256]{2,1,0:T(8,128)(2,1)S(1)}, u32[]{:S(2)}) copy-start(bf16[16,32,256]{2,1,0:T(8,128)(2,1)S(1)} %collective-permute-done.16.refs_9_) | copy-start | bytes 786436
  109.1 4.1 %collective-permute-start.22 = (bf16[16,32,256]{2,1,0:T(8,128)(2,1)S(1)}, bf16[16,32,256]{2,1,0:T(8,128)(2,1)S(1)}, u32[]{:S(2)}, u32[]{:S(2)}) collective-permute-start(bf16[16,32,256]{2,1,0:T(8,128)(2,1)S(1)} %collective-permute-done.16.refs_9_), channel_id=1, source_target_pairs={{0,4},{4,0},{8,12},{12,8},{16,20},{20,16},{24,28},{28,24},{1,5},{5... | collective-permute-start | bytes 786440 | tf_op jit(solution)/shard_map/ppermute | solution.py:331
  109.2 10.5 %collective-permute-start.18 = (bf16[32,32,256]{2,1,0:T(8,128)(2,1)S(1)}, bf16[32,32,256]{2,1,0:T(8,128)(2,1)S(1)}, u32[]{:S(2)}, u32[]{:S(2)}) collective-permute-start(bf16[32,32,256]{2,1,0:T(8,128)(2,1)S(1)} %pad_maximum_fusion), channel_id=1, source_target_pairs={{4,8},{8,4},{12,16},{16,12},{20,24},{24,20},{5,9},{9,5},{13,17},{1... | collective-permute-start | bytes 1572872 | tf_op jit(solution)/shard_map/ppermute | solution.py:328
  111.3 8.4 %copy-start.22 = (bf16[32,32,256]{2,1,0:T(8,128)(2,1)}, bf16[32,32,256]{2,1,0:T(8,128)(2,1)S(1)}, u32[]{:S(2)}) copy-start(bf16[32,32,256]{2,1,0:T(8,128)(2,1)S(1)} %collective-permute-done.11.refs_2_) | copy-start | bytes 1572868
  111.3 8.3 %collective-permute-start.19 = (bf16[32,32,256]{2,1,0:T(8,128)(2,1)}, bf16[32,32,256]{2,1,0:T(8,128)(2,1)S(1)}, u32[]{:S(2)}, u32[]{:S(2)}) collective-permute-start(bf16[32,32,256]{2,1,0:T(8,128)(2,1)} %get-tuple-element.41.refs_6_), channel_id=1, source_target_pairs={{0,4},{4,0},{8,12},{12,8},{16,20},{20,16},{24,28},{28,24},{1,5},{5... | collective-permute-start | bytes 1572872 | tf_op jit(solution)/shard_map/ppermute | solution.py:331
  112.7 7.1 %copy-start.23 = (bf16[32,32,256]{2,1,0:T(8,128)(2,1)}, bf16[32,32,256]{2,1,0:T(8,128)(2,1)S(1)}, u32[]{:S(2)}) copy-start(bf16[32,32,256]{2,1,0:T(8,128)(2,1)S(1)} %collective-permute-done.15.refs_4_) | copy-start | bytes 1572868
  112.7 7.0 %collective-permute-start.20 = (bf16[32,32,256]{2,1,0:T(8,128)(2,1)S(1)}, bf16[32,32,256]{2,1,0:T(8,128)(2,1)S(1)}, u32[]{:S(2)}, u32[]{:S(2)}) collective-permute-start(bf16[32,32,256]{2,1,0:T(8,128)(2,1)S(1)} %collective-permute-done.12.refs_7_), channel_id=1, source_target_pairs={{0,4},{4,0},{8,12},{12,8},{16,20},{20,16},{24,28},{28,24},{1,5},{5... | collective-permute-start | bytes 1572872 | tf_op jit(solution)/shard_map/ppermute | solution.py:331
  112.8 7.0 %copy-start.24 = (bf16[32,32,256]{2,1,0:T(8,128)(2,1)}, bf16[32,32,256]{2,1,0:T(8,128)(2,1)S(1)}, u32[]{:S(2)}) copy-start(bf16[32,32,256]{2,1,0:T(8,128)(2,1)S(1)} %collective-permute-done.13.refs_3_) | copy-start | bytes 1572868
  112.8 6.9 %collective-permute-start.21 = (bf16[32,32,256]{2,1,0:T(8,128)(2,1)S(1)}, bf16[32,32,256]{2,1,0:T(8,128)(2,1)S(1)}, u32[]{:S(2)}, u32[]{:S(2)}) collective-permute-start(bf16[32,32,256]{2,1,0:T(8,128)(2,1)S(1)} %collective-permute-done.14.refs_8_), channel_id=1, source_target_pairs={{0,4},{4,0},{8,12},{12,8},{16,20},{20,16},{24,28},{28,24},{1,5},{5... | collective-permute-start | bytes 1572872 | tf_op jit(solution)/shard_map/ppermute | solution.py:331
  113.2 6.6 %copy-start.31 = (bf16[16,32,256]{2,1,0:T(8,128)(2,1)}, bf16[16,32,256]{2,1,0:T(8,128)(2,1)S(1)}, u32[]{:S(2)}) copy-start(bf16[16,32,256]{2,1,0:T(8,128)(2,1)S(1)} %collective-permute-done.22.refs_14_) | copy-start | bytes 786436
  113.2 2.9 %collective-permute-start.23 = (bf16[16,32,256]{2,1,0:T(8,128)(2,1)S(1)}, bf16[16,32,256]{2,1,0:T(8,128)(2,1)S(1)}, u32[]{:S(2)}, u32[]{:S(2)}) collective-permute-start(bf16[16,32,256]{2,1,0:T(8,128)(2,1)S(1)} %collective-permute-done.17.refs_10_), channel_id=1, source_target_pairs={{0,4},{4,0},{8,12},{12,8},{16,20},{20,16},{24,28},{28,24},{1,5},{5... | collective-permute-start | bytes 786440 | tf_op jit(solution)/shard_map/ppermute | solution.py:331
  116.1 3.7 %copy-start.32 = (bf16[16,32,256]{2,1,0:T(8,128)(2,1)}, bf16[16,32,256]{2,1,0:T(8,128)(2,1)S(1)}, u32[]{:S(2)}) copy-start(bf16[16,32,256]{2,1,0:T(8,128)(2,1)S(1)} %collective-permute-done.23.refs_15_) | copy-start | bytes 786436
  119.7 0.9 copy-start.25
  119.7 1.0 copy-start.26
  119.7 1.2 copy-start.27
  120.8 0.8 copy-start.28
  134.6 15.3 %collective-permute-start.24 = (s16[33,32,256]{2,1,0:T(8,128)(2,1)}, s16[33,32,256]{2,1,0:T(8,128)(2,1)S(1)}, u32[]{:S(2)}, u32[]{:S(2)}) collective-permute-start(s16[33,32,256]{2,1,0:T(8,128)(2,1)} %get-tuple-element.47), channel_id=1, source_target_pairs={{0,1},{1,0},{2,3},{3,2},{4,5},{5,4},{6,7},{7,6},{8,9},{9,8},{10,11... | collective-permute-start | bytes 1622024 | tf_op jit(solution)/shard_map/ppermute | solution.py:334
  136.1 26.2 %collective-permute-start.25 = (s16[33,32,256]{2,1,0:T(8,128)(2,1)}, s16[33,32,256]{2,1,0:T(8,128)(2,1)S(1)}, u32[]{:S(2)}, u32[]{:S(2)}) collective-permute-start(s16[33,32,256]{2,1,0:T(8,128)(2,1)} %get-tuple-element.48), channel_id=1, source_target_pairs={{0,2},{1,3},{2,0},{3,1},{4,6},{5,7},{6,4},{7,5},{8,10},{9,11},{10,... | collective-permute-start | bytes 1622024 | tf_op jit(solution)/shard_map/ppermute | solution.py:334
  136.7 25.6 %collective-permute-start.26 = (s16[33,32,256]{2,1,0:T(8,128)(2,1)}, s16[33,32,256]{2,1,0:T(8,128)(2,1)S(1)}, u32[]{:S(2)}, u32[]{:S(2)}) collective-permute-start(s16[33,32,256]{2,1,0:T(8,128)(2,1)} %get-tuple-element.49), channel_id=1, source_target_pairs={{0,3},{1,2},{2,1},{3,0},{4,7},{5,6},{6,5},{7,4},{8,11},{9,10},{10,... | collective-permute-start | bytes 1622024 | tf_op jit(solution)/shard_map/ppermute | solution.py:334
  149.9 12.4 %copy-start.17 = (s16[33,32,256]{2,1,0:T(8,128)(2,1)}, s16[33,32,256]{2,1,0:T(8,128)(2,1)S(1)}, u32[]{:S(2)}) copy-start(s16[33,32,256]{2,1,0:T(8,128)(2,1)S(1)} %collective-permute-done.24.refs_1_) | copy-start | bytes 1622020
  162.3 0.8 copy-start.19
  162.3 1.0 copy-start.20
  166.4 13.9 %collective-permute-start.29 = (s16[33,32,256]{2,1,0:T(8,128)(2,1)}, s16[33,32,256]{2,1,0:T(8,128)(2,1)S(1)}, u32[]{:S(2)}, u32[]{:S(2)}) collective-permute-start(s16[33,32,256]{2,1,0:T(8,128)(2,1)} %update.3.refs_1_), channel_id=1, source_target_pairs={{0,2},{1,3},{2,0},{3,1},{4,6},{5,7},{6,4},{7,5},{8,10},{9,11},{10,... | collective-permute-start | bytes 1622024 | tf_op jit(solution)/shard_map/ppermute | solution.py:334
  167.1 13.8 %collective-permute-start.27 = (s16[33,32,256]{2,1,0:T(8,128)(2,1)}, s16[33,32,256]{2,1,0:T(8,128)(2,1)S(1)}, u32[]{:S(2)}, u32[]{:S(2)}) collective-permute-start(s16[33,32,256]{2,1,0:T(8,128)(2,1)} %update.3.refs_1_), channel_id=1, source_target_pairs={{0,1},{1,0},{2,3},{3,2},{4,5},{5,4},{6,7},{7,6},{8,9},{9,8},{10,11... | collective-permute-start | bytes 1622024 | tf_op jit(solution)/shard_map/ppermute | solution.py:334
  180.3 2.1 %copy-start.7 = (s16[33,32,256]{2,1,0:T(8,128)(2,1)}, s16[33,32,256]{2,1,0:T(8,128)(2,1)S(1)}, u32[]{:S(2)}) copy-start(s16[33,32,256]{2,1,0:T(8,128)(2,1)S(1)} %collective-permute-done.29.refs_3_) | copy-start | bytes 1622020
  180.3 7.1 %collective-permute-start.30 = (s16[17,32,256]{2,1,0:T(8,128)(2,1)S(1)}, s16[17,32,256]{2,1,0:T(8,128)(2,1)S(1)}, u32[]{:S(2)}, u32[]{:S(2)}) collective-permute-start(s16[17,32,256]{2,1,0:T(8,128)(2,1)S(1)} %slice.65), channel_id=1, source_target_pairs={{0,1},{1,0},{2,3},{3,2},{4,5},{5,4},{6,7},{7,6},{8,9},{9,8},{10,11... | collective-permute-start | bytes 835592 | tf_op jit(solution)/shard_map/ppermute | solution.py:334
  180.9 1.5 copy-start.8
  180.9 6.9 %collective-permute-start.28 = (s16[17,32,256]{2,1,0:T(8,128)(2,1)S(1)}, s16[17,32,256]{2,1,0:T(8,128)(2,1)S(1)}, u32[]{:S(2)}, u32[]{:S(2)}) collective-permute-start(s16[17,32,256]{2,1,0:T(8,128)(2,1)S(1)} %pad_add_fusion), channel_id=1, source_target_pairs={{0,2},{1,3},{2,0},{3,1},{4,6},{5,7},{6,4},{7,5},{8,10},{9,11},{10,... | collective-permute-start | bytes 835592 | tf_op jit(solution)/shard_map/ppermute | solution.py:334
  188.2 0.7 copy-start.30
  (1 other events, 0.7 us)

commit v5 on v4

--- a/solution.py
+++ b/solution.py
@@ -361,7 +361,9 @@
     far_piece = far(first_piece)
     bottom, top = data[:REACH], data[core - REACH :]
     to_far, to_near = jnp.where(even, bottom, top), jnp.where(even, top, bottom)
-    far_piece, to_far, psf_bank = lax.optimization_barrier((far_piece, to_far, psf_bank))
+    far_piece, to_far, psf_bank, psf_index, margin_extent = lax.optimization_barrier(
+        (far_piece, to_far, psf_bank, psf_index, margin_extent)
+    )
     far_blocks, _ = share(far_piece)
     measured = (far(to_far), data, near(to_near))
     start = jnp.transpose(volume.astype(half), (1, 0, 2))

time: 192 us -> 191 us (level)
  waiting for transfers between devices: 84.3 us -> 86.6 us
  other arithmetic: 7.1 us -> 5.15 us
    ppermute x6, waiting for transfers between devices: 3.59 us -> 5.53 us  [far(): return lax.ppermute(x, 'tile', far_pairs)]
  transfers between devices with their start and end apart: 31 -> 31, of which waited for: 15 -> 17; matrix products, arithmetic and copies ran while one was open for 9% -> 8% of each run, Pallas kernels for 2% -> 2%
where the time goes in v5:
time: 191 us; the launch traced here: 190 us
  waiting for transfers between devices  86.6 us (45%)
  starting transfers between devices  39.2 us (21%)
  Pallas kernels  38 us (20%)
  local copies, waits for them, and re-layouts  18.5 us (10%)
  other arithmetic  5.15 us (3%)
  between operations  2.46 us (1%)
    ppermute x18, waiting for transfers between devices, from_view(): return lax.ppermute(x, 'view', [(v, v ^ bits) for v in range(views)])  78.3 us
    pallas_call x2, Pallas kernels, sweep(): pl.pallas_call(functools.partial(sweep_kernel, (pieces, shares, pieces_ou...  26.2 us
    ppermute x18, starting transfers between devices, from_view(): return lax.ppermute(x, 'view', [(v, v ^ bits) for v in range(views)])  21.2 us
    ppermute x6, starting transfers between devices, far(): return lax.ppermute(x, 'tile', far_pairs)  13.6 us
    unnamed x69, local copies, waits for them, and re-layouts  7.6 us
    pallas_call x2, Pallas kernels, update(): pl.pallas_call(functools.partial(update_kernel, last, views), out_shape=s...  6.33 us
    ppermute x6, waiting for transfers between devices, far(): return lax.ppermute(x, 'tile', far_pairs)  5.53 us
    pallas_call x2, Pallas kernels, gather(): pl.pallas_call(functools.partial(gather_kernel, pieces, rows // views, co...  5.48 us
  transfers between devices with their start and end apart: 31, of which 17 were waited for; matrix products, arithmetic and copies ran while one was open for 8% of the time, Pallas kernels for 2%

profile of v5, /device:TPU:8, one launch (start us, length us, event | category | flops | bytes accessed | tf_op | source)
XLA Modules:
  0.0 190.1 jit_solution(13973560308027723040)
XLA Ops:
  0.0 1.4 constant_dynamic-slice_fusion
  1.5 1.1 copy.32
  2.6 1.9 %collective-permute-start = (bf16[32,32,256]{2,1,0:T(8,128)(2,1)}, bf16[32,32,256]{2,1,0:T(8,128)(2,1)}, u32[]{:S(2)}, u32[]{:S(2)}) collective-permute-start(bf16[32,32,256]{2,1,0:T(8,128)(2,1)} %bitcast.29), channel_id=1, source_target_pairs={{4,8},{8,4},{12,16},{16,12},{20,24},{24,20},{5,9},{9,5},{13,17},{1... | collective-permute-start | bytes 1572872 | tf_op jit(solution)/shard_map/ppermute | solution.py:328
  4.5 1.4 broadcast_select_fusion
  5.9 1.7 collective-permute-start.7
  7.6 2.2 %copy.31 = bf16[32,128,256]{2,0,1:T(8,128)(2,1)S(1)} copy(f32[32,128,256]{2,1,0:T(8,128)S(1)} %copy-done.1) | data formatting | bytes 6291456 | tf_op jit(solution)/shard_map/optimization_barrier | solution.py:360
  9.9 1.6 collective-permute-start.5
  12.2 1.2 collective-permute-done.refs_2_
  13.4 1.5 collective-permute-start.2
  14.9 1.5 collective-permute-start.1
  16.5 2.1 %collective-permute-start.6 = (bf16[16,128,256]{2,1,0:T(8,128)(2,1)}, bf16[16,128,256]{2,1,0:T(8,128)(2,1)}, u32[]{:S(2)}, u32[]{:S(2)}) collective-permute-start(bf16[16,128,256]{2,1,0:T(8,128)(2,1)} %get-tuple-element.35), channel_id=1, source_target_pairs={{4,8},{8,4},{12,16},{16,12},{20,24},{24,20},{5,9},{9,5},{13,17},{1... | collective-permute-start | bytes 3145736 | tf_op jit(solution)/shard_map/ppermute | solution.py:328
  20.4 0.6 and_convert_fusion
  21.7 0.9 select_reduce_fusion.refs_17_.refs_24_
  22.6 4.9 %collective-permute-done.2.refs_4_ = bf16[32,32,256]{2,1,0:T(8,128)(2,1)S(1)} collective-permute-done((bf16[32,32,256]{2,1,0:T(8,128)(2,1)}, bf16[32,32,256]{2,1,0:T(8,128)(2,1)S(1)}, u32[]{:S(2)}, u32[]{:S(2)}) %collective-permute-start.2) | collective-permute-done | bytes 524320 | tf_op jit(solution)/shard_map/ppermute | solution.py:334
  27.5 0.8 copy-done.9
  28.3 0.7 slice.60
  29.0 1.5 collective-permute-start.4
  30.5 0.8 copy-done.10
  31.3 0.7 slice.59
  32.1 1.5 collective-permute-start.3
  33.6 0.7 select_reduce_fusion.3
  34.4 0.7 copy.17.refs_14_.refs_21_
  35.2 0.8 copy.18.refs_16_.refs_23_
  35.9 0.6 select_convert_fusion.refs_12_.refs_19_
  37.0 2.7 %collective-permute-done.3.refs_5_ = bf16[16,32,256]{2,1,0:T(8,128)(2,1)} collective-permute-done((bf16[16,32,256]{2,1,0:T(8,128)(2,1)}, bf16[16,32,256]{2,1,0:T(8,128)(2,1)}, u32[]{:S(2)}, u32[]{:S(2)}) %collective-permute-start.3) | collective-permute-done | bytes 262176 | tf_op jit(solution)/shard_map/ppermute | solution.py:334
  39.8 13.3 %sweep.2 = (s16[33,32,256]{2,1,0:T(8,128)(2,1)}, s16[33,32,256]{2,1,0:T(8,128)(2,1)}, s16[33,32,256]{2,1,0:T(8,128)(2,1)}, s16[33,32,256]{2,1,0:T(8,128)(2,1)}) custom-call(s32[1]{0:T(128)} %bitcast.refs_0_, s32[64]{0:T(128)} %get-tuple-element.57.refs_1_, bf16[32,32,256]{2,1,0:T(8,128)(2,1)} %collective-permute-done.refs_2_, ...), custom_call_target="tpu_custom_call" | custom-call | tf_op jit(solution)/shard_map/sweep/pallas_call | solution.py:169
  53.7 1.5 collective-permute-start.9
  55.2 1.4 collective-permute-start.10
  56.7 2.4 %copy.19 = f32[32,128,256]{2,0,1:T(8,128)S(1)} copy(f32[32,128,256]{2,1,0:T(8,128)S(1)} %copy-done.2) | data formatting | bytes 8388608 | tf_op jit(solution)/shard_map/optimization_barrier | solution.py:409
  59.1 1.1 dynamic-slice_bitcast_fusion.refs_4_
  60.1 8.4 %collective-permute-done.8.refs_1_ = s16[33,32,256]{2,1,0:T(8,128)(2,1)S(1)} collective-permute-done((s16[33,32,256]{2,1,0:T(8,128)(2,1)}, s16[33,32,256]{2,1,0:T(8,128)(2,1)S(1)}, u32[]{:S(2)}, u32[]{:S(2)}) %collective-permute-start.8) | collective-permute-done | bytes 540704 | tf_op jit(solution)/shard_map/ppermute | solution.py:334
  68.6 8.2 %collective-permute-done.9.refs_2_ = s16[33,32,256]{2,1,0:T(8,128)(2,1)S(1)} collective-permute-done((s16[33,32,256]{2,1,0:T(8,128)(2,1)}, s16[33,32,256]{2,1,0:T(8,128)(2,1)S(1)}, u32[]{:S(2)}, u32[]{:S(2)}) %collective-permute-start.9) | collective-permute-done | bytes 540704 | tf_op jit(solution)/shard_map/ppermute | solution.py:334
  76.8 1.5 collective-permute-done.10.refs_3_
  78.3 0.8 copy-done.18
  79.1 3.2 %update.2 = (f32[32,32,256]{2,1,0:T(8,128)}, bf16[32,32,256]{2,1,0:T(8,128)(2,1)}) custom-call(s16[33,32,256]{2,1,0:T(8,128)(2,1)} %get-tuple-element.39.refs_0_, s16[33,32,256]{2,1,0:T(8,128)(2,1)} %copy-done.15, s16[33,32,256]{2,1,0:T(8,128)(2,1)} %copy-done.16, s16[33,32,256]{2,1,0:T(8,128)(2,1)} %copy-done.18, ...), custom_call_target="tpu_custom_call" | custom-call | tf_op jit(solution)/shard_map/update/pallas_call | solution.py:247
  82.3 1.7 collective-permute-start.14
  84.0 1.5 collective-permute-start.12
  85.5 1.9 %collective-permute-start.11 = (bf16[32,32,256]{2,1,0:T(8,128)(2,1)}, bf16[32,32,256]{2,1,0:T(8,128)(2,1)S(1)}, u32[]{:S(2)}, u32[]{:S(2)}) collective-permute-start(bf16[32,32,256]{2,1,0:T(8,128)(2,1)} %get-tuple-element.45.refs_6_), channel_id=1, source_target_pairs={{4,8},{8,4},{12,16},{16,12},{20,24},{24,20},{5,9},{9,5},{13,17},{1... | collective-permute-start | bytes 1572872 | tf_op jit(solution)/shard_map/ppermute | solution.py:328
  87.4 6.3 %collective-permute-done.14.refs_8_ = bf16[32,32,256]{2,1,0:T(8,128)(2,1)S(1)} collective-permute-done((bf16[32,32,256]{2,1,0:T(8,128)(2,1)}, bf16[32,32,256]{2,1,0:T(8,128)(2,1)S(1)}, u32[]{:S(2)}, u32[]{:S(2)}) %collective-permute-start.14) | collective-permute-done | bytes 524320 | tf_op jit(solution)/shard_map/ppermute | solution.py:334
  93.7 1.9 %collective-permute-start.15 = (bf16[32,32,256]{2,1,0:T(8,128)(2,1)S(1)}, bf16[32,32,256]{2,1,0:T(8,128)(2,1)S(1)}, u32[]{:S(2)}, u32[]{:S(2)}) collective-permute-start(bf16[32,32,256]{2,1,0:T(8,128)(2,1)S(1)} %collective-permute-done.14.refs_8_), channel_id=1, source_target_pairs={{4,8},{8,4},{12,16},{16,12},{20,24},{24,20},{5,9},{9,5},{13,17},{1... | collective-permute-start | bytes 1572872 | tf_op jit(solution)/shard_map/ppermute | solution.py:328
  95.6 3.6 %collective-permute-start.13 = (bf16[32,32,256]{2,1,0:T(8,128)(2,1)S(1)}, bf16[32,32,256]{2,1,0:T(8,128)(2,1)S(1)}, u32[]{:S(2)}, u32[]{:S(2)}) collective-permute-start(bf16[32,32,256]{2,1,0:T(8,128)(2,1)S(1)} %collective-permute-done.12.refs_7_), channel_id=1, source_target_pairs={{4,8},{8,4},{12,16},{16,12},{20,24},{24,20},{5,9},{9,5},{13,17},{1... | collective-permute-start | bytes 1572872 | tf_op jit(solution)/shard_map/ppermute | solution.py:328
  99.3 0.6 collective-permute-start.17
  100.0 0.7 collective-permute-start.16
  100.6 6.9 %collective-permute-done.17.refs_10_ = bf16[16,32,256]{2,1,0:T(8,128)(2,1)S(1)} collective-permute-done((bf16[16,32,256]{2,1,0:T(8,128)(2,1)S(1)}, bf16[16,32,256]{2,1,0:T(8,128)(2,1)S(1)}, u32[]{:S(2)}, u32[]{:S(2)}) %collective-permute-start.17) | collective-permute-done | bytes 262176 | tf_op jit(solution)/shard_map/ppermute | solution.py:334
  107.9 2.1 %collective-permute-start.18 = (bf16[32,32,256]{2,1,0:T(8,128)(2,1)S(1)}, bf16[32,32,256]{2,1,0:T(8,128)(2,1)S(1)}, u32[]{:S(2)}, u32[]{:S(2)}) collective-permute-start(bf16[32,32,256]{2,1,0:T(8,128)(2,1)S(1)} %pad_maximum_fusion), channel_id=1, source_target_pairs={{4,8},{8,4},{12,16},{16,12},{20,24},{24,20},{5,9},{9,5},{13,17},{1... | collective-permute-start | bytes 1572872 | tf_op jit(solution)/shard_map/ppermute | solution.py:328
  111.3 2.8 %collective-permute-done.23.refs_15_ = bf16[16,32,256]{2,1,0:T(8,128)(2,1)S(1)} collective-permute-done((bf16[16,32,256]{2,1,0:T(8,128)(2,1)S(1)}, bf16[16,32,256]{2,1,0:T(8,128)(2,1)S(1)}, u32[]{:S(2)}, u32[]{:S(2)}) %collective-permute-start.23) | collective-permute-done | bytes 262176 | tf_op jit(solution)/shard_map/ppermute | solution.py:331
  114.1 4.3 %collective-permute-done.18.refs_5_ = bf16[32,32,256]{2,1,0:T(8,128)(2,1)S(1)} collective-permute-done((bf16[32,32,256]{2,1,0:T(8,128)(2,1)S(1)}, bf16[32,32,256]{2,1,0:T(8,128)(2,1)S(1)}, u32[]{:S(2)}, u32[]{:S(2)}) %collective-permute-start.18) | collective-permute-done | bytes 524320 | tf_op jit(solution)/shard_map/ppermute | solution.py:328
  118.6 0.7 copy-done.25
  119.6 0.8 copy-done.28
  120.5 12.9 %sweep.3 = (s16[33,32,256]{2,1,0:T(8,128)(2,1)}, s16[33,32,256]{2,1,0:T(8,128)(2,1)}, s16[33,32,256]{2,1,0:T(8,128)(2,1)}, s16[33,32,256]{2,1,0:T(8,128)(2,1)}) custom-call(s32[1]{0:T(128)} %bitcast.refs_0_, s32[64]{0:T(128)} %get-tuple-element.57.refs_1_, bf16[32,32,256]{2,1,0:T(8,128)(2,1)} %copy-done.22, bf16[32,32,256]{2,1,0:T(8,128)(2,1)} %copy-done.24, ...), custom_call_target="tpu_custom_call" | custom-call | tf_op jit(solution)/shard_map/sweep/pallas_call | solution.py:169
  133.4 1.5 collective-permute-start.24
  135.4 1.5 collective-permute-start.26
  136.9 11.8 %collective-permute-done.24.refs_1_ = s16[33,32,256]{2,1,0:T(8,128)(2,1)S(1)} collective-permute-done((s16[33,32,256]{2,1,0:T(8,128)(2,1)}, s16[33,32,256]{2,1,0:T(8,128)(2,1)S(1)}, u32[]{:S(2)}, u32[]{:S(2)}) %collective-permute-start.24) | collective-permute-done | bytes 540704 | tf_op jit(solution)/shard_map/ppermute | solution.py:334
  148.7 12.4 %collective-permute-done.25.refs_2_ = s16[33,32,256]{2,1,0:T(8,128)(2,1)S(1)} collective-permute-done((s16[33,32,256]{2,1,0:T(8,128)(2,1)}, s16[33,32,256]{2,1,0:T(8,128)(2,1)S(1)}, u32[]{:S(2)}, u32[]{:S(2)}) %collective-permute-start.25) | collective-permute-done | bytes 540704 | tf_op jit(solution)/shard_map/ppermute | solution.py:334
  161.1 0.8 copy-done.19
  162.1 3.1 %update.3.refs_1_ = s16[33,32,256]{2,1,0:T(8,128)(2,1)} custom-call(s16[33,32,256]{2,1,0:T(8,128)(2,1)} %get-tuple-element.50.refs_0_, s16[33,32,256]{2,1,0:T(8,128)(2,1)} %copy-done.17, s16[33,32,256]{2,1,0:T(8,128)(2,1)} %copy-done.19, s16[33,32,256]{2,1,0:T(8,128)(2,1)} %copy-done.20, f32[32,32,256]{2,1,0:T(8,128)} %get-tuple-element.54.refs_4_), custom_call_target="tpu_custom_call" | custom-call | tf_op jit(solution)/shard_map/update/pallas_call | solution.py:247
  165.3 0.6 collective-permute-start.29
  165.9 1.0 collective-permute-start.27
  166.9 12.3 %collective-permute-done.29.refs_3_ = s16[33,32,256]{2,1,0:T(8,128)(2,1)S(1)} collective-permute-done((s16[33,32,256]{2,1,0:T(8,128)(2,1)}, s16[33,32,256]{2,1,0:T(8,128)(2,1)S(1)}, u32[]{:S(2)}, u32[]{:S(2)}) %collective-permute-start.29) | collective-permute-done | bytes 540704 | tf_op jit(solution)/shard_map/ppermute | solution.py:334
  179.7 1.5 collective-permute-start.28
  181.2 3.3 %gather.2.refs_3_ = f32[32,128,256]{2,1,0:T(8,128)} custom-call(s32[1]{0:T(128)} %bitcast.refs_0_, s16[33,32,256]{2,1,0:T(8,128)(2,1)} %update.3.refs_1_, s16[33,32,256]{2,1,0:T(8,128)(2,1)} %copy-done.8, s16[33,32,256]{2,1,0:T(8,128)(2,1)} %copy-done.7), custom_call_target="tpu_custom_call" | custom-call | tf_op jit(solution)/shard_map/gather/pallas_call | solution.py:291
  184.6 1.8 collective-permute-done.30.refs_2_
  187.0 0.7 copy-done.30
  187.7 2.2 %gather.3 = f32[32,128,256]{2,1,0:T(8,128)} custom-call(s32[1]{0:T(128)} %bitcast.refs_0_, s16[17,32,256]{2,1,0:T(8,128)(2,1)} %copy-done.30, s16[17,32,256]{2,1,0:T(8,128)(2,1)} %copy-done.29, f32[32,128,256]{2,1,0:T(8,128)} %gather.2.refs_3_), custom_call_target="tpu_custom_call", output_to_operand_aliasing={{}: (3, {})} | custom-call | tf_op jit(solution)/shard_map/gather/pallas_call | solution.py:291
  (109 shorter events, 6.7 us)
Async XLA Ops:
  0.0 16.4 %copy-start = (bf16[8,3,33]{2,0,1:T(8,128)(2,1)S(1)}, bf16[8,3,33]{2,0,1:T(8,128)(2,1)}, u32[]{:S(2)}) copy-start(bf16[8,3,33]{2,0,1:T(8,128)(2,1)} %param.7) | copy-start | bytes 4756
  0.0 4.5 %copy-start.3 = (bf16[1,32,128,256]{3,2,1,0:T(8,128)(2,1)S(1)}, bf16[1,32,128,256]{3,2,1,0:T(8,128)(2,1)}, u32[]{:S(2)}) copy-start(bf16[1,32,128,256]{3,2,1,0:T(8,128)(2,1)} %param.6) | copy-start | bytes 6291460
  2.6 10.8 %collective-permute-start = (bf16[32,32,256]{2,1,0:T(8,128)(2,1)}, bf16[32,32,256]{2,1,0:T(8,128)(2,1)}, u32[]{:S(2)}, u32[]{:S(2)}) collective-permute-start(bf16[32,32,256]{2,1,0:T(8,128)(2,1)} %bitcast.29), channel_id=1, source_target_pairs={{4,8},{8,4},{12,16},{16,12},{20,24},{24,20},{5,9},{9,5},{13,17},{1... | collective-permute-start | bytes 1572872 | tf_op jit(solution)/shard_map/ppermute | solution.py:328
  4.5 3.1 %copy-start.1 = (f32[32,128,256]{2,1,0:T(8,128)S(1)}, f32[32,128,256]{2,1,0:T(8,128)}, u32[]{:S(2)}) copy-start(f32[32,128,256]{2,1,0:T(8,128)} %param.5) | copy-start | bytes 12582916
  5.9 12.7 %copy-start.33 = (s32[1,2]{1,0:T(1,128)S(1)}, s32[1,2]{1,0:T(1,128)}, u32[]{:S(2)}) copy-start(s32[1,2]{1,0:T(1,128)} %param.9) | copy-start | bytes 28
  5.9 30.6 %collective-permute-start.7 = (bf16[16,128,256]{2,1,0:T(8,128)(2,1)}, bf16[16,128,256]{2,1,0:T(8,128)(2,1)S(1)}, u32[]{:S(2)}, u32[]{:S(2)}) collective-permute-start(bf16[16,128,256]{2,1,0:T(8,128)(2,1)} %get-tuple-element.59), channel_id=1, source_target_pairs={{0,4},{4,0},{8,12},{12,8},{16,20},{20,16},{24,28},{28,24},{1,5},{5... | collective-permute-start | bytes 3145736 | tf_op jit(solution)/shard_map/ppermute | solution.py:331
  9.9 29.9 %copy-start.4 = (bf16[32,128,256]{2,0,1:T(8,128)(2,1)}, bf16[32,128,256]{2,0,1:T(8,128)(2,1)S(1)}, u32[]{:S(2)}) copy-start(bf16[32,128,256]{2,0,1:T(8,128)(2,1)S(1)} %copy.31) | copy-start | bytes 6291460
  9.9 29.8 %collective-permute-start.5 = (bf16[128,32,256]{2,1,0:T(8,128)(2,1)S(1)}, bf16[128,32,256]{2,1,0:T(8,128)(2,1)}, u32[]{:S(2)}, u32[]{:S(2)}) collective-permute-start(bf16[128,32,256]{2,1,0:T(8,128)(2,1)S(1)} %bitcast.35), channel_id=1, source_target_pairs={{0,4},{4,0},{8,12},{12,8},{16,20},{20,16},{24,28},{28,24},{1,5},{5... | collective-permute-start | bytes 6291464 | tf_op jit(solution)/shard_map/ppermute | solution.py:331
  13.4 14.2 %collective-permute-start.2 = (bf16[32,32,256]{2,1,0:T(8,128)(2,1)}, bf16[32,32,256]{2,1,0:T(8,128)(2,1)S(1)}, u32[]{:S(2)}, u32[]{:S(2)}) collective-permute-start(bf16[32,32,256]{2,1,0:T(8,128)(2,1)} %collective-permute-done.refs_2_), channel_id=1, source_target_pairs={{0,2},{1,3},{2,0},{3,1},{4,6},{5,7},{6,4},{7,5},{8,10},{9,11},{10,... | collective-permute-start | bytes 1572872 | tf_op jit(solution)/shard_map/ppermute | solution.py:334
  14.9 15.7 %collective-permute-start.1 = (bf16[32,32,256]{2,1,0:T(8,128)(2,1)}, bf16[32,32,256]{2,1,0:T(8,128)(2,1)S(1)}, u32[]{:S(2)}, u32[]{:S(2)}) collective-permute-start(bf16[32,32,256]{2,1,0:T(8,128)(2,1)} %collective-permute-done.refs_2_), channel_id=1, source_target_pairs={{0,1},{1,0},{2,3},{3,2},{4,5},{5,4},{6,7},{7,6},{8,9},{9,8},{10,11... | collective-permute-start | bytes 1572872 | tf_op jit(solution)/shard_map/ppermute | solution.py:334
  16.5 23.2 %collective-permute-start.6 = (bf16[16,128,256]{2,1,0:T(8,128)(2,1)}, bf16[16,128,256]{2,1,0:T(8,128)(2,1)}, u32[]{:S(2)}, u32[]{:S(2)}) collective-permute-start(bf16[16,128,256]{2,1,0:T(8,128)(2,1)} %get-tuple-element.35), channel_id=1, source_target_pairs={{4,8},{8,4},{12,16},{16,12},{20,24},{24,20},{5,9},{9,5},{13,17},{1... | collective-permute-start | bytes 3145736 | tf_op jit(solution)/shard_map/ppermute | solution.py:328
  22.6 17.1 %copy-start.6 = (bf16[256,256]{1,0:T(8,128)(2,1)}, bf16[256,256]{1,0:T(8,128)(2,1)S(1)}, u32[]{:S(2)}) copy-start(bf16[256,256]{1,0:T(8,128)(2,1)S(1)} %select_reduce_fusion.refs_17_.refs_24_) | copy-start | bytes 393220
  27.5 0.8 copy-start.9
  29.0 7.9 %collective-permute-start.4 = (bf16[16,32,256]{2,1,0:T(8,128)(2,1)}, bf16[16,32,256]{2,1,0:T(8,128)(2,1)}, u32[]{:S(2)}, u32[]{:S(2)}) collective-permute-start(bf16[16,32,256]{2,1,0:T(8,128)(2,1)} %slice.60), channel_id=1, source_target_pairs={{0,1},{1,0},{2,3},{3,2},{4,5},{5,4},{6,7},{7,6},{8,9},{9,8},{10,11... | collective-permute-start | bytes 786440 | tf_op jit(solution)/shard_map/ppermute | solution.py:334
  30.5 0.8 copy-start.10
  32.1 7.6 %collective-permute-start.3 = (bf16[16,32,256]{2,1,0:T(8,128)(2,1)}, bf16[16,32,256]{2,1,0:T(8,128)(2,1)}, u32[]{:S(2)}, u32[]{:S(2)}) collective-permute-start(bf16[16,32,256]{2,1,0:T(8,128)(2,1)} %slice.59), channel_id=1, source_target_pairs={{0,2},{1,3},{2,0},{3,1},{4,6},{5,7},{6,4},{7,5},{8,10},{9,11},{10,... | collective-permute-start | bytes 786440 | tf_op jit(solution)/shard_map/ppermute | solution.py:334
  34.4 5.3 %copy-start.21 = (bf16[128,128]{0,1:T(8,128)(2,1)}, bf16[128,128]{0,1:T(8,128)(2,1)S(1)}, u32[]{:S(2)}) copy-start(bf16[128,128]{0,1:T(8,128)(2,1)S(1)} %copy.16) | copy-start | bytes 98308
  36.5 3.2 %copy-start.5 = (bf16[16,128,256]{2,1,0:T(8,128)(2,1)}, bf16[16,128,256]{2,1,0:T(8,128)(2,1)S(1)}, u32[]{:S(2)}) copy-start(bf16[16,128,256]{2,1,0:T(8,128)(2,1)S(1)} %collective-permute-done.7.refs_11_.refs_18_) | copy-start | bytes 3145732
  39.7 16.9 %copy-start.2 = (f32[32,128,256]{2,1,0:T(8,128)S(1)}, f32[32,128,256]{2,1,0:T(8,128)}, u32[]{:S(2)}) copy-start(f32[32,128,256]{2,1,0:T(8,128)} %param.5) | copy-start | bytes 12582916
  53.1 15.5 %collective-permute-start.8 = (s16[33,32,256]{2,1,0:T(8,128)(2,1)}, s16[33,32,256]{2,1,0:T(8,128)(2,1)S(1)}, u32[]{:S(2)}, u32[]{:S(2)}) collective-permute-start(s16[33,32,256]{2,1,0:T(8,128)(2,1)} %get-tuple-element.40), channel_id=1, source_target_pairs={{0,1},{1,0},{2,3},{3,2},{4,5},{5,4},{6,7},{7,6},{8,9},{9,8},{10,11... | collective-permute-start | bytes 1622024 | tf_op jit(solution)/shard_map/ppermute | solution.py:334
  53.7 23.1 %collective-permute-start.9 = (s16[33,32,256]{2,1,0:T(8,128)(2,1)}, s16[33,32,256]{2,1,0:T(8,128)(2,1)S(1)}, u32[]{:S(2)}, u32[]{:S(2)}) collective-permute-start(s16[33,32,256]{2,1,0:T(8,128)(2,1)} %get-tuple-element.41), channel_id=1, source_target_pairs={{0,2},{1,3},{2,0},{3,1},{4,6},{5,7},{6,4},{7,5},{8,10},{9,11},{10,... | collective-permute-start | bytes 1622024 | tf_op jit(solution)/shard_map/ppermute | solution.py:334
  55.2 23.1 %collective-permute-start.10 = (s16[33,32,256]{2,1,0:T(8,128)(2,1)}, s16[33,32,256]{2,1,0:T(8,128)(2,1)S(1)}, u32[]{:S(2)}, u32[]{:S(2)}) collective-permute-start(s16[33,32,256]{2,1,0:T(8,128)(2,1)} %get-tuple-element.42), channel_id=1, source_target_pairs={{0,3},{1,2},{2,1},{3,0},{4,7},{5,6},{6,5},{7,4},{8,11},{9,10},{10,... | collective-permute-start | bytes 1622024 | tf_op jit(solution)/shard_map/ppermute | solution.py:334
  68.6 9.7 %copy-start.15 = (s16[33,32,256]{2,1,0:T(8,128)(2,1)}, s16[33,32,256]{2,1,0:T(8,128)(2,1)S(1)}, u32[]{:S(2)}) copy-start(s16[33,32,256]{2,1,0:T(8,128)(2,1)S(1)} %collective-permute-done.8.refs_1_) | copy-start | bytes 1622020
  76.8 1.5 copy-start.16
  78.3 0.8 copy-start.18
  82.3 11.4 %collective-permute-start.14 = (bf16[32,32,256]{2,1,0:T(8,128)(2,1)}, bf16[32,32,256]{2,1,0:T(8,128)(2,1)S(1)}, u32[]{:S(2)}, u32[]{:S(2)}) collective-permute-start(bf16[32,32,256]{2,1,0:T(8,128)(2,1)} %get-tuple-element.45.refs_6_), channel_id=1, source_target_pairs={{0,2},{1,3},{2,0},{3,1},{4,6},{5,7},{6,4},{7,5},{8,10},{9,11},{10,... | collective-permute-start | bytes 1572872 | tf_op jit(solution)/shard_map/ppermute | solution.py:334
  84.0 11.6 %collective-permute-start.12 = (bf16[32,32,256]{2,1,0:T(8,128)(2,1)}, bf16[32,32,256]{2,1,0:T(8,128)(2,1)S(1)}, u32[]{:S(2)}, u32[]{:S(2)}) collective-permute-start(bf16[32,32,256]{2,1,0:T(8,128)(2,1)} %get-tuple-element.45.refs_6_), channel_id=1, source_target_pairs={{0,1},{1,0},{2,3},{3,2},{4,5},{5,4},{6,7},{7,6},{8,9},{9,8},{10,11... | collective-permute-start | bytes 1572872 | tf_op jit(solution)/shard_map/ppermute | solution.py:334
  85.5 24.6 %collective-permute-start.11 = (bf16[32,32,256]{2,1,0:T(8,128)(2,1)}, bf16[32,32,256]{2,1,0:T(8,128)(2,1)S(1)}, u32[]{:S(2)}, u32[]{:S(2)}) collective-permute-start(bf16[32,32,256]{2,1,0:T(8,128)(2,1)} %get-tuple-element.45.refs_6_), channel_id=1, source_target_pairs={{4,8},{8,4},{12,16},{16,12},{20,24},{24,20},{5,9},{9,5},{13,17},{1... | collective-permute-start | bytes 1572872 | tf_op jit(solution)/shard_map/ppermute | solution.py:328
  93.7 24.8 %copy-start.11 = (bf16[32,32,256]{2,1,0:T(8,128)(2,1)}, bf16[32,32,256]{2,1,0:T(8,128)(2,1)S(1)}, u32[]{:S(2)}) copy-start(bf16[32,32,256]{2,1,0:T(8,128)(2,1)S(1)} %collective-permute-done.14.refs_8_) | copy-start | bytes 1572868
  93.7 17.0 %collective-permute-start.15 = (bf16[32,32,256]{2,1,0:T(8,128)(2,1)S(1)}, bf16[32,32,256]{2,1,0:T(8,128)(2,1)S(1)}, u32[]{:S(2)}, u32[]{:S(2)}) collective-permute-start(bf16[32,32,256]{2,1,0:T(8,128)(2,1)S(1)} %collective-permute-done.14.refs_8_), channel_id=1, source_target_pairs={{4,8},{8,4},{12,16},{16,12},{20,24},{24,20},{5,9},{9,5},{13,17},{1... | collective-permute-start | bytes 1572872 | tf_op jit(solution)/shard_map/ppermute | solution.py:328
  95.6 22.9 %copy-start.12 = (bf16[32,32,256]{2,1,0:T(8,128)(2,1)}, bf16[32,32,256]{2,1,0:T(8,128)(2,1)S(1)}, u32[]{:S(2)}) copy-start(bf16[32,32,256]{2,1,0:T(8,128)(2,1)S(1)} %collective-permute-done.12.refs_7_) | copy-start | bytes 1572868
  95.6 15.2 %collective-permute-start.13 = (bf16[32,32,256]{2,1,0:T(8,128)(2,1)S(1)}, bf16[32,32,256]{2,1,0:T(8,128)(2,1)S(1)}, u32[]{:S(2)}, u32[]{:S(2)}) collective-permute-start(bf16[32,32,256]{2,1,0:T(8,128)(2,1)S(1)} %collective-permute-done.12.refs_7_), channel_id=1, source_target_pairs={{4,8},{8,4},{12,16},{16,12},{20,24},{24,20},{5,9},{9,5},{13,17},{1... | collective-permute-start | bytes 1572872 | tf_op jit(solution)/shard_map/ppermute | solution.py:328
  99.3 8.2 %collective-permute-start.17 = (bf16[16,32,256]{2,1,0:T(8,128)(2,1)S(1)}, bf16[16,32,256]{2,1,0:T(8,128)(2,1)S(1)}, u32[]{:S(2)}, u32[]{:S(2)}) collective-permute-start(bf16[16,32,256]{2,1,0:T(8,128)(2,1)S(1)} %slice.62), channel_id=1, source_target_pairs={{0,1},{1,0},{2,3},{3,2},{4,5},{5,4},{6,7},{7,6},{8,9},{9,8},{10,11... | collective-permute-start | bytes 786440 | tf_op jit(solution)/shard_map/ppermute | solution.py:334
  100.0 7.9 %collective-permute-start.16 = (bf16[16,32,256]{2,1,0:T(8,128)(2,1)S(1)}, bf16[16,32,256]{2,1,0:T(8,128)(2,1)S(1)}, u32[]{:S(2)}, u32[]{:S(2)}) collective-permute-start(bf16[16,32,256]{2,1,0:T(8,128)(2,1)S(1)} %slice.61), channel_id=1, source_target_pairs={{0,2},{1,3},{2,0},{3,1},{4,6},{5,7},{6,4},{7,5},{8,10},{9,11},{10,... | collective-permute-start | bytes 786440 | tf_op jit(solution)/shard_map/ppermute | solution.py:334
  107.5 11.0 %copy-start.13 = (bf16[16,32,256]{2,1,0:T(8,128)(2,1)}, bf16[16,32,256]{2,1,0:T(8,128)(2,1)S(1)}, u32[]{:S(2)}) copy-start(bf16[16,32,256]{2,1,0:T(8,128)(2,1)S(1)} %collective-permute-done.17.refs_10_) | copy-start | bytes 786436
  107.9 10.6 %copy-start.14 = (bf16[16,32,256]{2,1,0:T(8,128)(2,1)}, bf16[16,32,256]{2,1,0:T(8,128)(2,1)S(1)}, u32[]{:S(2)}) copy-start(bf16[16,32,256]{2,1,0:T(8,128)(2,1)S(1)} %collective-permute-done.16.refs_9_) | copy-start | bytes 786436
  107.9 3.3 %collective-permute-start.22 = (bf16[16,32,256]{2,1,0:T(8,128)(2,1)S(1)}, bf16[16,32,256]{2,1,0:T(8,128)(2,1)S(1)}, u32[]{:S(2)}, u32[]{:S(2)}) collective-permute-start(bf16[16,32,256]{2,1,0:T(8,128)(2,1)S(1)} %collective-permute-done.16.refs_9_), channel_id=1, source_target_pairs={{0,4},{4,0},{8,12},{12,8},{16,20},{20,16},{24,28},{28,24},{1,5},{5... | collective-permute-start | bytes 786440 | tf_op jit(solution)/shard_map/ppermute | solution.py:331
  107.9 10.5 %collective-permute-start.18 = (bf16[32,32,256]{2,1,0:T(8,128)(2,1)S(1)}, bf16[32,32,256]{2,1,0:T(8,128)(2,1)S(1)}, u32[]{:S(2)}, u32[]{:S(2)}) collective-permute-start(bf16[32,32,256]{2,1,0:T(8,128)(2,1)S(1)} %pad_maximum_fusion), channel_id=1, source_target_pairs={{4,8},{8,4},{12,16},{16,12},{20,24},{24,20},{5,9},{9,5},{13,17},{1... | collective-permute-start | bytes 1572872 | tf_op jit(solution)/shard_map/ppermute | solution.py:328
  110.1 8.4 %copy-start.22 = (bf16[32,32,256]{2,1,0:T(8,128)(2,1)}, bf16[32,32,256]{2,1,0:T(8,128)(2,1)S(1)}, u32[]{:S(2)}) copy-start(bf16[32,32,256]{2,1,0:T(8,128)(2,1)S(1)} %collective-permute-done.11.refs_2_) | copy-start | bytes 1572868
  110.1 8.3 %collective-permute-start.19 = (bf16[32,32,256]{2,1,0:T(8,128)(2,1)}, bf16[32,32,256]{2,1,0:T(8,128)(2,1)S(1)}, u32[]{:S(2)}, u32[]{:S(2)}) collective-permute-start(bf16[32,32,256]{2,1,0:T(8,128)(2,1)} %get-tuple-element.45.refs_6_), channel_id=1, source_target_pairs={{0,4},{4,0},{8,12},{12,8},{16,20},{20,16},{24,28},{28,24},{1,5},{5... | collective-permute-start | bytes 1572872 | tf_op jit(solution)/shard_map/ppermute | solution.py:331
  110.7 7.8 %copy-start.23 = (bf16[32,32,256]{2,1,0:T(8,128)(2,1)}, bf16[32,32,256]{2,1,0:T(8,128)(2,1)S(1)}, u32[]{:S(2)}) copy-start(bf16[32,32,256]{2,1,0:T(8,128)(2,1)S(1)} %collective-permute-done.15.refs_4_) | copy-start | bytes 1572868
  110.7 7.8 %collective-permute-start.20 = (bf16[32,32,256]{2,1,0:T(8,128)(2,1)S(1)}, bf16[32,32,256]{2,1,0:T(8,128)(2,1)S(1)}, u32[]{:S(2)}, u32[]{:S(2)}) collective-permute-start(bf16[32,32,256]{2,1,0:T(8,128)(2,1)S(1)} %collective-permute-done.12.refs_7_), channel_id=1, source_target_pairs={{0,4},{4,0},{8,12},{12,8},{16,20},{20,16},{24,28},{28,24},{1,5},{5... | collective-permute-start | bytes 1572872 | tf_op jit(solution)/shard_map/ppermute | solution.py:331
  110.8 7.8 %copy-start.24 = (bf16[32,32,256]{2,1,0:T(8,128)(2,1)}, bf16[32,32,256]{2,1,0:T(8,128)(2,1)S(1)}, u32[]{:S(2)}) copy-start(bf16[32,32,256]{2,1,0:T(8,128)(2,1)S(1)} %collective-permute-done.13.refs_3_) | copy-start | bytes 1572868
  110.8 7.7 %collective-permute-start.21 = (bf16[32,32,256]{2,1,0:T(8,128)(2,1)S(1)}, bf16[32,32,256]{2,1,0:T(8,128)(2,1)S(1)}, u32[]{:S(2)}, u32[]{:S(2)}) collective-permute-start(bf16[32,32,256]{2,1,0:T(8,128)(2,1)S(1)} %collective-permute-done.14.refs_8_), channel_id=1, source_target_pairs={{0,4},{4,0},{8,12},{12,8},{16,20},{20,16},{24,28},{28,24},{1,5},{5... | collective-permute-start | bytes 1572872 | tf_op jit(solution)/shard_map/ppermute | solution.py:331
  111.2 7.3 %copy-start.31 = (bf16[16,32,256]{2,1,0:T(8,128)(2,1)}, bf16[16,32,256]{2,1,0:T(8,128)(2,1)S(1)}, u32[]{:S(2)}) copy-start(bf16[16,32,256]{2,1,0:T(8,128)(2,1)S(1)} %collective-permute-done.22.refs_14_) | copy-start | bytes 786436
  111.2 2.9 %collective-permute-start.23 = (bf16[16,32,256]{2,1,0:T(8,128)(2,1)S(1)}, bf16[16,32,256]{2,1,0:T(8,128)(2,1)S(1)}, u32[]{:S(2)}, u32[]{:S(2)}) collective-permute-start(bf16[16,32,256]{2,1,0:T(8,128)(2,1)S(1)} %collective-permute-done.17.refs_10_), channel_id=1, source_target_pairs={{0,4},{4,0},{8,12},{12,8},{16,20},{20,16},{24,28},{28,24},{1,5},{5... | collective-permute-start | bytes 786440 | tf_op jit(solution)/shard_map/ppermute | solution.py:331
  114.1 4.5 %copy-start.32 = (bf16[16,32,256]{2,1,0:T(8,128)(2,1)}, bf16[16,32,256]{2,1,0:T(8,128)(2,1)S(1)}, u32[]{:S(2)}) copy-start(bf16[16,32,256]{2,1,0:T(8,128)(2,1)S(1)} %collective-permute-done.23.refs_15_) | copy-start | bytes 786436
  118.4 0.9 copy-start.25
  118.5 1.0 copy-start.26
  118.5 1.2 copy-start.27
  119.6 0.8 copy-start.28
  133.4 15.3 %collective-permute-start.24 = (s16[33,32,256]{2,1,0:T(8,128)(2,1)}, s16[33,32,256]{2,1,0:T(8,128)(2,1)S(1)}, u32[]{:S(2)}, u32[]{:S(2)}) collective-permute-start(s16[33,32,256]{2,1,0:T(8,128)(2,1)} %get-tuple-element.51), channel_id=1, source_target_pairs={{0,1},{1,0},{2,3},{3,2},{4,5},{5,4},{6,7},{7,6},{8,9},{9,8},{10,11... | collective-permute-start | bytes 1622024 | tf_op jit(solution)/shard_map/ppermute | solution.py:334
  134.9 26.2 %collective-permute-start.25 = (s16[33,32,256]{2,1,0:T(8,128)(2,1)}, s16[33,32,256]{2,1,0:T(8,128)(2,1)S(1)}, u32[]{:S(2)}, u32[]{:S(2)}) collective-permute-start(s16[33,32,256]{2,1,0:T(8,128)(2,1)} %get-tuple-element.52), channel_id=1, source_target_pairs={{0,2},{1,3},{2,0},{3,1},{4,6},{5,7},{6,4},{7,5},{8,10},{9,11},{10,... | collective-permute-start | bytes 1622024 | tf_op jit(solution)/shard_map/ppermute | solution.py:334
  135.4 25.7 %collective-permute-start.26 = (s16[33,32,256]{2,1,0:T(8,128)(2,1)}, s16[33,32,256]{2,1,0:T(8,128)(2,1)S(1)}, u32[]{:S(2)}, u32[]{:S(2)}) collective-permute-start(s16[33,32,256]{2,1,0:T(8,128)(2,1)} %get-tuple-element.53), channel_id=1, source_target_pairs={{0,3},{1,2},{2,1},{3,0},{4,7},{5,6},{6,5},{7,4},{8,11},{9,10},{10,... | collective-permute-start | bytes 1622024 | tf_op jit(solution)/shard_map/ppermute | solution.py:334
  148.7 12.4 %copy-start.17 = (s16[33,32,256]{2,1,0:T(8,128)(2,1)}, s16[33,32,256]{2,1,0:T(8,128)(2,1)S(1)}, u32[]{:S(2)}) copy-start(s16[33,32,256]{2,1,0:T(8,128)(2,1)S(1)} %collective-permute-done.24.refs_1_) | copy-start | bytes 1622020
  161.1 0.8 copy-start.19
  161.1 1.0 copy-start.20
  165.3 13.9 %collective-permute-start.29 = (s16[33,32,256]{2,1,0:T(8,128)(2,1)}, s16[33,32,256]{2,1,0:T(8,128)(2,1)S(1)}, u32[]{:S(2)}, u32[]{:S(2)}) collective-permute-start(s16[33,32,256]{2,1,0:T(8,128)(2,1)} %update.3.refs_1_), channel_id=1, source_target_pairs={{0,2},{1,3},{2,0},{3,1},{4,6},{5,7},{6,4},{7,5},{8,10},{9,11},{10,... | collective-permute-start | bytes 1622024 | tf_op jit(solution)/shard_map/ppermute | solution.py:334
  165.9 13.8 %collective-permute-start.27 = (s16[33,32,256]{2,1,0:T(8,128)(2,1)}, s16[33,32,256]{2,1,0:T(8,128)(2,1)S(1)}, u32[]{:S(2)}, u32[]{:S(2)}) collective-permute-start(s16[33,32,256]{2,1,0:T(8,128)(2,1)} %update.3.refs_1_), channel_id=1, source_target_pairs={{0,1},{1,0},{2,3},{3,2},{4,5},{5,4},{6,7},{7,6},{8,9},{9,8},{10,11... | collective-permute-start | bytes 1622024 | tf_op jit(solution)/shard_map/ppermute | solution.py:334
  179.2 2.1 %copy-start.7 = (s16[33,32,256]{2,1,0:T(8,128)(2,1)}, s16[33,32,256]{2,1,0:T(8,128)(2,1)S(1)}, u32[]{:S(2)}) copy-start(s16[33,32,256]{2,1,0:T(8,128)(2,1)S(1)} %collective-permute-done.29.refs_3_) | copy-start | bytes 1622020
  179.2 7.1 %collective-permute-start.30 = (s16[17,32,256]{2,1,0:T(8,128)(2,1)S(1)}, s16[17,32,256]{2,1,0:T(8,128)(2,1)S(1)}, u32[]{:S(2)}, u32[]{:S(2)}) collective-permute-start(s16[17,32,256]{2,1,0:T(8,128)(2,1)S(1)} %slice.65), channel_id=1, source_target_pairs={{0,1},{1,0},{2,3},{3,2},{4,5},{5,4},{6,7},{7,6},{8,9},{9,8},{10,11... | collective-permute-start | bytes 835592 | tf_op jit(solution)/shard_map/ppermute | solution.py:334
  179.7 1.6 copy-start.8
  179.7 6.9 %collective-permute-start.28 = (s16[17,32,256]{2,1,0:T(8,128)(2,1)S(1)}, s16[17,32,256]{2,1,0:T(8,128)(2,1)S(1)}, u32[]{:S(2)}, u32[]{:S(2)}) collective-permute-start(s16[17,32,256]{2,1,0:T(8,128)(2,1)S(1)} %pad_add_fusion), channel_id=1, source_target_pairs={{0,2},{1,3},{2,0},{3,1},{4,6},{5,7},{6,4},{7,5},{8,10},{9,11},{10,... | collective-permute-start | bytes 835592 | tf_op jit(solution)/shard_map/ppermute | solution.py:334
  187.0 0.7 copy-start.30
  (1 other events, 0.7 us)
